TPU v7x, 32 devices: a whole 2x2x4 slice. The times are simulated.
32 devices in a mesh: node: 2 (over core), expert: 16 (over z, y, x).
Axes of the slice: x: 2, y: 2, z: 4, core: 2. Of those that a mesh axis runs over, the one named last changes fastest.
Arguments:
- tokens: bfloat16 [16, 1024, 1024], P('expert', 'node'), may hold values from -6 to 6
- cotangent: bfloat16 [16, 1024, 1024], P('expert', 'node'), may hold values from -6 to 6
- routes: int32 [16, 1024, 1], P('expert'), may hold values from 0 to 15
- ln1_gain: float32 [1024], replicated, may hold values from 0.1 to 1.9
- w_qkv: bfloat16 [1024, 3072], replicated, may hold values from -0.1875 to 0.1875
- w_out: bfloat16 [1024, 1024], replicated, may hold values from -0.75 to 0.75
- ln2_gain: float32 [1024], replicated, may hold values from 0.1 to 1.9
- w_router: bfloat16 [1024, 16], replicated, may hold values from -0.25 to 0.25
- w_mix: bfloat16 [1024, 2], replicated, may hold values from -0.375 to 0.375
- w_up: bfloat16 [1024, 4096], P(None, 'node'), may hold values from -0.1875 to 0.1875
- w_down: bfloat16 [1024, 4096], P(None, 'node'), may hold values from -0.09375 to 0.09375
- expert_up: bfloat16 [16, 1024, 4096], P('expert', None, 'node'), may hold values from -0.1875 to 0.1875
- expert_down: bfloat16 [16, 4096, 1024], P('expert', 'node'), may hold values from -3 to 3
Outputs:
- mixed_out: bfloat16 [16, 1024, 1024], P('expert', 'node')
- input_grad: float32 [16, 1024, 1024], P('expert', 'node')
- grad_ln1: float32 [1024], P(('node', 'expert'))
- grad_w_qkv: float32 [1024, 3072], P(('node', 'expert'))
- grad_w_out: float32 [1024, 1024], P(('node', 'expert'))
- grad_ln2: float32 [1024], P(('node', 'expert'))
- grad_router: float32 [1024, 16], P(('node', 'expert'))
- grad_mix: float32 [1024, 2], P(('node', 'expert'))
- grad_w_up: float32 [1024, 4096], P('expert', 'node')
- grad_w_down: float32 [1024, 4096], P('expert', 'node')
- grad_expert_up: float32 [16, 1024, 4096], P('expert', None, 'node')
- grad_expert_down: float32 [16, 4096, 1024], P('expert', 'node')
All inputs are finite; a program needn't handle non-finite values.
Results may differ from a plain program's by a relative error of at most 0.02.
Values may be sent and summed in bfloat16 or wider, within the bound.
A program may use at most 320 MiB of HBM per device.

v0:
```python
import jax
import jax.numpy as jnp
from jax import lax
from jax.sharding import PartitionSpec as P

HEADS = 16
HEAD_DIM = 64


EPS = 1e-05
HIGHEST_PRECISION = lax.Precision.HIGHEST


def layer_norm(values, gain):
    average = jnp.mean(values, axis=-1, keepdims=True)
    centered = values - average
    inverse = lax.rsqrt(jnp.mean(centered * centered, axis=-1, keepdims=True) + EPS)
    normed = centered * inverse
    return (normed * gain, normed, inverse)


def norm_backward(upstream, normed, inverse, gain):
    scaled = upstream * gain
    inner_term = (
        scaled
        - jnp.mean(scaled, axis=-1, keepdims=True)
        - normed * jnp.mean(scaled * normed, axis=-1, keepdims=True)
    )
    return (inner_term * inverse, jnp.sum(upstream * normed, axis=0))


def gelu_backward(pre_act, upstream):
    return jax.vjp(jax.nn.gelu, pre_act)[1](upstream)[0]


def masked_scores(queries, key_rows, query_start, scale):
    block_rows = queries.shape[0]
    scores = (
        jnp.einsum("qhd,khd->hqk", queries, key_rows, preferred_element_type=jnp.float32) * scale
    )
    positions = jnp.arange(key_rows.shape[0])
    query_pos = query_start + jnp.arange(block_rows)
    allowed = query_pos[:, None] >= positions[None, :]
    return jnp.where(allowed[None], scores, -1000000000.0)


def reduce_mlp(grad_up, grad_down):
    return (
        lax.psum_scatter(grad_up, "expert", scatter_dimension=0, tiled=True),
        lax.psum_scatter(grad_down, "expert", scatter_dimension=0, tiled=True),
    )


def shards(
    tokens,
    cotangent,
    routes,
    ln1_gain,
    w_qkv,
    w_out,
    ln2_gain,
    w_router,
    w_mix,
    w_up,
    w_down,
    expert_up,
    expert_down,
):
    width = tokens.shape[2]
    token_rows = tokens.reshape(-1, width).astype(jnp.float32)
    row_count = token_rows.shape[0]
    scale = HEAD_DIM ** (-0.5)
    own_start = lax.axis_index("node") * row_count
    block_rows = min(512, row_count)
    block_count = row_count // block_rows
    normed_one, base_one, inverse_one = layer_norm(token_rows, ln1_gain)
    normed_low = normed_one.astype(jnp.bfloat16)
    packed = jnp.dot(normed_low, w_qkv, preferred_element_type=jnp.float32).astype(jnp.bfloat16)
    packed = packed.reshape(row_count, 3, HEADS, HEAD_DIM)
    queries = packed[:, 0]
    seq_keys, seq_values = (
        lax.all_gather(packed[:, 1], "node", axis=0, tiled=True),
        lax.all_gather(packed[:, 2], "node", axis=0, tiled=True),
    )
    seq_len = seq_keys.shape[0]

    def attend_block(block_index):
        block_start = block_index * block_rows
        scores = masked_scores(queries, seq_keys, own_start + block_start, scale)
        highest = jnp.max(scores, axis=-1, keepdims=True)
        shifted = jnp.exp(scores - highest)
        totals = jnp.sum(shifted, axis=-1, keepdims=True)
        probs = shifted / totals
        attended = jnp.einsum(
            "hqk,khd->qhd",
            probs.astype(jnp.bfloat16),
            seq_values,
            preferred_element_type=jnp.float32,
        )
        return (attended, highest[..., 0] + jnp.log(totals[..., 0]))

    attended, log_totals = lax.map(attend_block, jnp.arange(block_count))
    attended_low = attended.reshape(row_count, width).astype(jnp.bfloat16)
    hidden = token_rows + jnp.dot(attended_low, w_out, preferred_element_type=jnp.float32)
    normed_two, base_two, inverse_two = layer_norm(hidden, ln2_gain)
    inner_low = normed_two.astype(jnp.bfloat16)
    group_rows = lax.all_gather(inner_low, "node", axis=0, tiled=True)
    dense_pre = jnp.dot(group_rows, w_up, preferred_element_type=jnp.float32)
    dense_act = jax.nn.gelu(dense_pre).astype(jnp.bfloat16)
    dense_part = jnp.einsum("tf,df->td", dense_act, w_down, preferred_element_type=jnp.float32)
    group_routes = routes.reshape(-1)
    group_len = group_routes.shape[0]
    experts = w_router.shape[1]
    capacity = 3 * group_len // (2 * experts)
    route_onehot = (group_routes[:, None] == jnp.arange(experts)[None, :]).astype(jnp.int32)
    slot_order = jnp.sum(jnp.cumsum(route_onehot, axis=0) * route_onehot, axis=1) - 1
    slot_index = group_routes * capacity + slot_order
    slot_onehot = (
        (slot_index[:, None] == jnp.arange(experts * capacity)[None, :])
        & (slot_order < capacity)[:, None]
    ).astype(jnp.bfloat16)
    outgoing = jnp.einsum("ts,td->sd", slot_onehot, group_rows, preferred_element_type=jnp.float32)
    outgoing = outgoing.astype(jnp.bfloat16).reshape(experts, capacity, width)
    up_local = expert_up[0]
    down_local = expert_down[0]
    received = lax.all_to_all(outgoing, "expert", split_axis=0, concat_axis=0, tiled=True)
    flat_rows = received.reshape(-1, width)
    pre_expert = jnp.dot(flat_rows, up_local, preferred_element_type=jnp.float32)
    partial_out = jnp.dot(
        jax.nn.gelu(pre_expert).astype(jnp.bfloat16), down_local, preferred_element_type=jnp.float32
    )
    partial_out = partial_out.astype(jnp.bfloat16).reshape(received.shape)
    results = (received, partial_out)
    received = results[0]
    returned = lax.all_to_all(results[-1], "expert", split_axis=0, concat_axis=0, tiled=True)
    expert_tok = jnp.einsum(
        "ts,sd->td", slot_onehot, returned.reshape(-1, width), preferred_element_type=jnp.float32
    )
    dense_own, expert_own = (
        lax.psum_scatter(
            dense_part.astype(jnp.bfloat16), "node", scatter_dimension=0, tiled=True
        ).astype(jnp.float32),
        lax.psum_scatter(
            expert_tok.astype(jnp.bfloat16), "node", scatter_dimension=0, tiled=True
        ).astype(jnp.float32),
    )
    own_routes = lax.dynamic_slice_in_dim(group_routes, own_start, row_count, 0)
    own_onehot = (own_routes[:, None] == jnp.arange(experts)[None, :]).astype(jnp.float32)
    router_probs = jax.nn.softmax(
        jnp.dot(inner_low, w_router, preferred_element_type=jnp.float32), axis=-1
    )
    gate_value = jnp.sum(router_probs * own_onehot, axis=-1, keepdims=True)
    mix_weights = jax.nn.softmax(
        jnp.dot(inner_low, w_mix, preferred_element_type=jnp.float32), axis=-1
    )
    combined = (
        hidden + mix_weights[:, 0:1] * dense_own + mix_weights[:, 1:2] * gate_value * expert_own
    )
    mixed_out = combined.astype(jnp.bfloat16).reshape(tokens.shape)
    upstream = cotangent.reshape(-1, width).astype(jnp.float32)
    grad_dense = (mix_weights[:, 0:1] * upstream).astype(jnp.bfloat16)
    grad_expert = (mix_weights[:, 1:2] * gate_value * upstream).astype(jnp.bfloat16)
    mix_upstream = jnp.stack(
        [
            jnp.sum(upstream * dense_own, axis=1),
            jnp.sum(upstream * gate_value * expert_own, axis=1),
        ],
        axis=1,
    )
    gate_upstream = mix_weights[:, 1:2] * jnp.sum(upstream * expert_own, axis=1, keepdims=True)
    mix_logit_grad = mix_weights * (
        mix_upstream - jnp.sum(mix_weights * mix_upstream, axis=1, keepdims=True)
    )
    router_logit_grad = gate_upstream * gate_value * (own_onehot - router_probs)
    group_dense, group_expert = (
        lax.all_gather(grad_dense, "node", axis=0, tiled=True),
        lax.all_gather(grad_expert, "node", axis=0, tiled=True),
    )
    grad_w_down = jnp.einsum(
        "td,tf->df", group_dense, dense_act, preferred_element_type=jnp.float32
    )
    act_grad = jnp.einsum("td,df->tf", group_dense, w_down, preferred_element_type=jnp.float32)
    pre_grad = gelu_backward(dense_pre, act_grad).astype(jnp.bfloat16)
    grad_w_up = jnp.einsum("td,tf->df", group_rows, pre_grad, preferred_element_type=jnp.float32)
    inner_grad = jnp.einsum("tf,df->td", pre_grad, w_up, preferred_element_type=jnp.float32)
    outgoing_grad = jnp.einsum(
        "ts,td->sd", slot_onehot, group_expert, preferred_element_type=jnp.float32
    )
    outgoing_grad = outgoing_grad.astype(jnp.bfloat16).reshape(experts, capacity, width)
    received_grad = lax.all_to_all(outgoing_grad, "expert", split_axis=0, concat_axis=0, tiled=True)
    flat_in = received.reshape(-1, width)
    flat_grad = received_grad.reshape(-1, width)
    pre_expert = jnp.dot(flat_in, up_local, preferred_element_type=jnp.float32)
    act_expert = jax.nn.gelu(pre_expert).astype(jnp.bfloat16)
    grad_expert_down = jnp.einsum(
        "rf,rd->fd", act_expert, flat_grad, preferred_element_type=jnp.float32
    )
    act_expert_grad = jnp.einsum(
        "rd,fd->rf", flat_grad, down_local, preferred_element_type=jnp.float32
    )
    pre_expert_grad = gelu_backward(pre_expert, act_expert_grad).astype(jnp.bfloat16)
    grad_expert_up = jnp.einsum(
        "rd,rf->df", flat_in, pre_expert_grad, preferred_element_type=jnp.float32
    )
    back_rows = jnp.einsum(
        "rf,df->rd", pre_expert_grad, up_local, preferred_element_type=jnp.float32
    )
    back_rows = back_rows.astype(jnp.bfloat16).reshape(received.shape)
    returned_grad = lax.all_to_all(back_rows, "expert", split_axis=0, concat_axis=0, tiled=True)
    inner_grad = inner_grad + jnp.einsum(
        "ts,sd->td",
        slot_onehot,
        returned_grad.reshape(-1, width),
        preferred_element_type=jnp.float32,
    )
    own_grad = lax.psum_scatter(
        inner_grad.astype(jnp.bfloat16), "node", scatter_dimension=0, tiled=True
    ).astype(jnp.float32)
    router_f32 = w_router.astype(jnp.float32)
    mix_f32 = w_mix.astype(jnp.float32)
    own_grad = own_grad + jnp.einsum(
        "te,de->td", router_logit_grad, router_f32, precision=HIGHEST_PRECISION
    )
    own_grad = own_grad + jnp.einsum(
        "te,de->td", mix_logit_grad, mix_f32, precision=HIGHEST_PRECISION
    )
    inner_f32 = inner_low.astype(jnp.float32)
    grad_router = jnp.einsum("td,te->de", inner_f32, router_logit_grad, precision=HIGHEST_PRECISION)
    grad_mix = jnp.einsum("td,te->de", inner_f32, mix_logit_grad, precision=HIGHEST_PRECISION)
    hidden_from_norm, grad_ln2 = norm_backward(own_grad, base_two, inverse_two, ln2_gain)
    hidden_grad = upstream + hidden_from_norm
    attn_grad = hidden_grad.astype(jnp.bfloat16)
    grad_w_out = jnp.einsum(
        "td,te->de", attended_low, attn_grad, preferred_element_type=jnp.float32
    )
    attended_grad = jnp.einsum("te,de->td", attn_grad, w_out, preferred_element_type=jnp.float32)
    attended_grad = attended_grad.astype(jnp.bfloat16).reshape(row_count, HEADS, HEAD_DIM)

    def backward_block(carry, block_index):
        key_grad, value_grad = carry
        block_start = block_index * block_rows
        scores = masked_scores(queries, seq_keys, own_start + block_start, scale)
        probs = jnp.exp(scores - log_totals[block_index][..., None])
        prob_grad = jnp.einsum(
            "qhd,khd->hqk", attended_grad, seq_values, preferred_element_type=jnp.float32
        )
        row_delta = jnp.sum(probs * prob_grad, axis=-1, keepdims=True)
        score_grad = (probs * (prob_grad - row_delta)).astype(jnp.bfloat16)
        query_grad = (
            jnp.einsum("hqk,khd->qhd", score_grad, seq_keys, preferred_element_type=jnp.float32)
            * scale
        )
        key_grad = (
            key_grad
            + jnp.einsum("hqk,qhd->khd", score_grad, queries, preferred_element_type=jnp.float32)
            * scale
        )
        value_grad = value_grad + jnp.einsum(
            "hqk,qhd->khd",
            probs.astype(jnp.bfloat16),
            attended_grad,
            preferred_element_type=jnp.float32,
        )
        return ((key_grad, value_grad), query_grad)

    zero_grads = jnp.zeros((seq_len, HEADS, HEAD_DIM), jnp.float32)
    (key_partial, value_partial), query_grads = lax.scan(
        backward_block, (zero_grads, zero_grads), jnp.arange(block_count)
    )
    key_grad, value_grad = (
        lax.psum_scatter(
            key_partial.astype(jnp.bfloat16), "node", scatter_dimension=0, tiled=True
        ).astype(jnp.float32),
        lax.psum_scatter(
            value_partial.astype(jnp.bfloat16), "node", scatter_dimension=0, tiled=True
        ).astype(jnp.float32),
    )
    query_grad = query_grads.reshape(row_count, HEADS, HEAD_DIM)
    packed_grad = (
        jnp.stack([query_grad, key_grad, value_grad], axis=1)
        .astype(jnp.bfloat16)
        .reshape(row_count, 3 * width)
    )
    grad_w_qkv = jnp.einsum(
        "td,te->de", normed_low, packed_grad, preferred_element_type=jnp.float32
    )
    normed_grad = jnp.einsum("te,de->td", packed_grad, w_qkv, preferred_element_type=jnp.float32)
    input_from_norm, grad_ln1 = norm_backward(normed_grad, base_one, inverse_one, ln1_gain)
    input_grad = (hidden_grad + input_from_norm).reshape(tokens.shape)
    mlp_grads = reduce_mlp(grad_w_up, grad_w_down)
    summed_grads = (
        lax.psum_scatter(grad_ln1, ("node", "expert"), scatter_dimension=0, tiled=True),
        lax.psum_scatter(grad_w_qkv, ("node", "expert"), scatter_dimension=0, tiled=True),
        lax.psum_scatter(grad_w_out, ("node", "expert"), scatter_dimension=0, tiled=True),
        lax.psum_scatter(grad_ln2, ("node", "expert"), scatter_dimension=0, tiled=True),
        lax.psum_scatter(grad_router, ("node", "expert"), scatter_dimension=0, tiled=True),
        lax.psum_scatter(grad_mix, ("node", "expert"), scatter_dimension=0, tiled=True),
    )
    return (
        mixed_out,
        input_grad,
        summed_grads[0],
        summed_grads[1],
        summed_grads[2],
        summed_grads[3],
        summed_grads[4],
        summed_grads[5],
        mlp_grads[0],
        mlp_grads[1],
        grad_expert_up[None],
        grad_expert_down[None],
    )


def solution(mesh):
    return jax.shard_map(
        shards,
        mesh=mesh,
        in_specs=(
            P("expert", "node", None),
            P("expert", "node", None),
            P("expert", None, None),
            P(),
            P(),
            P(),
            P(),
            P(),
            P(),
            P(None, "node"),
            P(None, "node"),
            P("expert", None, "node"),
            P("expert", "node", None),
        ),
        out_specs=(
            P("expert", "node", None),
            P("expert", "node", None),
            P(("node", "expert")),
            P(("node", "expert"), None),
            P(("node", "expert"), None),
            P(("node", "expert")),
            P(("node", "expert"), None),
            P(("node", "expert"), None),
            P("expert", "node"),
            P("expert", "node"),
            P("expert", None, "node"),
            P("expert", "node", None),
        ),
        check_vma=False,
    )
```

profile of v0, /device:TPU:0, one launch (start us, length us, event | category | flops | bytes accessed | tf_op | source)
XLA Modules:
  0.0 1580.5 jit_solution(3569802367145324202)
XLA Ops:
  28.8 11.7 all-gather.16.cloned.1.call-done
  40.6 16.4 %fusion.136 = (f32[16,512]{1,0:T(8,128)S(1)}, f32[16,512,1024]{2,1,0:T(8,128)}) fusion(bf16[1024,1,16,64]{0,3,2,1:T(8,128)(2,1)} %all-gather.16.cloned.1.call-done, bf16[512,3,16,64]{0,3,2,1:T(8,128)(2,1)} %bitcast.191, pred[512,1024]{1,0:T(8,128)(4,1)S(1)} %iota_compare_fusion.1), kind=kOutput, calls=%fused_computation.182 | convolution fusion | flops 1098899456 | bytes 37257216 | tf_op jit(solution)/shard_map/while/body/eval_jaxpr/qhd,khd->hqk/dot_general | solution.py:39
  57.0 14.3 fusion
  71.4 13.7 fusion.100
  106.4 78.7 %all_to_all.20 = bf16[16,96,1024]{2,1,0:T(8,128)(2,1)S(1)} all-to-all(bf16[16,96,1024]{2,1,0:T(8,128)(2,1)S(1)} %bitcast.206), channel_id=1, replica_groups=mesh['node'=2,'expert'=16] {'expert'}, dimensions={0} | all-to-all | bytes 6291456 | tf_op jit(solution)/shard_map/all_to_all | solution.py:126
  193.7 9.0 fusion.48
  224.4 43.0 %all-to-all-done.1 = bf16[16,96,1024]{2,1,0:T(8,128)(2,1)} async-done(((bf16[16,96,1024]{2,1,0:T(8,128)(2,1)}), bf16[16,96,1024]{2,1,0:T(8,128)(2,1)}, u32[]{:S(2)}, u32[]{:S(2)}) %all-to-all-start.1) | async-done | bytes 3145760 | tf_op jit(solution)/shard_map/all_to_all | solution.py:135
  275.4 17.4 %reduce-scatter.18.cloned.1.call-done = bf16[512,1024]{1,0:T(8,128)(2,1)} async-done(((bf16[1024,1024]{1,0:T(8,128)(2,1)}), bf16[512,1024]{1,0:T(8,128)(2,1)}) %reduce-scatter.18.cloned.1.call-update) | async-done | bytes 1048592 | tf_op jit(solution)/shard_map/reduce_scatter | solution.py:143
  298.8 12.0 all-gather.12.cloned.1.call-done
  316.1 78.9 %all_to_all.21 = bf16[16,96,1024]{2,1,0:T(8,128)(2,1)S(1)} all-to-all(bf16[16,96,1024]{2,1,0:T(8,128)(2,1)S(1)} %bitcast.205), channel_id=1, replica_groups=mesh['node'=2,'expert'=16] {'expert'}, dimensions={0} | all-to-all | bytes 6291456 | tf_op jit(solution)/shard_map/all_to_all | solution.py:190
  395.1 18.1 %fusion.12 = bf16[1536,2048]{1,0:T(8,128)(2,1)} fusion(f32[1536,2048]{1,0:T(8,128)} %copy-done.39, bf16[1536,1024]{1,0:T(8,128)(2,1)S(1)} %bitcast.199, bf16[1,2048,1024]{2,1,0:T(8,128)(2,1)S(1)} %copy-done.32), kind=kOutput, calls=%fused_computation.19 | convolution fusion | flops 6505365504 | bytes 26214400 | tf_op jit(solution)/shard_map/rd,fd->rf/dot_general | solution.py:198
  413.2 10.0 fusion.45
  428.6 13.8 all-gather.10.cloned.1.call-done
  442.4 13.6 fusion.19
  456.0 31.8 %all-to-all-done.3 = bf16[16,96,1024]{2,1,0:T(8,128)(2,1)} async-done(((bf16[16,96,1024]{2,1,0:T(8,128)(2,1)}), bf16[16,96,1024]{2,1,0:T(8,128)(2,1)}, u32[]{:S(2)}, u32[]{:S(2)}) %all-to-all-start.3) | async-done | bytes 3145760 | tf_op jit(solution)/shard_map/all_to_all | solution.py:209
  502.0 15.7 reduce-scatter.20.cloned.1.call-done
  529.8 14.9 convert_bitcast_fusion.1
  545.0 23.3 %multiply_reduce_fusion = (f32[16,512]{1,0:T(8,128)S(1)}, f32[16,512,1024]{2,1,0:T(8,128)}) fusion(f32[16,512,1024]{2,1,0:T(8,128)} %get-tuple-element.86, f32[16,512]{1,0:T(8,128)S(1)} %log_add_fusion, bf16[512,16,64]{0,2,1:T(8,128)(2,1)S(1)} %bitcast.194, bf16[1024,1,16,64]{0,3,2,1:T(8,128)(2,1)} %all-gather.14.cloned.1.call-done), kind=kOutput, calls=%fused_computation.1 | convolution fusion | flops 1098899456 | bytes 70320128 | tf_op jit(solution)/shard_map/while/body/eval_jaxpr/qhd,khd->hqk/dot_general | solution.py:244
  568.4 27.8 %multiply_convert_fusion = bf16[16,512,1024]{2,1,0:T(8,128)(2,1)} fusion(f32[16,512,1024]{2,1,0:T(8,128)} %get-tuple-element.95, f32[16,512,1024]{2,1,0:T(8,128)} %get-tuple-element.86, f32[16,512]{1,0:T(8,128)S(1)} %get-tuple-element.94, f32[16,512]{1,0:T(8,128)S(1)} %log_add_fusion), kind=kLoop, calls=%fused_computation | loop fusion | flops 33554432 | bytes 83951616 | tf_op jit(solution)/shard_map/while/body/eval_jaxpr/convert_element_type | solution.py:248
  596.1 10.5 fusion.99
  611.4 12.6 fusion.133
  624.1 10.7 fusion.141
  641.1 12.6 multiply_bitcast_fusion
  664.6 95.9 %reduce-scatter.36.cloned.1.call-done = f32[32,2]{1,0:T(8,128)} async-done(((f32[1024,2]{1,0:T(8,128)}), f32[32,2]{1,0:T(8,128)}) %reduce-scatter.36.cloned.1.call-update) | async-done | bytes 272
  761.8 136.6 %reduce-scatter.34.cloned.1.call-done = f32[32,16]{1,0:T(8,128)} async-done(((f32[1024,16]{1,0:T(8,128)}), f32[32,16]{1,0:T(8,128)}) %reduce-scatter.34.cloned.1.call-update) | async-done | bytes 2064
  899.8 12.0 convolution_bitcast_fusion.1
  911.7 13.6 convolution_bitcast_fusion
  930.7 41.5 %all-reduce.2 = (f32[1024]{0:T(1024)S(1)}, f32[1024]{0:T(1024)S(1)}) all-reduce(f32[1024]{0:T(1024)S(1)} %get-tuple-element.55, f32[1024]{0:T(1024)S(1)} %get-tuple-element.53), channel_id=9, replica_groups=mesh['node'=2,'expert'=16] {'node','expert'}, use_global_device_ids=true, to_apply=%region_29.30.clone | all-reduce | flops 2048 | bytes 16384
  977.5 99.8 %reduce-scatter.32.cloned.1.call-done = f32[64,2048]{1,0:T(8,128)} async-done(((f32[1024,2048]{1,0:T(8,128)}), f32[64,2048]{1,0:T(8,128)}) %reduce-scatter.32.cloned.1.call-update) | async-done | bytes 524304 | tf_op jit(solution)/shard_map/reduce_scatter | solution.py:50
  1077.3 183.0 %reduce-scatter.30.cloned.1.call-done = f32[64,2048]{1,0:T(8,128)} async-done(((f32[1024,2048]{1,0:T(8,128)}), f32[64,2048]{1,0:T(8,128)}) %reduce-scatter.30.cloned.1.call-update) | async-done | bytes 524304 | tf_op jit(solution)/shard_map/reduce_scatter | solution.py:49
  1260.4 152.5 %reduce-scatter.28.cloned.1.call-done = f32[32,1024]{1,0:T(8,128)} async-done(((f32[1024,1024]{1,0:T(8,128)}), f32[32,1024]{1,0:T(8,128)}) %reduce-scatter.28.cloned.1.call-update) | async-done | bytes 131088 | tf_op jit(solution)/shard_map/reduce_scatter | solution.py:294
  1412.9 160.8 %reduce-scatter.26.cloned.1.call-done = f32[32,3072]{1,0:T(8,128)} async-done(((f32[1024,3072]{1,0:T(8,128)}), f32[32,3072]{1,0:T(8,128)}) %reduce-scatter.26.cloned.1.call-update) | async-done | bytes 393232 | tf_op jit(solution)/shard_map/reduce_scatter | solution.py:293
  (187 shorter events, 159.2 us)
Async XLA Ops:
  7.2 78.0 %copy-start = (bf16[1024,1024]{1,0:T(8,128)(2,1)S(1)}, bf16[1024,1024]{1,0:T(8,128)(2,1)}, u32[]{:S(2)}) copy-start(bf16[1024,1024]{1,0:T(8,128)(2,1)} %param.18) | copy-start | bytes 6291460
  7.2 33.4 %all-gather.16.cloned.1.call-start = ((), (), s32[]{:S(2)}) async-start(), calls=%async_computation.28 | async-start | bytes 3145728 | tf_op jit(solution)/shard_map/all_gather | solution.py:82
  27.1 44.2 %all-gather.14.cloned.1.call-start = ((), (), s32[]{:S(2)}) async-start(), calls=%async_computation.27 | async-start | bytes 3145728 | tf_op jit(solution)/shard_map/all_gather | solution.py:83
  27.9 73.3 %all-gather.8.cloned.1.call-start = ((), (), s32[]{:S(2)}) async-start(), calls=%async_computation.15 | async-start | bytes 3145728 | tf_op jit(solution)/shard_map/all_gather | solution.py:107
  57.0 14.4 copy-start.18
  71.3 13.8 copy-start.21
  71.3 13.8 copy-start.6
  106.4 80.4 %copy-start.33 = (bf16[1,1024,2048]{2,1,0:T(8,128)(2,1)S(1)}, bf16[1,1024,2048]{2,1,0:T(8,128)(2,1)}, u32[]{:S(2)}) copy-start(bf16[1,1024,2048]{2,1,0:T(8,128)(2,1)} %param.24) | copy-start | bytes 12582916
  202.7 64.7 %all-to-all-start.1 = ((bf16[16,96,1024]{2,1,0:T(8,128)(2,1)}), bf16[16,96,1024]{2,1,0:T(8,128)(2,1)}, u32[]{:S(2)}, u32[]{:S(2)}) async-start(bf16[16,96,1024]{2,1,0:T(8,128)(2,1)} %bitcast.204), calls=%async_computation.2 | async-start | bytes 6291456 | tf_op jit(solution)/shard_map/all_to_all | solution.py:135
  207.2 68.2 %reduce-scatter.16.cloned.1.call-start = ((), (), s32[]{:S(2)}) async-start(), calls=%async_computation.16 | async-start | bytes 3145728 | tf_op jit(solution)/shard_map/reduce_scatter | solution.py:140
  224.4 68.5 %reduce-scatter.18.cloned.1.call-start = ((), (), s32[]{:S(2)}) async-start(), calls=%async_computation.17 | async-start | bytes 3145728 | tf_op jit(solution)/shard_map/reduce_scatter | solution.py:143
  274.4 36.4 %all-gather.12.cloned.1.call-start = ((), (), s32[]{:S(2)}) async-start(), calls=%async_computation.19 | async-start | bytes 3145728 | tf_op jit(solution)/shard_map/all_gather | solution.py:177
  316.1 78.9 %copy-start.32 = (bf16[1,2048,1024]{2,1,0:T(8,128)(2,1)S(1)}, bf16[1,2048,1024]{2,1,0:T(8,128)(2,1)}, u32[]{:S(2)}) copy-start(bf16[1,2048,1024]{2,1,0:T(8,128)(2,1)} %param.25) | copy-start | bytes 12582916
  395.1 18.2 %copy-start.14 = (bf16[16,96,1024]{2,1,0:T(8,128)(2,1)}, bf16[16,96,1024]{2,1,0:T(8,128)(2,1)S(1)}, u32[]{:S(2)}) copy-start(bf16[16,96,1024]{2,1,0:T(8,128)(2,1)S(1)} %all_to_all.21) | copy-start | bytes 9437188
  395.1 18.2 %copy-start.34 = (bf16[1,1024,2048]{2,1,0:T(8,128)(2,1)S(1)}, bf16[1,1024,2048]{2,1,0:T(8,128)(2,1)}, u32[]{:S(2)}) copy-start(bf16[1,1024,2048]{2,1,0:T(8,128)(2,1)} %param.24) | copy-start | bytes 12582916
  423.2 64.7 %all-to-all-start.3 = ((bf16[16,96,1024]{2,1,0:T(8,128)(2,1)}), bf16[16,96,1024]{2,1,0:T(8,128)(2,1)}, u32[]{:S(2)}, u32[]{:S(2)}) async-start(bf16[16,96,1024]{2,1,0:T(8,128)(2,1)} %bitcast.203), calls=%async_computation.5 | async-start | bytes 6291456 | tf_op jit(solution)/shard_map/all_to_all | solution.py:209
  427.7 14.7 all-gather.10.cloned.1.call-start
  428.4 89.3 %reduce-scatter.20.cloned.1.call-start = ((), (), s32[]{:S(2)}) async-start(), calls=%async_computation.20 | async-start | bytes 3145728 | tf_op jit(solution)/shard_map/reduce_scatter | solution.py:216
  499.3 154.4 %reduce-scatter.24.cloned.1.call-start = ((), (), s32[]{:S(2)}) async-start(), calls=%async_computation.22 | async-start | bytes 3145728 | tf_op jit(solution)/shard_map/reduce_scatter | solution.py:274
  502.0 20.4 %copy-start.8 = (bf16[1,512,1024]{2,1,0:T(8,128)(2,1)S(1)}, bf16[1,512,1024]{2,1,0:T(8,128)(2,1)}, u32[]{:S(2)}) copy-start(bf16[1,512,1024]{2,1,0:T(8,128)(2,1)} %param.14) | copy-start | bytes 3145732
  544.7 109.0 %reduce-scatter.22.cloned.1.call-start = ((), (), s32[]{:S(2)}) async-start(), calls=%async_computation.21 | async-start | bytes 3145728 | tf_op jit(solution)/shard_map/reduce_scatter | solution.py:271
  596.1 10.6 copy-start.4
  606.7 153.7 %reduce-scatter.36.cloned.1.call-start = ((), (), s32[]{:S(2)}) async-start(), calls=%async_computation.30 | async-start | bytes 540672
  608.8 289.6 %reduce-scatter.34.cloned.1.call-start = ((), (), s32[]{:S(2)}) async-start(), calls=%async_computation.29 | async-start | bytes 540672
  610.9 466.5 %reduce-scatter.32.cloned.1.call-start = ((), (), s32[]{:S(2)}) async-start(), calls=%async_computation.26 | async-start | bytes 8912896 | tf_op jit(solution)/shard_map/reduce_scatter | solution.py:50
  624.0 636.3 %reduce-scatter.30.cloned.1.call-start = ((), (), s32[]{:S(2)}) async-start(), calls=%async_computation.25 | async-start | bytes 8912896 | tf_op jit(solution)/shard_map/reduce_scatter | solution.py:49
  634.8 778.0 %reduce-scatter.28.cloned.1.call-start = ((), (), s32[]{:S(2)}) async-start(), calls=%async_computation.24 | async-start | bytes 4325376 | tf_op jit(solution)/shard_map/reduce_scatter | solution.py:294
  640.8 932.9 %reduce-scatter.26.cloned.1.call-start = ((), (), s32[]{:S(2)}) async-start(), calls=%async_computation.23 | async-start | bytes 12976128 | tf_op jit(solution)/shard_map/reduce_scatter | solution.py:293
  899.8 12.0 copy-start.15
  899.8 25.5 %slice-start = ((s8[6291456]{0:T(1024)(128)(4,1)}), s8[4194304]{0:T(1024)(128)(4,1)S(1)}, s32[]{:S(2)}) async-start(s8[6291456]{0:T(1024)(128)(4,1)} %bitcast.231), calls=%async_computation.31 | async-start | bytes 8388608
  911.7 13.6 copy-start.17
  911.7 13.6 slice-start.1
  (28 other events, 121.3 us)
Sparse Core Ops, SparseCore 0:
  27.3 13.2 all-gather.15
  42.7 11.7 all-gather.13
  89.4 11.7 all-gather.7
  224.5 10.9 reduce-scatter.15
  274.5 18.2 reduce-scatter.17
  298.9 11.8 all-gather.11
  430.6 11.7 all-gather.9
  499.4 18.2 reduce-scatter.19
  544.9 10.8 reduce-scatter.23
  606.8 10.8 reduce-scatter.21
  620.0 140.3 reduce-scatter.35
  762.5 135.8 reduce-scatter.33
  901.2 176.0 reduce-scatter.31
  1080.0 180.2 reduce-scatter.29
  1263.0 149.7 reduce-scatter.27
  1419.3 154.3 reduce-scatter.25
where the time goes:
time: 1580 us
  waiting for transfers between devices  983 us (62%)
  matrix products  281 us (18%)
  blocking collectives  199 us (13%)
  other arithmetic  66.9 us (4%)
  local copies, waits for them, and re-layouts  24.2 us (2%)
    unnamed x18, waiting for transfers between devices  234 us
    reduce_scatter x1, waiting for transfers between devices, reduce_mlp(): lax.psum_scatter(grad_up, 'expert', scatter_dimension=0, tiled=True)  183 us
    reduce_scatter x1, waiting for transfers between devices, shards(): lax.psum_scatter(grad_w_qkv, ('node', 'expert'), scatter_dimension=0, til...  161 us
    reduce_scatter x1, waiting for transfers between devices, shards(): lax.psum_scatter(grad_w_out, ('node', 'expert'), scatter_dimension=0, til...  152 us
    reduce_scatter x1, waiting for transfers between devices, reduce_mlp(): lax.psum_scatter(grad_down, 'expert', scatter_dimension=0, tiled=True)  99.8 us
    all_to_all x1, blocking collectives, shards(): lax.all_to_all(outgoing_grad, 'expert', split_axis=0, concat_axis=0, tile...  78.9 us
    all_to_all x1, blocking collectives, shards(): lax.all_to_all(outgoing, 'expert', split_axis=0, concat_axis=0, tiled=True)  78.7 us
    all_to_all x1, waiting for transfers between devices, shards(): lax.all_to_all(results[-1], 'expert', split_axis=0, concat_axis=0, tiled=...  43 us
  transfers between devices with their start and end apart: 18, of which 14 were waited for; matrix products, arithmetic and copies ran while one was open for 14% of the time, Pallas kernels for 0%

commit v1 on v0

v1 whole, which is shorter than its diff:
```python
import functools

import jax
import jax.numpy as jnp
from jax import lax
from jax.experimental import pallas as pl
from jax.experimental.pallas import tpu as pltpu
from jax.sharding import PartitionSpec as P

HEAD_DIM = 64
EPS = 1e-05
LANES = 128
LOG2E = 1.4426950408889634
GELU_A = 0.7978845608028654
GELU_B = 0.044715
SWAP = [(0, 1), (1, 0)]
F32 = jnp.float32
BF16 = jnp.bfloat16


def dot(left, right):
    return jnp.dot(left, right, preferred_element_type=F32)


def dot_t(left, right):
    return lax.dot_general(left, right, (((1,), (1,)), ((), ())), preferred_element_type=F32)


def dot_n(left, right):
    return lax.dot_general(left, right, (((0,), (0,)), ((), ())), preferred_element_type=F32)


def layer_norm(values, gain):
    average = jnp.mean(values, axis=-1, keepdims=True)
    centered = values - average
    inverse = lax.rsqrt(jnp.mean(centered * centered, axis=-1, keepdims=True) + EPS)
    normed = centered * inverse
    return (normed * gain, normed, inverse)


def norm_backward(upstream, normed, inverse, gain):
    scaled = upstream * gain
    inner_term = (
        scaled
        - jnp.mean(scaled, axis=-1, keepdims=True)
        - normed * jnp.mean(scaled * normed, axis=-1, keepdims=True)
    )
    return inner_term * inverse


QB = 256


def attend_kernel(qkv_ref, out_ref, lse_ref, ot_ref):
    seq = qkv_ref.shape[0]
    factor = HEAD_DIM ** (-0.5) * LOG2E
    lane = lax.broadcasted_iota(jnp.int32, (1, LANES), 1)
    v_t = qkv_ref[:, 2 * LANES : 3 * LANES].T
    below = lax.broadcasted_iota(jnp.int32, (QB, QB), 0) <= lax.broadcasted_iota(
        jnp.int32, (QB, QB), 1
    )
    for head in range(2):
        keep = (lane // HEAD_DIM) == head
        keys = jnp.where(keep, qkv_ref[:, LANES : 2 * LANES], 0)
        v_rows = v_t[head * HEAD_DIM : (head + 1) * HEAD_DIM]
        for block in range(seq // QB):
            lo, hi = block * QB, (block + 1) * QB
            queries = qkv_ref[lo:hi, 0:LANES]
            diag = jnp.where(below, dot_t(keys[lo:hi], queries), -1e30)
            top = jnp.max(diag, axis=0, keepdims=True)
            if lo:
                past = dot_t(keys[:lo], queries)
                top = jnp.maximum(top, jnp.max(past, axis=0, keepdims=True))
            p_diag = jnp.exp2((diag - top) * factor)
            total = jnp.sum(p_diag, axis=0, keepdims=True)
            acc = dot(v_rows[:, lo:hi], p_diag.astype(BF16))
            if lo:
                p_past = jnp.exp2((past - top) * factor)
                total = total + jnp.sum(p_past, axis=0, keepdims=True)
                acc = acc + dot(v_rows[:, :lo], p_past.astype(BF16))
            ot_ref[head * HEAD_DIM : (head + 1) * HEAD_DIM, lo:hi] = acc * (1.0 / total)
            lse_ref[0, head : head + 1, lo:hi] = top * factor + jnp.log2(total)
    out_ref[...] = ot_ref[...].T.astype(BF16)


def attend(qkv, pairs):
    seq = qkv.shape[0]
    return pl.pallas_call(
        attend_kernel,
        grid=(pairs,),
        in_specs=[pl.BlockSpec((seq, 3 * LANES), lambda j: (0, j))],
        out_specs=[
            pl.BlockSpec((seq, LANES), lambda j: (0, j)),
            pl.BlockSpec((1, 8, seq), lambda j: (j, 0, 0)),
        ],
        out_shape=[
            jax.ShapeDtypeStruct((seq, pairs * LANES), BF16),
            jax.ShapeDtypeStruct((pairs, 8, seq), F32),
        ],
        scratch_shapes=[pltpu.VMEM((LANES, seq), F32)],
        cost_estimate=pl.CostEstimate(
            flops=pairs * 8 * seq * seq * LANES,
            bytes_accessed=pairs * seq * LANES * 8,
            transcendentals=pairs * seq * seq,
        ),
        compiler_params=pltpu.CompilerParams(vmem_limit_bytes=32 << 20),
        name="attend",
    )(qkv)


def attend_back_kernel(qkv_ref, out_ref, grad_ref, lse_ref, packed_ref, dqt_ref, dk_ref, dv_ref):
    seq = qkv_ref.shape[0]
    scale = HEAD_DIM ** (-0.5)
    factor = scale * LOG2E
    lane = lax.broadcasted_iota(jnp.int32, (1, LANES), 1)
    k_t = qkv_ref[:, LANES : 2 * LANES].T
    product = (grad_ref[...].astype(F32) * out_ref[...].astype(F32)).T
    below = lax.broadcasted_iota(jnp.int32, (QB, QB), 0) <= lax.broadcasted_iota(
        jnp.int32, (QB, QB), 1
    )
    dk_ref[...] = jnp.zeros_like(dk_ref)
    dv_ref[...] = jnp.zeros_like(dv_ref)
    for head in range(2):
        keep = (lane // HEAD_DIM) == head
        rows = slice(head * HEAD_DIM, (head + 1) * HEAD_DIM)
        keys = jnp.where(keep, qkv_ref[:, LANES : 2 * LANES], 0)
        values = jnp.where(keep, qkv_ref[:, 2 * LANES : 3 * LANES], 0)
        delta = jnp.sum(product[rows], axis=0, keepdims=True)
        for block in range(seq // QB):
            lo, hi = block * QB, (block + 1) * QB
            queries = jnp.where(keep, qkv_ref[lo:hi, 0:LANES], 0)
            grads = jnp.where(keep, grad_ref[lo:hi], 0)
            lse = lse_ref[0, head : head + 1, lo:hi]
            drop = delta[:, lo:hi]
            acc = None
            for start, stop in ((lo, hi), (0, lo)):
                if start == stop:
                    continue
                probs = jnp.exp2(dot_t(keys[start:stop], queries) * factor - lse)
                if start == lo:
                    probs = jnp.where(below, probs, 0.0)
                prob_grad = dot_t(values[start:stop], grads)
                score_grad = (probs * (prob_grad - drop)).astype(BF16)
                dv_ref[start:stop] += dot(probs.astype(BF16), grads)
                dk_ref[start:stop] += dot(score_grad, queries)
                part = dot(k_t[rows, start:stop], score_grad)
                acc = part if acc is None else acc + part
            dqt_ref[rows, lo:hi] = acc
    packed_ref[:, 0:LANES] = (dqt_ref[...].T * scale).astype(BF16)
    packed_ref[:, LANES : 2 * LANES] = (dk_ref[...] * scale).astype(BF16)
    packed_ref[:, 2 * LANES : 3 * LANES] = dv_ref[...].astype(BF16)


def attend_back(qkv, attended, grad, lse):
    seq = qkv.shape[0]
    pairs = lse.shape[0]
    return pl.pallas_call(
        attend_back_kernel,
        grid=(pairs,),
        in_specs=[
            pl.BlockSpec((seq, 3 * LANES), lambda j: (0, j)),
            pl.BlockSpec((seq, LANES), lambda j: (0, j)),
            pl.BlockSpec((seq, LANES), lambda j: (0, j)),
            pl.BlockSpec((1, 8, seq), lambda j: (j, 0, 0)),
        ],
        out_specs=pl.BlockSpec((seq, 3 * LANES), lambda j: (0, j)),
        out_shape=jax.ShapeDtypeStruct(qkv.shape, BF16),
        scratch_shapes=[
            pltpu.VMEM((LANES, seq), F32),
            pltpu.VMEM((seq, LANES), F32),
            pltpu.VMEM((seq, LANES), F32),
        ],
        cost_estimate=pl.CostEstimate(
            flops=pairs * 20 * seq * seq * LANES,
            bytes_accessed=pairs * seq * LANES * 16,
            transcendentals=pairs * seq * seq,
        ),
        compiler_params=pltpu.CompilerParams(vmem_limit_bytes=32 << 20),
        name="attend_back",
    )(qkv, attended, grad, lse)


def branch_kernel(dense, experts, x_ref, c_ref, sel_ref, wc_ref, wct_ref, up_ref, dn_ref, *refs):
    if dense:
        out_ref, dx_ref, gup_ref, gdn_ref, gsm_ref, probs_ref = refs[:6]
        xt_ref, g_ref, a_ref, acc_ref, dxa_ref, act_ref, dpre_ref, gt_ref = refs[6:]
    else:
        out_ref, dx_ref, gup_ref, gdn_ref, gsm_ref = refs[:5]
        xt_ref, g_ref, a_ref, acc_ref, dxa_ref, act_ref, dpre_ref = refs[5:]
    halves, rows, half = x_ref.shape
    width = halves * half
    step = pl.program_id(0)
    small = 256
    big = 512
    split = [slice(n * half, (n + 1) * half) for n in range(halves)]

    @pl.when(step == 0)
    def _():
        lane = lax.broadcasted_iota(jnp.int32, (1, LANES), 1)
        is_router = lane < experts
        is_mix = (lane >= experts) & (lane < experts + 2)
        picked = sel_ref[...]
        first = (lane == experts).astype(F32)
        second = (lane == experts + 1).astype(F32)

        def prepare(index, carry):
            at = pl.ds(pl.multiple_of(index * small, small), small)
            logits = sum(dot(x_ref[n, at, :], wc_ref[split[n], :]) for n in range(halves))

            def soft(mask):
                masked = jnp.where(mask, logits, -1e30)
                shifted = jnp.exp(masked - jnp.max(masked, axis=1, keepdims=True))
                return shifted / jnp.sum(shifted, axis=1, keepdims=True)

            mix = soft(is_mix)
            if dense:
                factor = jnp.sum(mix * first, axis=1, keepdims=True)
                probs_ref[at, :] = jnp.where(is_router, soft(is_router), mix)
                a_ref[at, :] = jnp.where(is_mix, first - mix, 0.0)
            else:
                router = soft(is_router)
                gate = jnp.sum(router * picked, axis=1, keepdims=True)
                factor = gate * jnp.sum(mix * second, axis=1, keepdims=True)
                a_ref[at, :] = jnp.where(
                    is_router, picked - router, jnp.where(is_mix, second - mix, 0.0)
                )
            for n in range(halves):
                xt_ref[split[n], at] = x_ref[n, at, :].T
                scaled = (factor * c_ref[n, at, :].astype(F32)).astype(BF16)
                g_ref[at, split[n]] = scaled
                if dense:
                    gt_ref[split[n], at] = scaled.T
            acc_ref[at, :] = jnp.zeros((small, width), F32)
            dxa_ref[at, :] = jnp.zeros((small, width), F32)
            return carry

        lax.fori_loop(0, rows // small, prepare, 0)

    def forward(index, carry):
        at = pl.ds(pl.multiple_of(index * big, big), big)
        pre = sum(dot(x_ref[n, at, :], up_ref[split[n], :]) for n in range(halves))
        square = pre * pre
        bend = jnp.tanh(pre * (GELU_A + GELU_A * GELU_B * square))
        side = 0.5 * (1.0 + bend)
        act = (pre * side).astype(BF16)
        slope = side + 0.5 * pre * (1.0 - bend * bend) * (GELU_A + 3.0 * GELU_A * GELU_B * square)
        act_ref[at, :] = act
        if dense:
            act_grad = dot(g_ref[at, :], dn_ref[...])
            acc_ref[at, :] += dot_t(act, dn_ref[...])
        else:
            act_grad = dot_t(g_ref[at, :], dn_ref[...])
            acc_ref[at, :] += dot(act, dn_ref[...])
        pre_grad = (slope * act_grad).astype(BF16)
        dpre_ref[at, :] = pre_grad
        dxa_ref[at, :] += dot_t(pre_grad, up_ref[...])
        return carry

    lax.fori_loop(0, rows // big, forward, 0)

    def weights(index, carry):
        at = pl.ds(pl.multiple_of(index * small, small), small)
        gup_ref[at, :] = dot(xt_ref[at, :], dpre_ref[...]).astype(gup_ref.dtype)
        if dense:
            gdn_ref[at, :] = dot(gt_ref[at, :], act_ref[...]).astype(gdn_ref.dtype)
        return carry

    lax.fori_loop(0, width // small, weights, 0)
    if not dense:
        gdn_ref[...] = dot_n(act_ref[...], g_ref[...]).astype(gdn_ref.dtype)

    @pl.when(step == pl.num_programs(0) - 1)
    def _():
        def finish(index, carry):
            at = pl.ds(pl.multiple_of(index * small, small), small)
            out = acc_ref[at, :]
            strength = jnp.sum(g_ref[at, :].astype(F32) * out, axis=1, keepdims=True)
            logit_grad = (strength * a_ref[at, :]).astype(BF16)
            act_ref[at, 0:LANES] = logit_grad
            grads = dxa_ref[at, :] + dot(logit_grad, wct_ref[...])
            if dense:
                mixes = probs_ref[at, :]
                lane = lax.broadcasted_iota(jnp.int32, (1, LANES), 1)
                first = jnp.sum(jnp.where(lane == experts, mixes, 0.0), axis=1, keepdims=True)
                out = out * first
            for n in range(out_ref.shape[0]):
                block = slice(n * out_ref.shape[2], (n + 1) * out_ref.shape[2])
                out_ref[n, at, :] = out[:, block].astype(BF16)
                dx_ref[n, at, :] = grads[:, block].astype(BF16)
            return carry

        lax.fori_loop(0, rows // small, finish, 0)
        gsm_ref[...] = dot(xt_ref[...], act_ref[:, 0:LANES])


def branch(x, c, picked, weights, weights_t, up, down, experts, dense):
    halves, rows, half = x.shape
    width = halves * half
    hidden = up.shape[1]
    block = 256
    up_spec = pl.BlockSpec((width, block), lambda f: (0, f))
    down_spec = up_spec if dense else pl.BlockSpec((block, width), lambda f: (f, 0))
    whole = lambda shape: pl.BlockSpec(
        shape, lambda f: (0,) * len(shape), pipeline_mode=pl.Buffered(1)
    )
    grad_type = BF16 if dense else F32
    result = (1, rows, width) if dense else (halves, rows, half)
    outs = [
        (whole(result), jax.ShapeDtypeStruct(result, BF16)),
        (whole(result), jax.ShapeDtypeStruct(result, BF16)),
        (up_spec, jax.ShapeDtypeStruct(up.shape, grad_type)),
        (down_spec, jax.ShapeDtypeStruct(down.shape, grad_type)),
        (whole((width, LANES)), jax.ShapeDtypeStruct((width, LANES), F32)),
    ]
    scratch = [
        pltpu.VMEM((width, rows), BF16),
        pltpu.VMEM((rows, width), BF16),
        pltpu.VMEM((rows, LANES), F32),
        pltpu.VMEM((rows, width), F32),
        pltpu.VMEM((rows, width), F32),
        pltpu.VMEM((rows, block), BF16),
        pltpu.VMEM((rows, block), BF16),
    ]
    if dense:
        outs.append((whole((rows, LANES)), jax.ShapeDtypeStruct((rows, LANES), F32)))
        scratch.append(pltpu.VMEM((width, rows), BF16))
    return pl.pallas_call(
        functools.partial(branch_kernel, dense, experts),
        grid=(hidden // block,),
        in_specs=[
            whole(x.shape),
            whole(c.shape),
            whole((1, LANES)),
            whole((width, LANES)),
            whole((LANES, width)),
            up_spec,
            down_spec,
        ],
        out_specs=[spec for spec, _ in outs],
        out_shape=[shape for _, shape in outs],
        scratch_shapes=scratch,
        cost_estimate=pl.CostEstimate(
            flops=12 * rows * width * hidden,
            bytes_accessed=12 * width * hidden + 8 * rows * width,
            transcendentals=rows * hidden,
        ),
        compiler_params=pltpu.CompilerParams(vmem_limit_bytes=58 << 20),
        name="dense_branch" if dense else "expert_branch",
    )(x, c, picked, weights, weights_t, up, down)


def shards(
    tokens,
    cotangent,
    routes,
    ln1_gain,
    w_qkv,
    w_out,
    ln2_gain,
    w_router,
    w_mix,
    w_up,
    w_down,
    expert_up,
    expert_down,
):
    node = lax.axis_index("node")
    member = lax.axis_index("expert")
    members = lax.axis_size("expert")
    width = tokens.shape[2]
    half = width // 2
    own_rows = tokens.shape[1]
    seq = 2 * own_rows
    experts = w_router.shape[1]
    capacity = 3 * seq // (2 * experts)
    slots = experts * capacity
    pairs = half // LANES
    own_start = node * own_rows

    seq_tokens = lax.all_gather(tokens[0], "node", axis=0, tiled=True)
    seq_cot = lax.all_gather(cotangent[0], "node", axis=0, tiled=True)

    group_routes = routes.reshape(-1)
    route_onehot = group_routes[:, None] == jnp.arange(experts)[None, :]
    ones = route_onehot.astype(BF16)
    row_at = jnp.arange(seq)
    earlier = (row_at[:, None] > row_at[None, :]).astype(BF16)
    order = jnp.sum(
        jnp.where(route_onehot, dot(earlier, ones), 0.0), axis=1
    ).astype(jnp.int32)
    place = jnp.where(order < capacity, group_routes * capacity + order, slots)
    slot_onehot = (place[:, None] == jnp.arange(slots)[None, :]).astype(BF16)

    def dispatch(rows):
        part = lax.dynamic_slice_in_dim(rows, node * half, half, 1)
        sent = dot_n(slot_onehot, part).astype(BF16).reshape(experts, capacity, half)
        got = lax.all_to_all(sent, "expert", split_axis=0, concat_axis=0, tiled=True)
        return lax.all_gather(got.reshape(slots, half), "node", axis=0)

    def give_back(parts):
        other = lax.ppermute(
            lax.dynamic_index_in_dim(parts, 1 - node, 0, False), "node", SWAP
        )
        mine = lax.dynamic_index_in_dim(parts, node, 0, False)
        total = (mine.astype(F32) + other.astype(F32)).astype(BF16)
        got = lax.all_to_all(
            total.reshape(experts, capacity, half), "expert", split_axis=0, concat_axis=0, tiled=True
        )
        return dot(slot_onehot, got.reshape(slots, half))

    expert_cot = dispatch(seq_cot)

    w_own = lax.dynamic_slice_in_dim(w_qkv.reshape(width, 3, width), node * half, half, 2)
    w_own = w_own.reshape(width, 3, pairs, LANES).transpose(0, 2, 1, 3).reshape(width, 3 * half)
    rows_f32 = seq_tokens.astype(F32)
    normed_one, _, _ = layer_norm(rows_f32, ln1_gain)
    normed_low = normed_one.astype(BF16)
    qkv = dot(normed_low, w_own).astype(BF16)
    attended_own, lse = attend(qkv, pairs)
    attended = lax.all_gather(attended_own, "node", axis=0)
    hidden = rows_f32 + dot(attended[0], w_out[:half]) + dot(attended[1], w_out[half:])
    normed_two, base_two, inverse_two = layer_norm(hidden, ln2_gain)
    inner_low = normed_two.astype(BF16)

    expert_rows = dispatch(inner_low)
    head = jnp.concatenate(
        [w_router, w_mix, jnp.zeros((width, LANES - experts - 2), BF16)], axis=1
    )
    head_t = head.T
    picked = (jnp.arange(LANES) == member).astype(F32)[None]
    dense_out, dense_dx, grad_up, grad_down, small_dense, probs = branch(
        inner_low[None], seq_cot[None], picked, head, head_t, w_up, w_down, experts, True
    )
    expert_out, expert_dx, grad_expert_up, grad_expert_down, small_expert = branch(
        expert_rows, expert_cot, picked, head, head_t, expert_up[0], expert_down[0], experts, False
    )
    grad_w_up = lax.psum_scatter(grad_up, "expert", scatter_dimension=0, tiled=True)
    grad_w_down = lax.psum_scatter(grad_down, "expert", scatter_dimension=0, tiled=True)

    dense_other = lax.ppermute(dense_dx[0], "node", SWAP)
    token_dx = give_back(expert_dx).astype(BF16)
    token_other = lax.ppermute(token_dx, "node", SWAP)

    def by_node(mine, other):
        return jnp.where(
            node == 0,
            jnp.concatenate([mine, other], axis=1),
            jnp.concatenate([other, mine], axis=1),
        )

    inner_grad = (
        dense_dx[0].astype(F32)
        + dense_other.astype(F32)
        + by_node(token_dx, token_other).astype(F32)
    )
    hidden_grad = seq_cot.astype(F32) + norm_backward(inner_grad, base_two, inverse_two, ln2_gain)
    grad_ln2 = 0.5 * jnp.sum(inner_grad * base_two, axis=0)
    attn_grad = hidden_grad.astype(BF16)
    w_out_own = lax.dynamic_slice_in_dim(w_out, node * half, half, 0)
    grad_w_out = dot_n(attended_own, attn_grad).astype(BF16)
    grad_w_out = lax.psum_scatter(grad_w_out, "expert", scatter_dimension=0, tiled=True)
    attended_grad = dot_t(attn_grad, w_out_own).astype(BF16)
    packed_grad = attend_back(qkv, attended_own, attended_grad, lse)

    token_out = give_back(expert_out)
    gate = jnp.sum(jnp.where(route_onehot, probs[:, :experts], 0.0), axis=1, keepdims=True)
    weight = gate * probs[:, experts + 1 : experts + 2]
    scaled = weight * token_out
    total_out = dense_out[0].astype(F32) + by_node(scaled, jnp.zeros_like(scaled))
    total_out = total_out.astype(BF16)

    def own_sum(partial):
        mine = lax.dynamic_slice_in_dim(partial, own_start, own_rows, 0)
        other = lax.dynamic_slice_in_dim(partial, own_rows - own_start, own_rows, 0)
        return mine.astype(F32) + lax.ppermute(other, "node", SWAP).astype(F32)

    hidden_own = lax.dynamic_slice_in_dim(hidden, own_start, own_rows, 0)
    mixed_out = (hidden_own + own_sum(total_out)).astype(BF16).reshape(tokens.shape)

    grad_qkv = dot_n(normed_low, packed_grad)
    normed_grad = own_sum(dot_t(packed_grad, w_own).astype(BF16))
    _, base_one, inverse_one = layer_norm(tokens[0].astype(F32), ln1_gain)
    input_grad = lax.dynamic_slice_in_dim(hidden_grad, own_start, own_rows, 0) + norm_backward(
        normed_grad, base_one, inverse_one, ln1_gain
    )
    grad_ln1 = jnp.sum(normed_grad * base_one, axis=0)
    small = small_dense + small_expert
    small = jnp.concatenate(
        [
            small[:, : experts + 2],
            grad_ln1[:, None],
            grad_ln2[:, None],
            jnp.zeros((width, LANES - experts - 4), F32),
        ],
        axis=1,
    )
    last = jnp.concatenate([grad_qkv.astype(BF16), small.astype(BF16)], axis=1)
    shard = width // (2 * members)
    last = last.reshape(2, members, shard, -1).transpose(1, 0, 2, 3).reshape(width, -1)
    last = lax.psum_scatter(last, "expert", scatter_dimension=0, tiled=True)
    last = last.reshape(2, shard, -1)
    kept = lax.dynamic_index_in_dim(last, node, 0, False)
    other = lax.ppermute(lax.dynamic_index_in_dim(last, 1 - node, 0, False), "node", SWAP)

    def columns(rows):
        return rows[:, : 3 * half].reshape(shard, pairs, 3, LANES).transpose(0, 2, 1, 3)

    grad_w_qkv = jnp.where(
        node == 0,
        jnp.concatenate([columns(kept), columns(other)], axis=2),
        jnp.concatenate([columns(other), columns(kept)], axis=2),
    )
    grad_w_qkv = grad_w_qkv.reshape(shard, 3 * width).astype(F32)
    small = kept[:, 3 * half :].astype(F32) + other[:, 3 * half :].astype(F32)
    return (
        mixed_out,
        input_grad.reshape(tokens.shape),
        small[:, experts + 2],
        grad_w_qkv,
        grad_w_out.astype(F32),
        small[:, experts + 3],
        small[:, :experts],
        small[:, experts : experts + 2],
        grad_w_up.astype(F32),
        grad_w_down.astype(F32),
        grad_expert_up[None],
        grad_expert_down[None],
    )


def solution(mesh):
    return jax.shard_map(
        shards,
        mesh=mesh,
        in_specs=(
            P("expert", "node", None),
            P("expert", "node", None),
            P("expert", None, None),
            P(),
            P(),
            P(),
            P(),
            P(),
            P(),
            P(None, "node"),
            P(None, "node"),
            P("expert", None, "node"),
            P("expert", "node", None),
        ),
        out_specs=(
            P("expert", "node", None),
            P("expert", "node", None),
            P(("node", "expert")),
            P(("node", "expert"), None),
            P(("node", "expert"), None),
            P(("node", "expert")),
            P(("node", "expert"), None),
            P(("node", "expert"), None),
            P("expert", "node"),
            P("expert", "node"),
            P("expert", None, "node"),
            P("expert", "node", None),
        ),
        check_vma=False,
    )
```

time: 1580 us -> 608 us (0.38)
  waiting for transfers between devices: 983 us -> 252 us
  matrix products: 281 us -> 41.6 us
  blocking collectives: 199 us -> 0 us
  Pallas kernels: 0 us -> 154 us
  starting transfers between devices: 11.6 us -> 49.5 us
  other arithmetic: 66.9 us -> 47.5 us
  local copies, waits for them, and re-layouts: 24.2 us -> 40.7 us
    reduce_scatter x9 -> x4, waiting for transfers between devices: 629 us -> 115 us  [the longest x1 76 us: shards(): lax.psum_scatter(grad_w_out, 'expert', scatter_dimension=0, tiled=True)]
    dot_general x32 -> x12, matrix products: 277 us -> 41.6 us  [the longest x6 18.8 us: dot(): return jnp.dot(left, right, preferred_element_type=F32)]
    unnamed x18 -> x9, waiting for transfers between devices: 234 us -> 2.17 us
    all_to_all x2 -> x0, blocking collectives: 158 us -> none  [the longest x1 78.9 us: shards(): lax.all_to_all(outgoing_grad, 'expert', split_axis=0, concat_axis=0, tile...]
    pallas_call x0 -> x4, Pallas kernels: none -> 154 us  [the longest x2 121 us: branch(): pl.pallas_call(functools.partial(branch_kernel, dense, experts), grid=(hi...]
    all_to_all x2 -> x4, waiting for transfers between devices: 74.9 us -> 127 us  [the longest x2 80.9 us: give_back(): lax.all_to_all(total.reshape(experts, capacity, half), 'expert', split_ax...]
    all_gather x5, waiting for transfers between devices: 44.5 us -> 1.16 us  [the longest x1 1.08 us: shards(): seq_tokens = lax.all_gather(tokens[0], 'node', axis=0, tiled=True)]
    unnamed x1 -> x0, blocking collectives: 41.5 us -> none
  transfers between devices with their start and end apart: 18 -> 20, of which waited for: 14 -> 9; matrix products, arithmetic and copies ran while one was open for 14% -> 20% of each run, Pallas kernels for 0% -> 26%
where the time goes in v1:
time: 608 us; the launch traced here: 600 us
  waiting for transfers between devices  252 us (41%)
  Pallas kernels  154 us (25%)
  starting transfers between devices  49.5 us (8%)
  other arithmetic  47.5 us (8%)
  matrix products  41.6 us (7%)
  local copies, waits for them, and re-layouts  40.7 us (7%)
  between operations  14.7 us (2%)
    pallas_call x2, Pallas kernels, branch(): pl.pallas_call(functools.partial(branch_kernel, dense, experts), grid=(hi...  121 us
    all_to_all x2, waiting for transfers between devices, give_back(): lax.all_to_all(total.reshape(experts, capacity, half), 'expert', split_ax...  80.9 us
    reduce_scatter x1, waiting for transfers between devices, shards(): lax.psum_scatter(grad_w_out, 'expert', scatter_dimension=0, tiled=True)  76 us
    all_to_all x2, waiting for transfers between devices, dispatch(): lax.all_to_all(sent, 'expert', split_axis=0, concat_axis=0, tiled=True)  46.4 us
    reduce_scatter x1, waiting for transfers between devices, shards(): last = lax.psum_scatter(last, 'expert', scatter_dimension=0, tiled=True)  38.9 us
    all_to_all x2, starting transfers between devices, give_back(): lax.all_to_all(total.reshape(experts, capacity, half), 'expert', split_ax...  20.8 us
    dot_general x6, matrix products, dot(): return jnp.dot(left, right, preferred_element_type=F32)  18.8 us
    pallas_call x1, Pallas kernels, attend_back(): pl.pallas_call(attend_back_kernel, grid=(pairs,), in_specs=[pl.BlockSpec(...  18.5 us
  transfers between devices with their start and end apart: 20, of which 9 were waited for; matrix products, arithmetic and copies ran while one was open for 20% of the time, Pallas kernels for 26%

profile of v1, /device:TPU:0, one launch (start us, length us, event | category | flops | bytes accessed | tf_op | source)
XLA Modules:
  0.0 600.0 jit_solution(12207086373860575061)
XLA Ops:
  8.7 8.6 %copy.110 = bf16[1024,3072]{0,1:T(8,128)(2,1)} copy(bf16[1024,3072]{1,0:T(8,128)(2,1)} %param.17) | data formatting | bytes 12582912 | tf_op args[4]
  26.4 5.9 convolution_convert_fusion.1.qkv_ref
  32.3 14.6 %attend.1 = (bf16[1024,512]{1,0:T(8,128)(2,1)}, f32[4,8,1024]{2,1,0:T(8,128)S(1)}) custom-call(bf16[1024,1536]{1,0:T(8,128)(2,1)S(1)} %convolution_convert_fusion.1.qkv_ref), custom_call_target="tpu_custom_call" | custom-call | flops 4294967296 | bytes 4194304 | tf_op jit(solution)/shard_map/attend/pallas_call | solution.py:88
  47.9 4.5 fusion.21
  52.4 7.4 %all-to-all-start.1 = ((bf16[16,96,512]{2,1,0:T(8,128)(2,1)}), bf16[16,96,512]{2,1,0:T(8,128)(2,1)}, u32[]{:S(2)}, u32[]{:S(2)}) async-start(bf16[16,96,512]{2,1,0:T(8,128)(2,1)} %bitcast.140), calls=%async_computation.1 | async-start | bytes 3145728 | tf_op jit(solution)/shard_map/all_to_all | solution.py:397
  59.8 11.9 %all-gather.11.cloned.1.call-start = ((), (), s32[]{:S(2)}) async-start(), calls=%async_computation.9 | async-start | bytes 4718592 | tf_op jit(solution)/shard_map/all_gather | solution.py:398
  80.5 13.4 %all-to-all-done.1 = bf16[16,96,512]{2,1,0:T(8,128)(2,1)} async-done(((bf16[16,96,512]{2,1,0:T(8,128)(2,1)}), bf16[16,96,512]{2,1,0:T(8,128)(2,1)}, u32[]{:S(2)}, u32[]{:S(2)}) %all-to-all-start.1) | async-done | bytes 1572896 | tf_op jit(solution)/shard_map/all_to_all | solution.py:397
  94.0 4.5 fusion.20
  98.5 7.8 %all-to-all-start = ((bf16[16,96,512]{2,1,0:T(8,128)(2,1)}), bf16[16,96,512]{2,1,0:T(8,128)(2,1)}, u32[]{:S(2)}, u32[]{:S(2)}) async-start(bf16[16,96,512]{2,1,0:T(8,128)(2,1)} %bitcast.141), calls=%async_computation | async-start | bytes 3145728 | tf_op jit(solution)/shard_map/all_to_all | solution.py:397
  107.0 32.9 %all-to-all-done = bf16[16,96,512]{2,1,0:T(8,128)(2,1)} async-done(((bf16[16,96,512]{2,1,0:T(8,128)(2,1)}), bf16[16,96,512]{2,1,0:T(8,128)(2,1)}, u32[]{:S(2)}, u32[]{:S(2)}) %all-to-all-start) | async-done | bytes 1572896 | tf_op jit(solution)/shard_map/all_to_all | solution.py:397
  142.9 4.1 fusion.70.x_ref
  147.0 50.4 %dense_branch.1 = (bf16[1,1024,1024]{2,1,0:T(8,128)(2,1)}, bf16[1,1024,1024]{2,1,0:T(8,128)(2,1)}, bf16[1024,2048]{1,0:T(8,128)(2,1)}, bf16[1024,2048]{1,0:T(8,1...) custom-call(bf16[1,1024,1024]{2,1,0:T(8,128)(2,1)} %fusion.70.x_ref, ...), custom_call_target="tpu_custom_call" | custom-call | flops 25769803776 | bytes 33554432 | tf_op jit(solution)/shard_map/dense_branch/pallas_call | solution.py:327
  197.4 70.3 %expert_branch.1 = (bf16[2,1536,512]{2,1,0:T(8,128)(2,1)}, bf16[2,1536,512]{2,1,0:T(8,128)(2,1)}, f32[1024,2048]{1,0:T(8,128)}, f32[2048,1024]{1,0:T(8,128)}, f32[1024,128]{1,0:T(8,128)}) custom-call(bf16[2,1536,512]{2,1,0:T(8,128)(2,1)} %all-gather.9.cloned.1.call-done.x_ref, bf16[2,1536,512]{2,1,0:T(8,128)(2,1)} %all-gather.11.cloned.1.call-done.c_ref, ...), custom_call_target="tpu_custom_call" | custom-call | flops 38654705664 | bytes 37748736 | tf_op jit(solution)/shard_map/expert_branch/pallas_call | solution.py:327
  270.4 3.7 collective-permute-done.3
  274.2 3.5 fusion.14
  277.7 7.5 %all-to-all-start.3 = ((bf16[16,96,512]{2,1,0:T(8,128)(2,1)}), bf16[16,96,512]{2,1,0:T(8,128)(2,1)}, u32[]{:S(2)}, u32[]{:S(2)}) async-start(bf16[16,96,512]{2,1,0:T(8,128)(2,1)} %bitcast.137), calls=%async_computation.3 | async-start | bytes 3145728 | tf_op jit(solution)/shard_map/all_to_all | solution.py:406
  286.0 38.0 %all-to-all-done.3 = bf16[16,96,512]{2,1,0:T(8,128)(2,1)} async-done(((bf16[16,96,512]{2,1,0:T(8,128)(2,1)}), bf16[16,96,512]{2,1,0:T(8,128)(2,1)}, u32[]{:S(2)}, u32[]{:S(2)}) %all-to-all-start.3) | async-done | bytes 1572896 | tf_op jit(solution)/shard_map/all_to_all | solution.py:406
  324.1 4.2 fusion.38
  331.6 6.6 %multiply_reduce_fusion = (f32[1024]{0:T(1024)S(1)}, f32[1024]{0:T(1024)S(1)}, f32[1024]{0:T(1024)S(1)}) fusion(f32[1024,1024]{1,0:T(8,128)} %copy-done, f32[1024]{0:T(1024)S(1)} %add_rsqrt_fusion, f32[1024]{0:T(1024)S(1)} %broadcast_multiply_fusion.2, bf16[1024,512]{1,0:T(8,128)(2,1)} %fusion.38, bf16[1024,512]{1,0:T(8,128)(2,1)} %collective-permute-done.4, ...), kind=kLoop, calls=%fused_computation.18 | loop fusion | flops 23065600 | bytes 10510337 | tf_op jit(solution)/shard_map/reduce_sum | solution.py:457
  338.2 5.5 convert_add_fusion
  345.6 18.5 %attend_back.1 = bf16[1024,1536]{1,0:T(8,128)(2,1)S(1)} custom-call(bf16[1024,1536]{1,0:T(8,128)(2,1)S(1)} %convolution_convert_fusion.1.qkv_ref, bf16[1024,512]{1,0:T(8,128)(2,1)} %get-tuple-element.25.out_ref, bf16[1024,512]{1,0:T(8,128)(2,1)S(1)} %convolution_convert_fusion.4.grad_ref, f32[4,8,1024]{2,1,0:T(8,128)S(1)} %get-tuple-element.31.lse_ref), custom_call_target="tpu_custom_call" | custom-call | flops 10737418240 | bytes 8388608 | tf_op jit(solution)/shard_map/attend_back/pallas_call | solution.py:157
  364.2 3.6 convolution_convert_fusion.2
  370.2 5.2 convolution_convert_fusion
  376.7 6.5 %concatenate.32 = bf16[1024,1664]{1,0:T(8,128)(2,1)} concatenate(bf16[1024,1536]{1,0:T(8,128)(2,1)} %convolution_convert_fusion, bf16[1024,18]{1,0:T(8,128)(2,1)S(1)} %fusion.53, bf16[1024,1]{1,0:T(8,128)(2,1)S(1)} %broadcast_in_dim.66, bf16[1024,1]{1,0:T(8,128)(2,1)S(1)} %mul.181, bf16[1024,108]{1,0:T(8,128)(2,1)S(1)} %broadcast_in_dim.33), dimensions={1} | concatenate | bytes 6815744 | tf_op jit(solution)/shard_map/concatenate | solution.py:497
  383.2 4.2 copy.122
  394.3 13.3 %all-to-all-start.2 = ((bf16[16,96,512]{2,1,0:T(8,128)(2,1)}), bf16[16,96,512]{2,1,0:T(8,128)(2,1)}, u32[]{:S(2)}, u32[]{:S(2)}) async-start(bf16[16,96,512]{2,1,0:T(8,128)(2,1)} %bitcast.19), calls=%async_computation.2 | async-start | bytes 3145728 | tf_op jit(solution)/shard_map/all_to_all | solution.py:406
  408.7 42.8 %all-to-all-done.2 = bf16[16,96,512]{2,1,0:T(8,128)(2,1)} async-done(((bf16[16,96,512]{2,1,0:T(8,128)(2,1)}), bf16[16,96,512]{2,1,0:T(8,128)(2,1)}, u32[]{:S(2)}, u32[]{:S(2)}) %all-to-all-start.2) | async-done | bytes 1572896 | tf_op jit(solution)/shard_map/all_to_all | solution.py:406
  451.5 3.4 fusion.36
  457.6 3.5 convolution_convert_fusion.3
  468.1 38.9 %reduce-scatter.5.cloned.1.call-done = bf16[64,1664]{1,0:T(8,128)(2,1)} async-done(((bf16[1024,1664]{1,0:T(8,128)(2,1)}), bf16[64,1664]{1,0:T(8,128)(2,1)}) %reduce-scatter.5.cloned.1.call-update) | async-done | bytes 213008 | tf_op jit(solution)/shard_map/reduce_scatter | solution.py:500
  508.0 4.4 fusion.32
  512.4 76.0 %reduce-scatter.7.cloned.1.call-done = bf16[32,1024]{1,0:T(8,128)(2,1)} async-done(((bf16[512,1024]{1,0:T(8,128)(2,1)}), bf16[32,1024]{1,0:T(8,128)(2,1)}) %reduce-scatter.7.cloned.1.call-update) | async-done | bytes 65552 | tf_op jit(solution)/shard_map/reduce_scatter | solution.py:461
  (159 shorter events, 59.6 us)
Async XLA Ops:
  7.2 15.7 %all-gather.13.cloned.1.call-start = ((), (), s32[]{:S(2)}) async-start(), calls=%async_computation.14 | async-start | bytes 3145728 | tf_op jit(solution)/shard_map/all_gather | solution.py:380
  7.9 40.0 %all-gather.17.cloned.1.call-start = ((), (), s32[]{:S(2)}) async-start(), calls=%async_computation.16 | async-start | bytes 3145728 | tf_op jit(solution)/shard_map/all_gather | solution.py:381
  8.7 63.1 %all-gather.15.cloned.1.call-start = ((), (), s32[]{:S(2)}) async-start(), calls=%async_computation.15 | async-start | bytes 3145728 | tf_op jit(solution)/shard_map/all_gather | solution.py:420
  32.3 14.6 %copy-start.23 = (s32[1,1024,1]{1,2,0:T(1,128)S(1)}, s32[1,1024,1]{1,2,0:T(1,128)}, u32[]{:S(2)}) copy-start(s32[1,1024,1]{1,2,0:T(1,128)} %param.15) | copy-start | bytes 12292
  47.8 46.1 %copy-start.27 = (s32[1024]{0:T(1024)}, s32[1024]{0:T(1024)S(1)}, u32[]{:S(2)}) copy-start(s32[1024]{0:T(1024)S(1)} %add_select_fusion) | copy-start | bytes 12292
  52.4 41.5 %all-to-all-start.1 = ((bf16[16,96,512]{2,1,0:T(8,128)(2,1)}), bf16[16,96,512]{2,1,0:T(8,128)(2,1)}, u32[]{:S(2)}, u32[]{:S(2)}) async-start(bf16[16,96,512]{2,1,0:T(8,128)(2,1)} %bitcast.140), calls=%async_computation.1 | async-start | bytes 3145728 | tf_op jit(solution)/shard_map/all_to_all | solution.py:397
  59.8 137.6 %all-gather.11.cloned.1.call-start = ((), (), s32[]{:S(2)}) async-start(), calls=%async_computation.9 | async-start | bytes 4718592 | tf_op jit(solution)/shard_map/all_gather | solution.py:398
  98.5 41.3 %all-to-all-start = ((bf16[16,96,512]{2,1,0:T(8,128)(2,1)}), bf16[16,96,512]{2,1,0:T(8,128)(2,1)}, u32[]{:S(2)}, u32[]{:S(2)}) async-start(bf16[16,96,512]{2,1,0:T(8,128)(2,1)} %bitcast.141), calls=%async_computation | async-start | bytes 3145728 | tf_op jit(solution)/shard_map/all_to_all | solution.py:397
  106.3 91.1 %all-gather.9.cloned.1.call-start = ((), (), s32[]{:S(2)}) async-start(), calls=%async_computation.8 | async-start | bytes 4718592 | tf_op jit(solution)/shard_map/all_gather | solution.py:398
  139.9 321.2 %reduce-scatter.9.cloned.1.call-start = ((), (), s32[]{:S(2)}) async-start(), calls=%async_computation.12 | async-start | bytes 4456448 | tf_op jit(solution)/shard_map/reduce_scatter | solution.py:437
  270.4 3.8 collective-permute-start.3
  277.7 46.4 %copy-start.28 = (s32[1024]{0:T(1024)S(1)}, s32[1024]{0:T(1024)}, u32[]{:S(2)}) copy-start(s32[1024]{0:T(1024)} %copy-done.27) | copy-start | bytes 12292
  277.7 46.4 %all-to-all-start.3 = ((bf16[16,96,512]{2,1,0:T(8,128)(2,1)}), bf16[16,96,512]{2,1,0:T(8,128)(2,1)}, u32[]{:S(2)}, u32[]{:S(2)}) async-start(bf16[16,96,512]{2,1,0:T(8,128)(2,1)} %bitcast.137), calls=%async_computation.3 | async-start | bytes 3145728 | tf_op jit(solution)/shard_map/all_to_all | solution.py:406
  285.1 177.8 %reduce-scatter.11.cloned.1.call-start = ((), (), s32[]{:S(2)}) async-start(), calls=%async_computation.13 | async-start | bytes 4456448 | tf_op jit(solution)/shard_map/reduce_scatter | solution.py:438
  285.9 221.1 %reduce-scatter.5.cloned.1.call-start = ((), (), s32[]{:S(2)}) async-start(), calls=%async_computation.10 | async-start | bytes 3620864 | tf_op jit(solution)/shard_map/reduce_scatter | solution.py:500
  285.9 45.6 %collective-permute-start.2 = (bf16[1024,1024]{1,0:T(8,128)(2,1)}, bf16[1024,1024]{1,0:T(8,128)(2,1)}, u32[]{:S(2)}, u32[]{:S(2)}) collective-permute-start(bf16[1024,1024]{1,0:T(8,128)(2,1)} %bitcast.136), channel_id=1, source_target_pairs={{0,16},{16,0},{1,17},{17,1},{2,18},{18,2},{3,19},{19,3},{4,20},{20... | collective-permute-start | bytes 6291464 | tf_op jit(solution)/shard_map/ppermute | solution.py:440
  328.3 3.3 collective-permute-start.4
  331.6 6.6 %copy-start.1 = (f32[1024,1024]{1,0:T(8,128)S(1)}, f32[1024,1024]{1,0:T(8,128)}, u32[]{:S(2)}) copy-start(f32[1024,1024]{1,0:T(8,128)} %copy-done) | copy-start | bytes 12582916
  331.6 6.6 %copy-start.13 = (bf16[1,1024,1024]{2,1,0:T(8,128)(2,1)S(1)}, bf16[1,1024,1024]{2,1,0:T(8,128)(2,1)}, u32[]{:S(2)}) copy-start(bf16[1,1024,1024]{2,1,0:T(8,128)(2,1)} %all-gather.17.cloned.1.call-done.c_ref) | copy-start | bytes 6291460
  338.2 5.5 copy-start.17
  345.6 18.5 %copy-start.11 = (bf16[1024,4,3,128]{0,3,2,1:T(8,128)(2,1)S(1)}, bf16[1024,4,3,128]{0,3,2,1:T(8,128)(2,1)}, u32[]{:S(2)}) copy-start(bf16[1024,4,3,128]{0,3,2,1:T(8,128)(2,1)} %copy.111) | copy-start | bytes 9437188
  367.8 7.6 %copy-start.9 = (bf16[1024,1024]{1,0:T(8,128)(2,1)}, bf16[1024,1024]{1,0:T(8,128)(2,1)S(1)}, u32[]{:S(2)}) copy-start(bf16[1024,1024]{1,0:T(8,128)(2,1)S(1)} %convolution_convert_fusion.2) | copy-start | bytes 6291460
  367.9 7.5 %collective-permute-start.5 = (bf16[512,1024]{1,0:T(8,128)(2,1)S(1)}, bf16[512,1024]{1,0:T(8,128)(2,1)S(1)}, u32[]{:S(2)}, u32[]{:S(2)}) collective-permute-start(bf16[512,1024]{1,0:T(8,128)(2,1)S(1)} %constant_dynamic-slice_fusion), channel_id=1, source_target_pairs={{0,16},{16,0},{1,17},{17,1},{2,18},{18,2},{3,19},{19,3},{4,20},{20... | collective-permute-start | bytes 3145736 | tf_op jit(solution)/shard_map/ppermute | solution.py:475
  370.2 5.3 copy-start.2
  387.4 5.3 copy-start.12
  389.1 18.6 %copy-start.15 = (f32[1024,128]{1,0:T(8,128)S(1)}, f32[1024,128]{1,0:T(8,128)}, u32[]{:S(2)}) copy-start(f32[1024,128]{1,0:T(8,128)} %get-tuple-element.27) | copy-start | bytes 1572868
  389.1 18.6 %copy-start.24 = (s32[1,1024,1]{1,2,0:T(1,128)S(1)}, s32[1,1024,1]{1,2,0:T(1,128)}, u32[]{:S(2)}) copy-start(s32[1,1024,1]{1,2,0:T(1,128)} %param.15) | copy-start | bytes 12292
  389.1 3.6 collective-permute-start
  394.3 57.2 %all-to-all-start.2 = ((bf16[16,96,512]{2,1,0:T(8,128)(2,1)}), bf16[16,96,512]{2,1,0:T(8,128)(2,1)}, u32[]{:S(2)}, u32[]{:S(2)}) async-start(bf16[16,96,512]{2,1,0:T(8,128)(2,1)} %bitcast.19), calls=%async_computation.2 | async-start | bytes 3145728 | tf_op jit(solution)/shard_map/all_to_all | solution.py:406
  407.7 180.7 %reduce-scatter.7.cloned.1.call-start = ((), (), s32[]{:S(2)}) async-start(), calls=%async_computation.11 | async-start | bytes 1114112 | tf_op jit(solution)/shard_map/reduce_scatter | solution.py:461
  456.8 7.9 %collective-permute-start.1 = (bf16[512,1024]{1,0:T(8,128)(2,1)}, bf16[512,1024]{1,0:T(8,128)(2,1)}, u32[]{:S(2)}, u32[]{:S(2)}) collective-permute-start(bf16[512,1024]{1,0:T(8,128)(2,1)} %constant_dynamic-slice_fusion.1), channel_id=1, source_target_pairs={{0,16},{16,0},{1,17},{17,1},{2,18},{18,2},{3,19},{19,3},{4,20},{20... | collective-permute-start | bytes 3145736 | tf_op jit(solution)/shard_map/ppermute | solution.py:475
  508.0 82.1 %collective-permute-start.6 = (bf16[32,1664]{1,0:T(8,128)(2,1)S(1)}, bf16[32,1664]{1,0:T(8,128)(2,1)S(1)}, u32[]{:S(2)}, u32[]{:S(2)}) collective-permute-start(bf16[32,1664]{1,0:T(8,128)(2,1)S(1)} %get-tuple-element.107), channel_id=1, source_target_pairs={{0,16},{16,0},{1,17},{17,1},{2,18},{18,2},{3,19},{19,3},{4,20},{20... | collective-permute-start | bytes 319496 | tf_op jit(solution)/shard_map/ppermute | solution.py:503
  (19 other events, 49.5 us)
Sparse Core Ops, SparseCore 0:
  9.5 13.2 all-gather.12
  24.4 11.7 all-gather.16
  47.0 12.2 all-gather.14
  94.1 14.2 all-gather.10
  140.0 13.7 all-gather.8
  197.5 98.8 reduce-scatter.8
  298.7 106.0 reduce-scatter.10
  407.1 99.8 reduce-scatter.4
  509.3 79.0 reduce-scatter.6

commit v2 on v1

v2 whole, which is shorter than its diff:
```python
import functools

import jax
import jax.numpy as jnp
from jax import lax
from jax.experimental import pallas as pl
from jax.experimental.pallas import tpu as pltpu
from jax.sharding import PartitionSpec as P

HEAD_DIM = 64
EPS = 1e-05
LANES = 128
LOG2E = 1.4426950408889634
GELU_A = 0.7978845608028654
GELU_B = 0.044715
SWAP = [(0, 1), (1, 0)]
F32 = jnp.float32
BF16 = jnp.bfloat16


def dot(left, right):
    return jnp.dot(left, right, preferred_element_type=F32)


def dot_t(left, right):
    return lax.dot_general(left, right, (((1,), (1,)), ((), ())), preferred_element_type=F32)


def dot_n(left, right):
    return lax.dot_general(left, right, (((0,), (0,)), ((), ())), preferred_element_type=F32)


def layer_norm(values, gain):
    average = jnp.mean(values, axis=-1, keepdims=True)
    centered = values - average
    inverse = lax.rsqrt(jnp.mean(centered * centered, axis=-1, keepdims=True) + EPS)
    normed = centered * inverse
    return (normed * gain, normed, inverse)


def norm_backward(upstream, normed, inverse, gain):
    scaled = upstream * gain
    inner_term = (
        scaled
        - jnp.mean(scaled, axis=-1, keepdims=True)
        - normed * jnp.mean(scaled * normed, axis=-1, keepdims=True)
    )
    return inner_term * inverse


def spec(shape, index):
    return pl.BlockSpec(shape, index)


def fixed(shape):
    return pl.BlockSpec(shape, lambda *_: (0,) * len(shape), pipeline_mode=pl.Buffered(1))


def struct(shape, kind):
    return jax.ShapeDtypeStruct(shape, kind)


def chunks(count, size, step):
    def run(index, carry):
        step(pl.ds(pl.multiple_of(index * size, size), size))
        return carry

    lax.fori_loop(0, count // size, run, 0)


def permutation(source, columns):
    lane = lax.broadcasted_iota(jnp.int32, (source.shape[0], columns), 1)
    return (source == lane).astype(F32).astype(BF16)


WIDE = 256


def front_kernel(node_ref, own_ref, other_ref, gain_ref, w_ref, qkv_ref, normed_ref):
    rows = own_ref.shape[0]
    node = node_ref[0]

    @pl.when(pl.program_id(0) == 0)
    def _():
        for place, part in ((node, own_ref), (1 - node, other_ref)):
            def norm(at):
                normed, _, _ = layer_norm(part[at, :].astype(F32), gain_ref[...])
                start = pl.multiple_of(place * rows + at.start, 128)
                normed_ref[pl.ds(start, 128), :] = normed.astype(BF16)

            chunks(rows, 128, norm)

    def project(at):
        qkv_ref[at, :] = dot(normed_ref[at, :], w_ref[...]).astype(BF16)

    chunks(2 * rows, 512, project)


def front(node, own, other, gain, w_qkv):
    rows, width = own.shape
    blocks = width // WIDE
    half = blocks // 2
    return pl.pallas_call(
        front_kernel,
        grid_spec=pltpu.PrefetchScalarGridSpec(
            num_scalar_prefetch=1,
            grid=(3 * half,),
            in_specs=[
                fixed(own.shape),
                fixed(own.shape),
                fixed((1, width)),
                spec((width, WIDE), lambda i, n: (0, (i % 3) * blocks + n[0] * half + i // 3)),
            ],
            out_specs=[
                spec((2 * rows, WIDE), lambda i, n: (0, i)),
                fixed((2 * rows, width)),
            ],
        ),
        out_shape=[struct((2 * rows, 3 * width // 2), BF16), struct((2 * rows, width), BF16)],
        cost_estimate=pl.CostEstimate(
            flops=6 * rows * width * width, bytes_accessed=14 * rows * width, transcendentals=0
        ),
        compiler_params=pltpu.CompilerParams(vmem_limit_bytes=32 << 20),
        name="front",
    )(node, own, other, gain[None], w_qkv)


QB = 256


def head_specs(seq):
    return [spec((seq, LANES), lambda j, at=at: (0, (j // 2) * 6 + at + j % 2)) for at in (0, 2, 4)]


def attend_kernel(q_ref, k_ref, v_ref, out_ref, lse_ref, ot_ref):
    seq = q_ref.shape[0]
    factor = HEAD_DIM ** (-0.5) * LOG2E
    lane = lax.broadcasted_iota(jnp.int32, (1, LANES), 1)
    v_t = v_ref[...].T
    below = lax.broadcasted_iota(jnp.int32, (QB, QB), 0) <= lax.broadcasted_iota(
        jnp.int32, (QB, QB), 1
    )
    for head in range(2):
        keep = (lane // HEAD_DIM) == head
        keys = jnp.where(keep, k_ref[...], 0)
        v_rows = v_t[head * HEAD_DIM : (head + 1) * HEAD_DIM]
        for block in range(seq // QB):
            lo, hi = block * QB, (block + 1) * QB
            queries = q_ref[lo:hi]
            diag = jnp.where(below, dot_t(keys[lo:hi], queries), -1e30)
            top = jnp.max(diag, axis=0, keepdims=True)
            if lo:
                past = dot_t(keys[:lo], queries)
                top = jnp.maximum(top, jnp.max(past, axis=0, keepdims=True))
            p_diag = jnp.exp2((diag - top) * factor)
            total = jnp.sum(p_diag, axis=0, keepdims=True)
            acc = dot(v_rows[:, lo:hi], p_diag.astype(BF16))
            if lo:
                p_past = jnp.exp2((past - top) * factor)
                total = total + jnp.sum(p_past, axis=0, keepdims=True)
                acc = acc + dot(v_rows[:, :lo], p_past.astype(BF16))
            ot_ref[head * HEAD_DIM : (head + 1) * HEAD_DIM, lo:hi] = acc * (1.0 / total)
            lse_ref[0, head : head + 1, lo:hi] = top * factor + jnp.log2(total)
    out_ref[...] = ot_ref[...].T.astype(BF16)


def attend(qkv, pairs):
    seq = qkv.shape[0]
    return pl.pallas_call(
        attend_kernel,
        grid=(pairs,),
        in_specs=head_specs(seq),
        out_specs=[
            spec((seq, LANES), lambda j: (0, j)),
            spec((1, 8, seq), lambda j: (j, 0, 0)),
        ],
        out_shape=[struct((seq, pairs * LANES), BF16), struct((pairs, 8, seq), F32)],
        scratch_shapes=[pltpu.VMEM((LANES, seq), F32)],
        cost_estimate=pl.CostEstimate(
            flops=pairs * 8 * seq * seq * LANES,
            bytes_accessed=pairs * seq * LANES * 8,
            transcendentals=pairs * seq * seq,
        ),
        compiler_params=pltpu.CompilerParams(vmem_limit_bytes=32 << 20),
        name="attend",
    )(qkv, qkv, qkv)


def attend_back_kernel(
    q_ref, k_ref, v_ref, out_ref, grad_ref, lse_ref, dq_ref, dk_ref, dv_ref, dqt_ref, dka_ref, dva_ref
):
    seq = q_ref.shape[0]
    scale = HEAD_DIM ** (-0.5)
    factor = scale * LOG2E
    lane = lax.broadcasted_iota(jnp.int32, (1, LANES), 1)
    k_t = k_ref[...].T
    product = (grad_ref[...].astype(F32) * out_ref[...].astype(F32)).T
    below = lax.broadcasted_iota(jnp.int32, (QB, QB), 0) <= lax.broadcasted_iota(
        jnp.int32, (QB, QB), 1
    )
    dka_ref[...] = jnp.zeros_like(dka_ref)
    dva_ref[...] = jnp.zeros_like(dva_ref)
    for head in range(2):
        keep = (lane // HEAD_DIM) == head
        rows = slice(head * HEAD_DIM, (head + 1) * HEAD_DIM)
        keys = jnp.where(keep, k_ref[...], 0)
        values = jnp.where(keep, v_ref[...], 0)
        delta = jnp.sum(product[rows], axis=0, keepdims=True)
        for block in range(seq // QB):
            lo, hi = block * QB, (block + 1) * QB
            queries = jnp.where(keep, q_ref[lo:hi], 0)
            grads = jnp.where(keep, grad_ref[lo:hi], 0)
            lse = lse_ref[0, head : head + 1, lo:hi]
            drop = delta[:, lo:hi]
            acc = None
            for start, stop in ((lo, hi), (0, lo)):
                if start == stop:
                    continue
                probs = jnp.exp2(dot_t(keys[start:stop], queries) * factor - lse)
                if start == lo:
                    probs = jnp.where(below, probs, 0.0)
                prob_grad = dot_t(values[start:stop], grads)
                score_grad = (probs * (prob_grad - drop)).astype(BF16)
                dva_ref[start:stop] += dot(probs.astype(BF16), grads)
                dka_ref[start:stop] += dot(score_grad, queries)
                part = dot(k_t[rows, start:stop], score_grad)
                acc = part if acc is None else acc + part
            dqt_ref[rows, lo:hi] = acc
    dq_ref[...] = (dqt_ref[...].T * scale).astype(BF16)
    dk_ref[...] = (dka_ref[...] * scale).astype(BF16)
    dv_ref[...] = dva_ref[...].astype(BF16)


def attend_back(qkv, attended, grad, lse):
    seq = qkv.shape[0]
    pairs = lse.shape[0]
    one = spec((seq, LANES), lambda j: (0, j))
    return pl.pallas_call(
        attend_back_kernel,
        grid=(pairs,),
        in_specs=head_specs(seq) + [one, one, spec((1, 8, seq), lambda j: (j, 0, 0))],
        out_specs=[one] * 3,
        out_shape=[struct(attended.shape, BF16)] * 3,
        scratch_shapes=[
            pltpu.VMEM((LANES, seq), F32),
            pltpu.VMEM((seq, LANES), F32),
            pltpu.VMEM((seq, LANES), F32),
        ],
        cost_estimate=pl.CostEstimate(
            flops=pairs * 20 * seq * seq * LANES,
            bytes_accessed=pairs * seq * LANES * 16,
            transcendentals=pairs * seq * seq,
        ),
        compiler_params=pltpu.CompilerParams(vmem_limit_bytes=32 << 20),
        name="attend_back",
    )(qkv, qkv, qkv, attended, grad, lse)


def middle_kernel(node_ref, tok_ref, own_ref, other_ref, w_ref, gain_ref, hidden_ref, normed_ref):
    half = own_ref.shape[1]
    node = node_ref[0]
    mine = pl.ds(pl.multiple_of(node * half, half), half)
    theirs = pl.ds(pl.multiple_of((1 - node) * half, half), half)
    hidden = tok_ref[...].astype(F32) + (
        dot(own_ref[...], w_ref[mine, :]) + dot(other_ref[...], w_ref[theirs, :])
    )
    normed, _, _ = layer_norm(hidden, gain_ref[...])
    hidden_ref[...] = hidden
    normed_ref[...] = normed.astype(BF16)


def middle(node, tokens, own, other, w_out, gain):
    seq, width = tokens.shape
    rows = 256
    row = lambda columns: spec((rows, columns), lambda i, n: (i, 0))
    return pl.pallas_call(
        middle_kernel,
        grid_spec=pltpu.PrefetchScalarGridSpec(
            num_scalar_prefetch=1,
            grid=(seq // rows,),
            in_specs=[
                row(width),
                row(width // 2),
                row(width // 2),
                fixed(w_out.shape),
                fixed((1, width)),
            ],
            out_specs=[row(width), row(width)],
        ),
        out_shape=[struct((seq, width), F32), struct((seq, width), BF16)],
        cost_estimate=pl.CostEstimate(
            flops=2 * seq * width * width, bytes_accessed=12 * seq * width, transcendentals=0
        ),
        compiler_params=pltpu.CompilerParams(vmem_limit_bytes=24 << 20),
        name="middle",
    )(node, tokens, own, other, w_out, gain[None])


def middle_back_kernel(
    parts,
    node_ref,
    source_ref,
    dense_ref,
    dense_other_ref,
    token_ref,
    token_other_ref,
    hidden_ref,
    cot_ref,
    attended_ref,
    gain_ref,
    w_ref,
    grad_ref,
    attended_grad_ref,
    ln_ref,
    *refs,
):
    weight_refs = refs[:parts]
    inner_ref, acc_ref = refs[parts:]
    half = token_ref.shape[1]
    node = node_ref[0]
    step = pl.program_id(0)

    @pl.when(step == 0)
    def _():
        ln_ref[...] = jnp.zeros_like(ln_ref)
        acc_ref[...] = jnp.zeros_like(acc_ref)

    inner_ref[...] = dense_ref[...].astype(F32) + dense_other_ref[...].astype(F32)
    inner_ref[:, pl.ds(pl.multiple_of(node * half, half), half)] += token_ref[...].astype(F32)
    inner_ref[:, pl.ds(pl.multiple_of((1 - node) * half, half), half)] += token_other_ref[
        ...
    ].astype(F32)
    inner = inner_ref[...]
    gain = gain_ref[...]
    _, base, inverse = layer_norm(hidden_ref[...], gain)
    ln_ref[0:1, :] += 0.5 * jnp.sum(inner * base, axis=0, keepdims=True)
    hidden_grad = cot_ref[...].astype(F32) + norm_backward(inner, base, inverse, gain)
    grad_ref[...] = hidden_grad
    low = hidden_grad.astype(BF16)
    attended_grad_ref[...] = dot_t(low, w_ref[...]).astype(BF16)
    turned = dot_t(permutation(source_ref[...], half), attended_ref[...]).astype(BF16)
    acc_ref[...] += dot(turned, low)

    @pl.when(step == pl.num_programs(0) - 1)
    def _():
        size = half // parts
        for part in range(parts):
            weight_refs[part][...] = acc_ref[part * size : (part + 1) * size].astype(BF16)


def middle_back(node, source, dense, dense_other, token, token_other, hidden, cot, attended, gain, w_out, parts):
    seq, width = hidden.shape
    half = width // 2
    rows = 256
    row = lambda columns: spec((rows, columns), lambda i, n: (i, 0))
    result = (half // parts, width)
    return pl.pallas_call(
        functools.partial(middle_back_kernel, parts),
        grid_spec=pltpu.PrefetchScalarGridSpec(
            num_scalar_prefetch=1,
            grid=(seq // rows,),
            in_specs=[
                fixed(source.shape),
                row(width),
                row(width),
                row(half),
                row(half),
                row(width),
                row(width),
                row(half),
                fixed((1, width)),
                spec((half, width), lambda i, n: (n[0], 0)),
            ],
            out_specs=[row(width), row(half), fixed((8, width))] + [fixed(result)] * parts,
            scratch_shapes=[pltpu.VMEM((rows, width), F32), pltpu.VMEM((half, width), F32)],
        ),
        out_shape=[
            struct((seq, width), F32),
            struct((seq, half), BF16),
            struct((8, width), F32),
        ]
        + [struct(result, BF16)] * parts,
        cost_estimate=pl.CostEstimate(
            flops=2 * seq * width * width, bytes_accessed=18 * seq * width, transcendentals=0
        ),
        compiler_params=pltpu.CompilerParams(vmem_limit_bytes=32 << 20),
        name="middle_back",
    )(node, source, dense, dense_other, token, token_other, hidden, cot, attended, gain[None], w_out)


def branch_kernel(dense, experts, parts, node_ref, *refs):
    if dense:
        x_refs, c_refs, refs = refs[:1], refs[1:2], refs[2:]
    else:
        x_refs, c_refs, refs = refs[:2], refs[2:4], refs[4:]
    side_ref, wc_ref, wct_ref, up_ref, dn_ref = refs[:5]
    refs = refs[5:]
    if dense:
        out_refs, dx_refs, gsm_ref, probs_ref = refs[:1], refs[1:2], refs[2], refs[3]
        gup_refs, gdn_refs = refs[4 : 4 + parts], refs[4 + parts : 4 + 2 * parts]
        xt_ref, g_ref, a_ref, acc_ref, dxa_ref, act_ref, dpre_ref, gt_ref = refs[4 + 2 * parts :]
    else:
        out_refs, dx_refs, gsm_ref = refs[:2], refs[2:4], refs[4]
        gup_ref, gdn_ref = refs[5:7]
        xt_ref, g_ref, a_ref, acc_ref, dxa_ref, act_ref, dpre_ref = refs[7:]
    halves = len(x_refs)
    rows, half = x_refs[0].shape
    width = halves * half
    step = pl.program_id(0)
    small = 256
    big = 512
    node = node_ref[0]
    if dense:
        split = [slice(0, width)]
    else:
        split = [
            pl.ds(pl.multiple_of(node * half, half), half),
            pl.ds(pl.multiple_of((1 - node) * half, half), half),
        ]

    @pl.when(step == 0)
    def _():
        lane = lax.broadcasted_iota(jnp.int32, (1, LANES), 1)
        is_router = lane < experts
        is_mix = (lane >= experts) & (lane < experts + 2)
        first = (lane == experts).astype(F32)
        second = (lane == experts + 1).astype(F32)
        if dense:
            turn = permutation(side_ref[...], width)
        else:
            picked = side_ref[...]

        def prepare(at):
            logits = sum(dot(x_refs[n][at, :], wc_ref[split[n], :]) for n in range(halves))

            def soft(mask):
                masked = jnp.where(mask, logits, -1e30)
                shifted = jnp.exp(masked - jnp.max(masked, axis=1, keepdims=True))
                return shifted / jnp.sum(shifted, axis=1, keepdims=True)

            mix = soft(is_mix)
            if dense:
                factor = jnp.sum(mix * first, axis=1, keepdims=True)
                probs_ref[at, :] = jnp.where(is_router, soft(is_router), mix)
                a_ref[at, :] = jnp.where(is_mix, first - mix, 0.0)
            else:
                router = soft(is_router)
                gate = jnp.sum(router * picked, axis=1, keepdims=True)
                factor = gate * jnp.sum(mix * second, axis=1, keepdims=True)
                a_ref[at, :] = jnp.where(
                    is_router, picked - router, jnp.where(is_mix, second - mix, 0.0)
                )
            for n in range(halves):
                scaled = (factor * c_refs[n][at, :].astype(F32)).astype(BF16)
                g_ref[at, split[n]] = scaled
                if dense:
                    xt_ref[:, at] = dot_t(turn, x_refs[n][at, :]).astype(BF16)
                    gt_ref[:, at] = dot_t(turn, scaled).astype(BF16)
                else:
                    xt_ref[split[n], at] = x_refs[n][at, :].T
            acc_ref[at, :] = jnp.zeros((small, width), F32)
            dxa_ref[at, :] = jnp.zeros((small, width), F32)

        chunks(rows, small, prepare)

    def forward(at):
        pre = sum(dot(x_refs[n][at, :], up_ref[split[n], :]) for n in range(halves))
        square = pre * pre
        bend = jnp.tanh(pre * (GELU_A + GELU_A * GELU_B * square))
        side = 0.5 * (1.0 + bend)
        act = (pre * side).astype(BF16)
        slope = side + 0.5 * pre * (1.0 - bend * bend) * (GELU_A + 3.0 * GELU_A * GELU_B * square)
        act_ref[at, :] = act
        if dense:
            act_grad = dot(g_ref[at, :], dn_ref[...])
            acc_ref[at, :] += dot_t(act, dn_ref[...])
        else:
            act_grad = dot_t(g_ref[at, :], dn_ref[...])
            acc_ref[at, :] += dot(act, dn_ref[...])
        pre_grad = (slope * act_grad).astype(BF16)
        dpre_ref[at, :] = pre_grad
        dxa_ref[at, :] += dot_t(pre_grad, up_ref[...])

    chunks(rows, big, forward)
    if dense:
        size = width // parts
        for part in range(parts):

            def weights(at):
                start = pl.multiple_of(part * size + at.start, small)
                rows_at = pl.ds(start, small)
                gup_refs[part][at, :] = dot(xt_ref[rows_at, :], dpre_ref[...]).astype(BF16)
                gdn_refs[part][at, :] = dot(gt_ref[rows_at, :], act_ref[...]).astype(BF16)

            chunks(size, small, weights)
    else:

        def weights(at):
            gup_ref[at, :] = dot(xt_ref[at, :], dpre_ref[...])

        chunks(width, small, weights)
        gdn_ref[...] = dot_n(act_ref[...], g_ref[...])

    @pl.when(step == pl.num_programs(0) - 1)
    def _():
        gsm_ref[...] = jnp.zeros_like(gsm_ref)

        def finish(at):
            out = acc_ref[at, :]
            strength = jnp.sum(g_ref[at, :].astype(F32) * out, axis=1, keepdims=True)
            logit_grad = strength * a_ref[at, :]
            low = logit_grad.astype(BF16)
            turned = logit_grad.T.astype(BF16)
            for n in range(halves):
                gsm_ref[:, split[n]] += dot(turned, x_refs[n][at, :])
                part = acc_ref[at, split[n]]
                if dense:
                    mixes = probs_ref[at, :]
                    lane = lax.broadcasted_iota(jnp.int32, (1, LANES), 1)
                    part = part * jnp.sum(
                        jnp.where(lane == experts, mixes, 0.0), axis=1, keepdims=True
                    )
                out_refs[n][at, :] = part.astype(BF16)
                dx_refs[n][at, :] = (dxa_ref[at, split[n]] + dot(low, wct_ref[:, split[n]])).astype(
                    BF16
                )

        chunks(rows, small, finish)


def branch(node, xs, cs, side, head, head_t, up, down, experts, parts):
    dense = len(xs) == 1
    rows, half = xs[0].shape
    width = len(xs) * half
    hidden = up.shape[1]
    block = 256
    column = lambda size: spec((size, block), lambda f, n: (0, f))
    up_spec = column(width)
    down_spec = up_spec if dense else spec((block, width), lambda f, n: (f, 0))
    outs = [(fixed((rows, half)), struct((rows, half), BF16))] * (2 * len(xs))
    outs = outs + [(fixed((LANES, width)), struct((LANES, width), F32))]
    scratch = [
        pltpu.VMEM((width, rows), BF16),
        pltpu.VMEM((rows, width), BF16),
        pltpu.VMEM((rows, LANES), F32),
        pltpu.VMEM((rows, width), F32),
        pltpu.VMEM((rows, width), F32),
        pltpu.VMEM((rows, block), BF16),
        pltpu.VMEM((rows, block), BF16),
    ]
    if dense:
        outs = outs + [(fixed((rows, LANES)), struct((rows, LANES), F32))]
        size = width // parts
        outs = outs + [(column(size), struct((size, hidden), BF16))] * (2 * parts)
        scratch = scratch + [pltpu.VMEM((width, rows), BF16)]
    else:
        outs = outs + [
            (up_spec, struct(up.shape, F32)),
            (down_spec, struct(down.shape, F32)),
        ]
    return pl.pallas_call(
        functools.partial(branch_kernel, dense, experts, parts),
        grid_spec=pltpu.PrefetchScalarGridSpec(
            num_scalar_prefetch=1,
            grid=(hidden // block,),
            in_specs=[fixed((rows, half))] * (2 * len(xs))
            + [
                fixed(side.shape),
                fixed((width, LANES)),
                fixed((LANES, width)),
                up_spec,
                down_spec,
            ],
            out_specs=[one for one, _ in outs],
            scratch_shapes=scratch,
        ),
        out_shape=[shape for _, shape in outs],
        cost_estimate=pl.CostEstimate(
            flops=12 * rows * width * hidden,
            bytes_accessed=12 * width * hidden + 8 * rows * width,
            transcendentals=rows * hidden,
        ),
        compiler_params=pltpu.CompilerParams(vmem_limit_bytes=58 << 20),
        name="dense_branch" if dense else "expert_branch",
    )(node, *xs, *cs, side, head, head_t, up, down)


def tail_kernel(
    parts,
    ln_lane,
    node_ref,
    source_ref,
    x_ref,
    gain_ref,
    small_ref,
    dq_ref,
    dk_ref,
    dv_ref,
    w_ref,
    keep_ref,
    send_ref,
    *refs,
):
    part_refs = refs[:parts]
    xt_ref, acc_ref = refs[parts:]
    seq, width = x_ref.shape
    size = width // parts
    own = keep_ref.shape[0]
    step = pl.program_id(0)
    last = pl.num_programs(0) - 1

    @pl.when(step == 0)
    def _():
        turn = permutation(source_ref[...], width)

        def prepare(at):
            xt_ref[:, at] = dot_t(turn, x_ref[at, :]).astype(BF16)
            acc_ref[at, :] = jnp.zeros((256, width), F32)

        chunks(seq, 256, prepare)

    for which, ref in enumerate((dq_ref, dk_ref, dv_ref)):

        @pl.when((step < last) & (step % 3 == which))
        def _():
            for part in range(parts):

                def weights(at):
                    rows_at = pl.ds(pl.multiple_of(part * size + at.start, 256), 256)
                    part_refs[part][at, :] = dot(xt_ref[rows_at, :], ref[...]).astype(BF16)

                chunks(size, 256, weights)

            def back(at):
                acc_ref[at, :] += dot_t(ref[at, :], w_ref[...])

            chunks(seq, 256, back)

    @pl.when(step == last)
    def _():
        gain = gain_ref[...]
        node = node_ref[0]
        total = jnp.zeros((1, width), F32)
        for piece in range(seq // 256):
            rows = slice(piece * 256, (piece + 1) * 256)
            total = total + jnp.sum(
                acc_ref[rows] * (x_ref[rows, :].astype(F32) / gain), axis=0, keepdims=True
            )
        row = lax.broadcasted_iota(jnp.int32, (LANES, 1), 0)
        small = (small_ref[...] + jnp.where(row == ln_lane, total, 0.0)).astype(BF16)
        turned = dot_t(permutation(source_ref[...], width), small).astype(BF16)
        for part in range(parts):
            part_refs[part][:, 0:LANES] = turned[part * size : (part + 1) * size]
            part_refs[part][:, LANES:WIDE] = jnp.zeros((size, WIDE - LANES), BF16)
        keep_ref[...] = acc_ref[pl.ds(pl.multiple_of(node * own, own), own), :]
        send_ref[...] = acc_ref[pl.ds(pl.multiple_of((1 - node) * own, own), own), :].astype(BF16)


def tail(node, source, normed, gain, small, dq, dk, dv, w_qkv, parts, ln_lane):
    seq, width = normed.shape
    blocks = width // WIDE
    half = blocks // 2
    steps = 3 * half
    grad_spec = spec((seq, WIDE), lambda i, n: (0, jnp.minimum(i // 3, half - 1)))

    def column(i, n):
        i = jnp.minimum(i, steps - 1)
        return (0, (i % 3) * blocks + n[0] * half + i // 3)

    part = (width // parts, WIDE)
    return pl.pallas_call(
        functools.partial(tail_kernel, parts, ln_lane),
        grid_spec=pltpu.PrefetchScalarGridSpec(
            num_scalar_prefetch=1,
            grid=(steps + 1,),
            in_specs=[
                fixed(source.shape),
                fixed(normed.shape),
                fixed((1, width)),
                fixed((LANES, width)),
                grad_spec,
                grad_spec,
                grad_spec,
                spec((width, WIDE), column),
            ],
            out_specs=[fixed((seq // 2, width)), fixed((seq // 2, width))]
            + [spec(part, lambda i, n: (0, i))] * parts,
            scratch_shapes=[pltpu.VMEM((width, seq), BF16), pltpu.VMEM((seq, width), F32)],
        ),
        out_shape=[struct((seq // 2, width), F32), struct((seq // 2, width), BF16)]
        + [struct((width // parts, (steps + 1) * WIDE), BF16)] * parts,
        cost_estimate=pl.CostEstimate(
            flops=6 * seq * width * width, bytes_accessed=16 * seq * width, transcendentals=0
        ),
        compiler_params=pltpu.CompilerParams(vmem_limit_bytes=32 << 20),
        name="tail",
    )(node, source, normed, gain[None], small, dq, dk, dv, w_qkv)


class Grid:

    def __init__(self, members):
        self.third = 4 if members % 4 == 0 else 1
        self.first = round((members // self.third) ** 0.5)
        assert self.third * self.first * self.first == members
        self.members = members
        self.sizes = (self.first, self.first, self.third)

    def digits(self, node, member):
        low, high = member % self.first, (member // self.first) % self.first
        top = member // (self.first * self.first)
        return (low, high, top) if node == 0 else (high, low, top)

    def index(self, node, digits):
        low, high = (digits[0], digits[1]) if node == 0 else (digits[1], digits[0])
        return (digits[2] * self.first + high) * self.first + low

    def shift(self, stage, by):
        pairs = []
        for node in range(2):
            for member in range(self.members):
                digits = list(self.digits(node, member))
                digits[stage] = (digits[stage] + by) % self.sizes[stage]
                target = self.index(node, digits)
                pairs.append((node * self.members + member, node * self.members + target))
        return pairs

    def order(self, node, member):
        tables = []
        for one in range(2):
            table = []
            for own in range(self.members):
                base = self.digits(one, own)
                row = []
                for place in range(self.members):
                    steps = (
                        place // (self.first * self.third),
                        (place // self.third) % self.first,
                        place % self.third,
                    )
                    row.append(
                        self.index(one, [(b + s) % k for b, s, k in zip(base, steps, self.sizes)])
                    )
                table.append(row)
            tables.append(table)
        return jnp.array(tables, jnp.int32)[node, member]

    def reduce(self, parts):
        for stage, size in enumerate(self.sizes):
            came = [
                lax.ppermute(parts[by], ("node", "expert"), self.shift(stage, by))
                for by in range(1, size)
            ]
            pieces = self.sizes[stage + 1] if stage < 2 else 1
            rows = parts[0].shape[0] // pieces
            sums = []
            for piece in range(pieces):
                at = slice(piece * rows, (piece + 1) * rows)
                total = parts[0][at].astype(F32)
                for other in came:
                    total = total + other[at].astype(F32)
                sums.append(total.astype(BF16) if stage < 2 else total)
            parts = sums
        return parts[0]


def shards(
    tokens,
    cotangent,
    routes,
    ln1_gain,
    w_qkv,
    w_out,
    ln2_gain,
    w_router,
    w_mix,
    w_up,
    w_down,
    expert_up,
    expert_down,
):
    node = lax.axis_index("node")
    member = lax.axis_index("expert")
    members = lax.axis_size("expert")
    width = tokens.shape[2]
    half = width // 2
    own_rows = tokens.shape[1]
    seq = 2 * own_rows
    experts = w_router.shape[1]
    capacity = 3 * seq // (2 * experts)
    slots = experts * capacity
    pairs = half // LANES
    own_start = node * own_rows
    scalar = node.astype(jnp.int32).reshape(1)
    grid = Grid(members)
    parts = grid.sizes[0]
    order_of = grid.order(node, member)

    def swap(value):
        return lax.ppermute(value, "node", SWAP)

    def in_order(mine, other, axis):
        return jnp.where(
            node == 0,
            jnp.concatenate([mine, other], axis=axis),
            jnp.concatenate([other, mine], axis=axis),
        )

    own_tokens, own_cot = tokens[0], cotangent[0]
    other_tokens, other_cot = swap(own_tokens), swap(own_cot)
    seq_cot = in_order(own_cot, other_cot, 0)
    seq_tokens = in_order(own_tokens, other_tokens, 0)

    group_routes = routes.reshape(-1)
    route_onehot = group_routes[:, None] == jnp.arange(experts)[None, :]
    ones = route_onehot.astype(BF16)
    row_at = jnp.arange(seq)
    earlier = (row_at[:, None] > row_at[None, :]).astype(BF16)
    order = jnp.sum(jnp.where(route_onehot, dot(earlier, ones), 0.0), axis=1).astype(jnp.int32)
    place = jnp.where(order < capacity, group_routes * capacity + order, slots)
    slot_onehot = (place[:, None] == jnp.arange(slots)[None, :]).astype(BF16)

    def dispatch(rows):
        part = lax.dynamic_slice_in_dim(rows, node * half, half, 1)
        sent = dot_n(slot_onehot, part).astype(BF16).reshape(experts, capacity, half)
        got = lax.all_to_all(sent, "expert", split_axis=0, concat_axis=0, tiled=True)
        got = got.reshape(slots, half)
        return [got, swap(got)]

    def give_back(mine, other):
        total = (mine.astype(F32) + swap(other).astype(F32)).astype(BF16)
        got = lax.all_to_all(
            total.reshape(experts, capacity, half), "expert", split_axis=0, concat_axis=0, tiled=True
        )
        return dot(slot_onehot, got.reshape(slots, half))

    expert_cot = dispatch(seq_cot)

    qkv, normed_low = front(scalar, own_tokens, other_tokens, ln1_gain, w_qkv)
    attended_own, lse = attend(qkv, pairs)
    hidden, inner_low = middle(
        scalar, seq_tokens, attended_own, swap(attended_own), w_out, ln2_gain
    )

    expert_rows = dispatch(inner_low)
    head = jnp.concatenate(
        [w_router, w_mix, jnp.zeros((width, LANES - experts - 2), BF16)], axis=1
    )
    head_t = head.T
    picked = (jnp.arange(LANES) == member).astype(F32)[None]

    def sources(block):
        return (order_of[:, None] * block + jnp.arange(block)[None, :]).reshape(-1, 1)

    results = branch(
        scalar, [inner_low], [seq_cot], sources(width // members), head, head_t, w_up, w_down,
        experts, parts,
    )
    dense_out, dense_dx, small_dense, probs = results[:4]
    grad_up, grad_down = results[4 : 4 + parts], results[4 + parts :]
    out_keep, out_send, dx_keep, dx_send, small_expert, grad_expert_up, grad_expert_down = branch(
        scalar, expert_rows, expert_cot, picked, head, head_t, expert_up[0], expert_down[0],
        experts, parts,
    )
    grad_w_up = grid.reduce(grad_up)
    grad_w_down = grid.reduce(grad_down)

    token_dx = give_back(dx_keep, dx_send).astype(BF16)
    results = middle_back(
        scalar, sources(half // members), dense_dx, swap(dense_dx), token_dx, swap(token_dx),
        hidden, seq_cot, attended_own, ln2_gain, w_out, parts,
    )
    hidden_grad, attended_grad, ln2_row = results[:3]
    grad_w_out = grid.reduce(results[3:])
    dq, dk, dv = attend_back(qkv, attended_own, attended_grad, lse)

    token_out = give_back(out_keep, out_send)
    gate = jnp.sum(jnp.where(route_onehot, probs[:, :experts], 0.0), axis=1, keepdims=True)
    scaled = gate * probs[:, experts + 1 : experts + 2] * token_out
    total_out = dense_out.astype(F32) + in_order(scaled, jnp.zeros_like(scaled), 1)
    total_out = total_out.astype(BF16)
    out_mine = lax.dynamic_slice_in_dim(total_out, own_start, own_rows, 0)
    out_other = swap(lax.dynamic_slice_in_dim(total_out, own_rows - own_start, own_rows, 0))
    hidden_own = lax.dynamic_slice_in_dim(hidden, own_start, own_rows, 0)
    mixed_out = (hidden_own + out_mine.astype(F32) + out_other.astype(F32)).astype(BF16)

    small = small_dense + small_expert
    small = small + jnp.where(jnp.arange(LANES)[:, None] == experts + 3, ln2_row[0:1], 0.0)
    block = width // (2 * members)
    source = (
        order_of[:, None, None] * block
        + jnp.arange(2)[None, :, None] * half
        + jnp.arange(block)[None, None, :]
    ).reshape(-1, 1)
    results = tail(
        scalar, source, normed_low, ln1_gain, small, dq, dk, dv, w_qkv, parts, experts + 2
    )
    normed_grad = results[0] + swap(results[1]).astype(F32)
    _, base_one, inverse_one = layer_norm(own_tokens.astype(F32), ln1_gain)
    input_grad = lax.dynamic_slice_in_dim(hidden_grad, own_start, own_rows, 0) + norm_backward(
        normed_grad, base_one, inverse_one, ln1_gain
    )
    last = grid.reduce(results[2:]).reshape(2, block, -1)
    kept = lax.dynamic_index_in_dim(last, node, 0, False)
    other = swap(lax.dynamic_index_in_dim(last, 1 - node, 0, False).astype(BF16)).astype(F32)

    def columns(rows):
        rows = rows[:, : 3 * half].reshape(block, half // WIDE, 3, WIDE)
        return rows.transpose(0, 2, 1, 3).reshape(block, 3, half)

    grad_w_qkv = in_order(columns(kept), columns(other), 2).reshape(block, 3 * width)
    small = kept[:, 3 * half :] + other[:, 3 * half :]
    return (
        mixed_out.reshape(tokens.shape),
        input_grad.reshape(tokens.shape),
        small[:, experts + 2],
        grad_w_qkv,
        grad_w_out,
        small[:, experts + 3],
        small[:, :experts],
        small[:, experts : experts + 2],
        grad_w_up,
        grad_w_down,
        grad_expert_up[None],
        grad_expert_down[None],
    )


def solution(mesh):
    return jax.shard_map(
        shards,
        mesh=mesh,
        in_specs=(
            P("expert", "node", None),
            P("expert", "node", None),
            P("expert", None, None),
            P(),
            P(),
            P(),
            P(),
            P(),
            P(),
            P(None, "node"),
            P(None, "node"),
            P("expert", None, "node"),
            P("expert", "node", None),
        ),
        out_specs=(
            P("expert", "node", None),
            P("expert", "node", None),
            P(("node", "expert")),
            P(("node", "expert"), None),
            P(("node", "expert"), None),
            P(("node", "expert")),
            P(("node", "expert"), None),
            P(("node", "expert"), None),
            P("expert", "node"),
            P("expert", "node"),
            P("expert", None, "node"),
            P("expert", "node", None),
        ),
        check_vma=False,
    )
```

time: 608 us -> 494 us (0.81)
  the two profiles are of different devices: /device:TPU:0 before, /device:TPU:11 now
where the time goes in v2:
time: 494 us; the launch traced here: 486 us
  Pallas kernels  203 us (41%)
  waiting for transfers between devices  142 us (29%)
  starting transfers between devices  57.6 us (12%)
  other arithmetic  42.2 us (9%)
  local copies, waits for them, and re-layouts  23.9 us (5%)
  matrix products  15.9 us (3%)
    pallas_call x2, Pallas kernels, branch(): pl.pallas_call(functools.partial(branch_kernel, dense, experts, parts), g...  125 us
    ppermute x20, waiting for transfers between devices, reduce(): lax.ppermute(parts[by], ('node', 'expert'), self.shift(stage, by))  101 us
    all_to_all x2, waiting for transfers between devices, dispatch(): lax.all_to_all(sent, 'expert', split_axis=0, concat_axis=0, tiled=True)  34.1 us
    pallas_call x1, Pallas kernels, tail(): pl.pallas_call(functools.partial(tail_kernel, parts, ln_lane), grid_spec=...  22.4 us
    ppermute x20, starting transfers between devices, reduce(): lax.ppermute(parts[by], ('node', 'expert'), self.shift(stage, by))  19.4 us
    pallas_call x1, Pallas kernels, attend_back(): pl.pallas_call(attend_back_kernel, grid=(pairs,), in_specs=head_specs(seq...  18.4 us
    pallas_call x1, Pallas kernels, attend(): pl.pallas_call(attend_kernel, grid=(pairs,), in_specs=head_specs(seq), ou...  14.3 us
    unnamed x95, local copies, waits for them, and re-layouts  13.9 us
  transfers between devices with their start and end apart: 36, of which 18 were waited for; matrix products, arithmetic and copies ran while one was open for 12% of the time, Pallas kernels for 27%

profile of v2, /device:TPU:11, one launch (start us, length us, event | category | flops | bytes accessed | tf_op | source)
XLA Modules:
  0.0 485.6 jit_solution(2858621614796625618)
XLA Ops:
  5.6 4.3 maximum_select_fusion
  9.9 3.3 fusion.10
  13.2 6.8 %all-to-all-start.1 = ((bf16[16,96,512]{2,1,0:T(8,128)(2,1)}), bf16[16,96,512]{2,1,0:T(8,128)(2,1)}, u32[]{:S(2)}, u32[]{:S(2)}) async-start(bf16[16,96,512]{2,1,0:T(8,128)(2,1)} %bitcast.71), calls=%async_computation.1 | async-start | bytes 3145728 | tf_op jit(solution)/shard_map/all_to_all | solution.py:826
  22.8 8.2 %front.1 = (bf16[1024,1536]{1,0:T(8,128)(2,1)S(1)}, bf16[1024,1024]{1,0:T(8,128)(2,1)S(1)}) custom-call(s32[1]{0:T(128)} %bitcast.node_ref, bf16[512,1024]{1,0:T(8,128)(2,1)S(1)} %bitcast.58, bf16[512,1024]{1,0:T(8,128)(2,1)S(1)} %collective-permute-done.other_ref, f32[1,1024]{1,0:T(1,128)S(1)} %bitcast.59, bf16[1024,3072]{1,0:T(8,128)(2,1)S(1)} %copy-done.14), custom_call_target="tpu_custom_call" | custom-call | flops 3221225472 | bytes 7340032 | tf_op jit(solution)/shard_map/front/pallas_call | solution.py:103
  32.4 14.3 %attend.1 = (bf16[1024,512]{1,0:T(8,128)(2,1)S(1)}, f32[4,8,1024]{2,1,0:T(8,128)S(1)}) custom-call(bf16[1024,1536]{1,0:T(8,128)(2,1)S(1)} %get-tuple-element.45.q_ref.k_ref.v_ref, bf16[1024,1536]{1,0:T(8,128)(2,1)S(1)} %get-tuple-element.45.q_ref.k_ref.v_ref, bf16[1024,1536]{1,0:T(8,128)(2,1)S(1)} %get-tuple-element.45.q_ref.k_ref.v_ref), custom_call_target="tpu_custom_call" | custom-call | flops 4294967296 | bytes 4194304 | tf_op jit(solution)/shard_map/attend/pallas_call | solution.py:169
  50.0 4.0 middle.1
  57.4 3.3 fusion.9
  60.7 7.1 %all-to-all-start = ((bf16[16,96,512]{2,1,0:T(8,128)(2,1)}), bf16[16,96,512]{2,1,0:T(8,128)(2,1)}, u32[]{:S(2)}, u32[]{:S(2)}) async-start(bf16[16,96,512]{2,1,0:T(8,128)(2,1)} %bitcast.72), calls=%async_computation | async-start | bytes 3145728 | tf_op jit(solution)/shard_map/all_to_all | solution.py:826
  68.9 34.1 %all-to-all-done = bf16[16,96,512]{2,1,0:T(8,128)(2,1)} async-done(((bf16[16,96,512]{2,1,0:T(8,128)(2,1)}), bf16[16,96,512]{2,1,0:T(8,128)(2,1)}, u32[]{:S(2)}, u32[]{:S(2)}) %all-to-all-start) | async-done | bytes 1572896 | tf_op jit(solution)/shard_map/all_to_all | solution.py:826
  108.8 70.7 %expert_branch.1 = (bf16[1536,512]{1,0:T(8,128)(2,1)}, bf16[1536,512]{1,0:T(8,128)(2,1)}, bf16[1536,512]{1,0:T(8,128)(2,1)}, bf16[1536,512]{1,0:T(8,128)(2,1)}, ...) custom-call(s32[1]{0:T(128)} %bitcast.node_ref, bf16[1536,512]{1,0:T(8,128)(2,1)} %bitcast.10.refs_0_, ...), custom_call_target="tpu_custom_call" | custom-call | flops 38654705664 | bytes 37748736 | tf_op jit(solution)/shard_map/expert_branch/pallas_call | solution.py:561
  183.2 3.5 add_convert_fusion.1
  186.7 5.1 %all-to-all-start.3 = ((bf16[16,96,512]{2,1,0:T(8,128)(2,1)}), bf16[16,96,512]{2,1,0:T(8,128)(2,1)}, u32[]{:S(2)}, u32[]{:S(2)}) async-start(bf16[16,96,512]{2,1,0:T(8,128)(2,1)} %bitcast.66), calls=%async_computation.3 | async-start | bytes 3145728 | tf_op jit(solution)/shard_map/all_to_all | solution.py:832
  191.8 54.7 %dense_branch.1 = (bf16[1024,1024]{1,0:T(8,128)(2,1)}, bf16[1024,1024]{1,0:T(8,128)(2,1)}, f32[128,1024]{1,0:T(8,128)}, f32[1024,128]{1,0:T(8,128)}, bf16[512,20...) custom-call(s32[1]{0:T(128)} %bitcast.node_ref, ...), custom_call_target="tpu_custom_call" | custom-call | flops 25769803776 | bytes 33554432 | tf_op jit(solution)/shard_map/dense_branch/pallas_call | solution.py:561
  253.6 3.0 add_convert_fusion.2
  256.5 6.7 %all-to-all-start.2 = ((bf16[16,96,512]{2,1,0:T(8,128)(2,1)}), bf16[16,96,512]{2,1,0:T(8,128)(2,1)}, u32[]{:S(2)}, u32[]{:S(2)}) async-start(bf16[16,96,512]{2,1,0:T(8,128)(2,1)} %bitcast.65), calls=%async_computation.2 | async-start | bytes 3145728 | tf_op jit(solution)/shard_map/all_to_all | solution.py:832
  263.2 15.0 %collective-permute-done.27 = bf16[512,2048]{1,0:T(8,128)(2,1)} collective-permute-done((bf16[512,2048]{1,0:T(8,128)(2,1)}, bf16[512,2048]{1,0:T(8,128)(2,1)}, u32[]{:S(2)}, u32[]{:S(2)}) %collective-permute-start.27) | collective-permute-done | bytes 2097184 | tf_op jit(solution)/shard_map/ppermute | solution.py:751
  278.2 4.4 add_convert_fusion.4
  286.6 33.9 %collective-permute-done.22 = bf16[512,2048]{1,0:T(8,128)(2,1)} collective-permute-done((bf16[512,2048]{1,0:T(8,128)(2,1)}, bf16[512,2048]{1,0:T(8,128)(2,1)}, u32[]{:S(2)}, u32[]{:S(2)}) %collective-permute-start.22) | collective-permute-done | bytes 2097184 | tf_op jit(solution)/shard_map/ppermute | solution.py:751
  320.5 3.2 add_convert_fusion.6
  330.8 4.2 fusion.22.token_ref
  341.5 3.4 fusion.21
  348.5 10.1 %middle_back.1 = (f32[1024,1024]{1,0:T(8,128)S(1)}, bf16[1024,512]{1,0:T(8,128)(2,1)S(1)}, f32[8,1024]{1,0:T(8,128)S(1)}, bf16[256,1024]{1,0:T(8,128)(2,1)S(1)}, bf16[256,1024]{1,0:T(8,128)(2,1)S(1)}) custom-call(s32[1]{0:T(128)} %bitcast.node_ref, s32[512,1]{1,0:T(8,128)S(1)} %add.340.source_ref, bf16[1024,1024]{1,0:T(8,128)(2,1)} %get-tuple-element.53.dense_ref, ...), custom_call_target="tpu_custom_call" | custom-call | flops 2147483648 | bytes 18874368 | tf_op jit(solution)/shard_map/middle_back/pallas_call | solution.py:357
  359.4 3.4 copy-done.19
  362.8 18.4 %attend_back.1 = (bf16[1024,512]{1,0:T(8,128)(2,1)S(1)}, bf16[1024,512]{1,0:T(8,128)(2,1)S(1)}, bf16[1024,512]{1,0:T(8,128)(2,1)S(1)}) custom-call(bf16[1024,1536]{1,0:T(8,128)(2,1)S(1)} %copy-done.19, bf16[1024,1536]{1,0:T(8,128)(2,1)S(1)} %copy-done.19, bf16[1024,1536]{1,0:T(8,128)(2,1)S(1)} %copy-done.19, bf16[1024,512]{1,0:T(8,128)(2,1)S(1)} %copy-done.10, ...), custom_call_target="tpu_custom_call" | custom-call | flops 10737418240 | bytes 8388608 | tf_op jit(solution)/shard_map/attend_back/pallas_call | solution.py:238
  383.0 22.4 %tail.1 = (f32[512,1024]{1,0:T(8,128)S(1)}, bf16[512,1024]{1,0:T(8,128)(2,1)S(1)}, bf16[512,1792]{1,0:T(8,128)(2,1)S(1)}, bf16[512,1792]{1,0:T(8,128)(2,1)S(1)}) custom-call(s32[1]{0:T(128)} %bitcast.node_ref, s32[1024,1]{1,0:T(8,128)S(1)} %copy-done.11, bf16[1024,1024]{1,0:T(8,128)(2,1)S(1)} %copy-done.21, f32[1,1024]{1,0:T(1,128)S(1)} %bitcast.60, ...), custom_call_target="tpu_custom_call" | custom-call | flops 6442450944 | bytes 16777216 | tf_op jit(solution)/shard_map/tail/pallas_call | solution.py:671
  414.0 12.0 %collective-permute-done.25 = bf16[64,2048]{1,0:T(8,128)(2,1)S(1)} collective-permute-done((bf16[64,2048]{1,0:T(8,128)(2,1)S(1)}, bf16[64,2048]{1,0:T(8,128)(2,1)S(1)}, u32[]{:S(2)}, u32[]{:S(2)}) %collective-permute-start.25) | collective-permute-done | bytes 262176 | tf_op jit(solution)/shard_map/ppermute | solution.py:751
  428.7 4.7 collective-permute-done.17
  435.5 3.7 collective-permute-done.18
  447.1 8.7 %collective-permute-done.12 = bf16[256,1792]{1,0:T(8,128)(2,1)S(1)} collective-permute-done((bf16[256,1792]{1,0:T(8,128)(2,1)S(1)}, bf16[256,1792]{1,0:T(8,128)(2,1)S(1)}, u32[]{:S(2)}, u32[]{:S(2)}) %collective-permute-start.12) | collective-permute-done | bytes 917536 | tf_op jit(solution)/shard_map/ppermute | solution.py:751
  456.3 3.0 collective-permute-start.14
  461.4 12.6 %collective-permute-done.14 = bf16[64,1792]{1,0:T(8,128)(2,1)S(1)} collective-permute-done((bf16[64,1792]{1,0:T(8,128)(2,1)S(1)}, bf16[64,1792]{1,0:T(8,128)(2,1)S(1)}, u32[]{:S(2)}, u32[]{:S(2)}) %collective-permute-start.14) | collective-permute-done | bytes 229408 | tf_op jit(solution)/shard_map/ppermute | solution.py:751
  474.0 5.0 %collective-permute-done.15 = bf16[64,1792]{1,0:T(8,128)(2,1)S(1)} collective-permute-done((bf16[64,1792]{1,0:T(8,128)(2,1)S(1)}, bf16[64,1792]{1,0:T(8,128)(2,1)S(1)}, u32[]{:S(2)}, u32[]{:S(2)}) %collective-permute-start.15) | collective-permute-done | bytes 229408 | tf_op jit(solution)/shard_map/ppermute | solution.py:751
  (212 shorter events, 86.7 us)
Async XLA Ops:
  1.4 4.1 collective-permute-start.2
  13.2 47.5 %all-to-all-start.1 = ((bf16[16,96,512]{2,1,0:T(8,128)(2,1)}), bf16[16,96,512]{2,1,0:T(8,128)(2,1)}, u32[]{:S(2)}, u32[]{:S(2)}) async-start(bf16[16,96,512]{2,1,0:T(8,128)(2,1)} %bitcast.71), calls=%async_computation.1 | async-start | bytes 3145728 | tf_op jit(solution)/shard_map/all_to_all | solution.py:826
  60.7 42.3 %all-to-all-start = ((bf16[16,96,512]{2,1,0:T(8,128)(2,1)}), bf16[16,96,512]{2,1,0:T(8,128)(2,1)}, u32[]{:S(2)}, u32[]{:S(2)}) async-start(bf16[16,96,512]{2,1,0:T(8,128)(2,1)} %bitcast.72), calls=%async_computation | async-start | bytes 3145728 | tf_op jit(solution)/shard_map/all_to_all | solution.py:826
  67.8 40.5 %collective-permute-start.4 = (bf16[1536,512]{1,0:T(8,128)(2,1)}, bf16[1536,512]{1,0:T(8,128)(2,1)}, u32[]{:S(2)}, u32[]{:S(2)}) collective-permute-start(bf16[1536,512]{1,0:T(8,128)(2,1)} %bitcast.12.refs_2_), channel_id=1, source_target_pairs={{0,16},{16,0},{1,17},{17,1},{2,18},{18,2},{3,19},{19,3},{4,20},{20... | collective-permute-start | bytes 4718600 | tf_op jit(solution)/shard_map/ppermute | solution.py:800
  103.0 5.8 %collective-permute-start.3 = (bf16[1536,512]{1,0:T(8,128)(2,1)}, bf16[1536,512]{1,0:T(8,128)(2,1)}, u32[]{:S(2)}, u32[]{:S(2)}) collective-permute-start(bf16[1536,512]{1,0:T(8,128)(2,1)} %bitcast.10.refs_0_), channel_id=1, source_target_pairs={{0,16},{16,0},{1,17},{17,1},{2,18},{18,2},{3,19},{19,3},{4,20},{20... | collective-permute-start | bytes 4718600 | tf_op jit(solution)/shard_map/ppermute | solution.py:800
  181.9 71.7 %collective-permute-start.5 = (bf16[1536,512]{1,0:T(8,128)(2,1)}, bf16[1536,512]{1,0:T(8,128)(2,1)}, u32[]{:S(2)}, u32[]{:S(2)}) collective-permute-start(bf16[1536,512]{1,0:T(8,128)(2,1)} %get-tuple-element.52), channel_id=1, source_target_pairs={{0,16},{16,0},{1,17},{17,1},{2,18},{18,2},{3,19},{19,3},{4,20},{20... | collective-permute-start | bytes 4718600 | tf_op jit(solution)/shard_map/ppermute | solution.py:800
  186.7 69.8 %all-to-all-start.3 = ((bf16[16,96,512]{2,1,0:T(8,128)(2,1)}), bf16[16,96,512]{2,1,0:T(8,128)(2,1)}, u32[]{:S(2)}, u32[]{:S(2)}) async-start(bf16[16,96,512]{2,1,0:T(8,128)(2,1)} %bitcast.66), calls=%async_computation.3 | async-start | bytes 3145728 | tf_op jit(solution)/shard_map/all_to_all | solution.py:832
  246.5 31.7 %collective-permute-start.27 = (bf16[512,2048]{1,0:T(8,128)(2,1)}, bf16[512,2048]{1,0:T(8,128)(2,1)}, u32[]{:S(2)}, u32[]{:S(2)}) collective-permute-start(bf16[512,2048]{1,0:T(8,128)(2,1)} %get-tuple-element.75), channel_id=1, source_target_pairs={{0,1},{1,0},{2,3},{3,2},{4,5},{5,4},{6,7},{7,6},{8,9},{9,8},{10,11... | collective-permute-start | bytes 6291464 | tf_op jit(solution)/shard_map/ppermute | solution.py:751
  252.1 68.4 %collective-permute-start.22 = (bf16[512,2048]{1,0:T(8,128)(2,1)}, bf16[512,2048]{1,0:T(8,128)(2,1)}, u32[]{:S(2)}, u32[]{:S(2)}) collective-permute-start(bf16[512,2048]{1,0:T(8,128)(2,1)} %get-tuple-element.73), channel_id=1, source_target_pairs={{0,1},{1,0},{2,3},{3,2},{4,5},{5,4},{6,7},{7,6},{8,9},{9,8},{10,11... | collective-permute-start | bytes 6291464 | tf_op jit(solution)/shard_map/ppermute | solution.py:751
  256.5 84.9 %all-to-all-start.2 = ((bf16[16,96,512]{2,1,0:T(8,128)(2,1)}), bf16[16,96,512]{2,1,0:T(8,128)(2,1)}, u32[]{:S(2)}, u32[]{:S(2)}) async-start(bf16[16,96,512]{2,1,0:T(8,128)(2,1)} %bitcast.65), calls=%async_computation.2 | async-start | bytes 3145728 | tf_op jit(solution)/shard_map/all_to_all | solution.py:832
  282.7 42.4 %collective-permute-start.28 = (bf16[256,2048]{1,0:T(8,128)(2,1)}, bf16[256,2048]{1,0:T(8,128)(2,1)}, u32[]{:S(2)}, u32[]{:S(2)}) collective-permute-start(bf16[256,2048]{1,0:T(8,128)(2,1)} %get-tuple-element.81), channel_id=1, source_target_pairs={{0,2},{1,3},{2,0},{3,1},{4,6},{5,7},{6,4},{7,5},{8,10},{9,11},{10,... | collective-permute-start | bytes 3145736 | tf_op jit(solution)/shard_map/ppermute | solution.py:751
  282.7 64.3 %collective-permute-start.7 = (bf16[1024,1024]{1,0:T(8,128)(2,1)}, bf16[1024,1024]{1,0:T(8,128)(2,1)}, u32[]{:S(2)}, u32[]{:S(2)}) collective-permute-start(bf16[1024,1024]{1,0:T(8,128)(2,1)} %get-tuple-element.53.dense_ref), channel_id=1, source_target_pairs={{0,16},{16,0},{1,17},{17,1},{2,18},{18,2},{3,19},{19,3},{4,20},{20... | collective-permute-start | bytes 6291464 | tf_op jit(solution)/shard_map/ppermute | solution.py:800
  323.8 14.1 %collective-permute-start.23 = (bf16[256,2048]{1,0:T(8,128)(2,1)S(1)}, bf16[256,2048]{1,0:T(8,128)(2,1)S(1)}, u32[]{:S(2)}, u32[]{:S(2)}) collective-permute-start(bf16[256,2048]{1,0:T(8,128)(2,1)S(1)} %get-tuple-element.83), channel_id=1, source_target_pairs={{0,2},{1,3},{2,0},{3,1},{4,6},{5,7},{6,4},{7,5},{8,10},{9,11},{10,... | collective-permute-start | bytes 3145736 | tf_op jit(solution)/shard_map/ppermute | solution.py:751
  327.2 79.4 %collective-permute-start.29 = (bf16[64,2048]{1,0:T(8,128)(2,1)}, bf16[64,2048]{1,0:T(8,128)(2,1)}, u32[]{:S(2)}, u32[]{:S(2)}) collective-permute-start(bf16[64,2048]{1,0:T(8,128)(2,1)} %get-tuple-element.86), channel_id=1, source_target_pairs={{0,4},{1,5},{2,6},{3,7},{4,8},{5,9},{6,10},{7,11},{8,12},{9,13},{1... | collective-permute-start | bytes 786440 | tf_op jit(solution)/shard_map/ppermute | solution.py:751
  328.4 80.4 %collective-permute-start.30 = (bf16[64,2048]{1,0:T(8,128)(2,1)}, bf16[64,2048]{1,0:T(8,128)(2,1)}, u32[]{:S(2)}, u32[]{:S(2)}) collective-permute-start(bf16[64,2048]{1,0:T(8,128)(2,1)} %get-tuple-element.88), channel_id=1, source_target_pairs={{0,8},{1,9},{2,10},{3,11},{4,12},{5,13},{6,14},{7,15},{8,0},{9,1},... | collective-permute-start | bytes 786440 | tf_op jit(solution)/shard_map/ppermute | solution.py:751
  329.5 79.8 %collective-permute-start.31 = (bf16[64,2048]{1,0:T(8,128)(2,1)}, bf16[64,2048]{1,0:T(8,128)(2,1)}, u32[]{:S(2)}, u32[]{:S(2)}) collective-permute-start(bf16[64,2048]{1,0:T(8,128)(2,1)} %get-tuple-element.87), channel_id=1, source_target_pairs={{0,12},{1,13},{2,14},{3,15},{4,0},{5,1},{6,2},{7,3},{8,4},{9,5},{1... | collective-permute-start | bytes 786440 | tf_op jit(solution)/shard_map/ppermute | solution.py:751
  337.9 10.4 %collective-permute-start.9 = (bf16[1024,512]{1,0:T(8,128)(2,1)}, bf16[1024,512]{1,0:T(8,128)(2,1)}, u32[]{:S(2)}, u32[]{:S(2)}) collective-permute-start(bf16[1024,512]{1,0:T(8,128)(2,1)} %fusion.22.token_ref), channel_id=1, source_target_pairs={{0,16},{16,0},{1,17},{17,1},{2,18},{18,2},{3,19},{19,3},{4,20},{20... | collective-permute-start | bytes 3145736 | tf_op jit(solution)/shard_map/ppermute | solution.py:800
  347.0 63.6 %collective-permute-start.24 = (bf16[64,2048]{1,0:T(8,128)(2,1)S(1)}, bf16[64,2048]{1,0:T(8,128)(2,1)S(1)}, u32[]{:S(2)}, u32[]{:S(2)}) collective-permute-start(bf16[64,2048]{1,0:T(8,128)(2,1)S(1)} %copy-done.36), channel_id=1, source_target_pairs={{0,4},{1,5},{2,6},{3,7},{4,8},{5,9},{6,10},{7,11},{8,12},{9,13},{1... | collective-permute-start | bytes 786440 | tf_op jit(solution)/shard_map/ppermute | solution.py:751
  405.4 37.5 %collective-permute-start.11 = (bf16[512,1792]{1,0:T(8,128)(2,1)S(1)}, bf16[512,1792]{1,0:T(8,128)(2,1)S(1)}, u32[]{:S(2)}, u32[]{:S(2)}) collective-permute-start(bf16[512,1792]{1,0:T(8,128)(2,1)S(1)} %get-tuple-element.69), channel_id=1, source_target_pairs={{0,1},{1,0},{2,3},{3,2},{4,5},{5,4},{6,7},{7,6},{8,9},{9,8},{10,11... | collective-permute-start | bytes 5505032 | tf_op jit(solution)/shard_map/ppermute | solution.py:751
  406.6 19.4 %collective-permute-start.25 = (bf16[64,2048]{1,0:T(8,128)(2,1)S(1)}, bf16[64,2048]{1,0:T(8,128)(2,1)S(1)}, u32[]{:S(2)}, u32[]{:S(2)}) collective-permute-start(bf16[64,2048]{1,0:T(8,128)(2,1)S(1)} %copy-done.35), channel_id=1, source_target_pairs={{0,8},{1,9},{2,10},{3,11},{4,12},{5,13},{6,14},{7,15},{8,0},{9,1},... | collective-permute-start | bytes 786440 | tf_op jit(solution)/shard_map/ppermute | solution.py:751
  408.8 17.2 %collective-permute-start.26 = (bf16[64,2048]{1,0:T(8,128)(2,1)S(1)}, bf16[64,2048]{1,0:T(8,128)(2,1)S(1)}, u32[]{:S(2)}, u32[]{:S(2)}) collective-permute-start(bf16[64,2048]{1,0:T(8,128)(2,1)S(1)} %copy-done.34), channel_id=1, source_target_pairs={{0,12},{1,13},{2,14},{3,15},{4,0},{5,1},{6,2},{7,3},{8,4},{9,5},{1... | collective-permute-start | bytes 786440 | tf_op jit(solution)/shard_map/ppermute | solution.py:751
  409.4 24.6 %collective-permute-start.6 = (bf16[512,1024]{1,0:T(8,128)(2,1)S(1)}, bf16[512,1024]{1,0:T(8,128)(2,1)S(1)}, u32[]{:S(2)}, u32[]{:S(2)}) collective-permute-start(bf16[512,1024]{1,0:T(8,128)(2,1)S(1)} %constant_dynamic-slice_fusion.1), channel_id=1, source_target_pairs={{0,16},{16,0},{1,17},{17,1},{2,18},{18,2},{3,19},{19,3},{4,20},{20... | collective-permute-start | bytes 3145736 | tf_op jit(solution)/shard_map/ppermute | solution.py:800
  410.6 22.8 %collective-permute-start.17 = (bf16[256,1024]{1,0:T(8,128)(2,1)S(1)}, bf16[256,1024]{1,0:T(8,128)(2,1)S(1)}, u32[]{:S(2)}, u32[]{:S(2)}) collective-permute-start(bf16[256,1024]{1,0:T(8,128)(2,1)S(1)} %copy-done.16), channel_id=1, source_target_pairs={{0,1},{1,0},{2,3},{3,2},{4,5},{5,4},{6,7},{7,6},{8,9},{9,8},{10,11... | collective-permute-start | bytes 1572872 | tf_op jit(solution)/shard_map/ppermute | solution.py:751
  428.0 18.4 %collective-permute-start.10 = (bf16[512,1024]{1,0:T(8,128)(2,1)S(1)}, bf16[512,1024]{1,0:T(8,128)(2,1)S(1)}, u32[]{:S(2)}, u32[]{:S(2)}) collective-permute-start(bf16[512,1024]{1,0:T(8,128)(2,1)S(1)} %get-tuple-element.67), channel_id=1, source_target_pairs={{0,16},{16,0},{1,17},{17,1},{2,18},{18,2},{3,19},{19,3},{4,20},{20... | collective-permute-start | bytes 3145736 | tf_op jit(solution)/shard_map/ppermute | solution.py:800
  433.6 5.6 %collective-permute-start.18 = (bf16[128,1024]{1,0:T(8,128)(2,1)S(1)}, bf16[128,1024]{1,0:T(8,128)(2,1)S(1)}, u32[]{:S(2)}, u32[]{:S(2)}) collective-permute-start(bf16[128,1024]{1,0:T(8,128)(2,1)S(1)} %get-tuple-element.96), channel_id=1, source_target_pairs={{0,2},{1,3},{2,0},{3,1},{4,6},{5,7},{6,4},{7,5},{8,10},{9,11},{10,... | collective-permute-start | bytes 786440 | tf_op jit(solution)/shard_map/ppermute | solution.py:751
  439.2 4.3 collective-permute-start.19
  440.4 4.1 collective-permute-start.20
  441.6 4.1 collective-permute-start.21
  443.3 12.6 %collective-permute-start.12 = (bf16[256,1792]{1,0:T(8,128)(2,1)S(1)}, bf16[256,1792]{1,0:T(8,128)(2,1)S(1)}, u32[]{:S(2)}, u32[]{:S(2)}) collective-permute-start(bf16[256,1792]{1,0:T(8,128)(2,1)S(1)} %get-tuple-element.85), channel_id=1, source_target_pairs={{0,2},{1,3},{2,0},{3,1},{4,6},{5,7},{6,4},{7,5},{8,10},{9,11},{10,... | collective-permute-start | bytes 2752520 | tf_op jit(solution)/shard_map/ppermute | solution.py:751
  456.0 5.4 %collective-permute-start.13 = (bf16[64,1792]{1,0:T(8,128)(2,1)S(1)}, bf16[64,1792]{1,0:T(8,128)(2,1)S(1)}, u32[]{:S(2)}, u32[]{:S(2)}) collective-permute-start(bf16[64,1792]{1,0:T(8,128)(2,1)S(1)} %get-tuple-element.92), channel_id=1, source_target_pairs={{0,4},{1,5},{2,6},{3,7},{4,8},{5,9},{6,10},{7,11},{8,12},{9,13},{1... | collective-permute-start | bytes 688136 | tf_op jit(solution)/shard_map/ppermute | solution.py:751
  456.3 17.7 %collective-permute-start.14 = (bf16[64,1792]{1,0:T(8,128)(2,1)S(1)}, bf16[64,1792]{1,0:T(8,128)(2,1)S(1)}, u32[]{:S(2)}, u32[]{:S(2)}) collective-permute-start(bf16[64,1792]{1,0:T(8,128)(2,1)S(1)} %get-tuple-element.94), channel_id=1, source_target_pairs={{0,8},{1,9},{2,10},{3,11},{4,12},{5,13},{6,14},{7,15},{8,0},{9,1},... | collective-permute-start | bytes 688136 | tf_op jit(solution)/shard_map/ppermute | solution.py:751
  459.3 19.8 %collective-permute-start.15 = (bf16[64,1792]{1,0:T(8,128)(2,1)S(1)}, bf16[64,1792]{1,0:T(8,128)(2,1)S(1)}, u32[]{:S(2)}, u32[]{:S(2)}) collective-permute-start(bf16[64,1792]{1,0:T(8,128)(2,1)S(1)} %get-tuple-element.93), channel_id=1, source_target_pairs={{0,12},{1,13},{2,14},{3,15},{4,0},{5,1},{6,2},{7,3},{8,4},{9,5},{1... | collective-permute-start | bytes 688136 | tf_op jit(solution)/shard_map/ppermute | solution.py:751
  (51 other events, 560.8 us)

commit v3 on v2

--- a/solution.py
+++ b/solution.py
@@ -6,6 +6,7 @@
 from jax.experimental import pallas as pl
 from jax.experimental.pallas import tpu as pltpu
 from jax.sharding import PartitionSpec as P
+
 
 HEAD_DIM = 64
 EPS = 1e-05
@@ -66,6 +67,14 @@
         return carry
 
     lax.fori_loop(0, count // size, run, 0)
+
+
+def after(value, *others):
+    return lax.optimization_barrier((value, others))[0]
+
+
+def row_pick(node, index, own, other):
+    return jnp.where(index == node, own, other)
 
 
 def permutation(source, columns):
@@ -256,12 +265,16 @@
     )(qkv, qkv, qkv, attended, grad, lse)
 
 
-def middle_kernel(node_ref, tok_ref, own_ref, other_ref, w_ref, gain_ref, hidden_ref, normed_ref):
+def middle_kernel(
+    node_ref, tok_ref, tok_other_ref, own_ref, other_ref, w_ref, gain_ref, hidden_ref, normed_ref
+):
     half = own_ref.shape[1]
     node = node_ref[0]
+    index = pl.program_id(0) // (pl.num_programs(0) // 2)
+    tok = row_pick(node, index, tok_ref[...], tok_other_ref[...])
     mine = pl.ds(pl.multiple_of(node * half, half), half)
     theirs = pl.ds(pl.multiple_of((1 - node) * half, half), half)
-    hidden = tok_ref[...].astype(F32) + (
+    hidden = tok.astype(F32) + (
         dot(own_ref[...], w_ref[mine, :]) + dot(other_ref[...], w_ref[theirs, :])
     )
     normed, _, _ = layer_norm(hidden, gain_ref[...])
@@ -269,9 +282,12 @@
     normed_ref[...] = normed.astype(BF16)
 
 
-def middle(node, tokens, own, other, w_out, gain):
-    seq, width = tokens.shape
+def middle(node, tokens, tokens_other, own, other, w_out, gain):
+    width = tokens.shape[1]
+    seq = 2 * tokens.shape[0]
     rows = 256
+    steps = seq // rows
+    half_row = spec((rows, width), lambda i, n: (i % (steps // 2), 0))
     row = lambda columns: spec((rows, columns), lambda i, n: (i, 0))
     return pl.pallas_call(
         middle_kernel,
@@ -279,7 +295,8 @@
             num_scalar_prefetch=1,
             grid=(seq // rows,),
             in_specs=[
-                row(width),
+                half_row,
+                half_row,
                 row(width // 2),
                 row(width // 2),
                 fixed(w_out.shape),
@@ -293,7 +310,7 @@
         ),
         compiler_params=pltpu.CompilerParams(vmem_limit_bytes=24 << 20),
         name="middle",
-    )(node, tokens, own, other, w_out, gain[None])
+    )(node, tokens, tokens_other, own, other, w_out, gain[None])
 
 
 def middle_back_kernel(
@@ -306,6 +323,7 @@
     token_other_ref,
     hidden_ref,
     cot_ref,
+    cot_other_ref,
     attended_ref,
     gain_ref,
     w_ref,
@@ -334,7 +352,9 @@
     gain = gain_ref[...]
     _, base, inverse = layer_norm(hidden_ref[...], gain)
     ln_ref[0:1, :] += 0.5 * jnp.sum(inner * base, axis=0, keepdims=True)
-    hidden_grad = cot_ref[...].astype(F32) + norm_backward(inner, base, inverse, gain)
+    index = step // (pl.num_programs(0) // 2)
+    cot = row_pick(node, index, cot_ref[...], cot_other_ref[...])
+    hidden_grad = cot.astype(F32) + norm_backward(inner, base, inverse, gain)
     grad_ref[...] = hidden_grad
     low = hidden_grad.astype(BF16)
     attended_grad_ref[...] = dot_t(low, w_ref[...]).astype(BF16)
@@ -348,10 +368,14 @@
             weight_refs[part][...] = acc_ref[part * size : (part + 1) * size].astype(BF16)
 
 
-def middle_back(node, source, dense, dense_other, token, token_other, hidden, cot, attended, gain, w_out, parts):
+def middle_back(
+    node, source, dense, dense_other, token, token_other, hidden, cot, cot_other, attended, gain, w_out, parts
+):
     seq, width = hidden.shape
     half = width // 2
     rows = 256
+    steps = seq // rows
+    half_row = spec((rows, width), lambda i, n: (i % (steps // 2), 0))
     row = lambda columns: spec((rows, columns), lambda i, n: (i, 0))
     result = (half // parts, width)
     return pl.pallas_call(
@@ -366,7 +390,8 @@
                 row(half),
                 row(half),
                 row(width),
-                row(width),
+                half_row,
+                half_row,
                 row(half),
                 fixed((1, width)),
                 spec((half, width), lambda i, n: (n[0], 0)),
@@ -385,12 +410,80 @@
         ),
         compiler_params=pltpu.CompilerParams(vmem_limit_bytes=32 << 20),
         name="middle_back",
-    )(node, source, dense, dense_other, token, token_other, hidden, cot, attended, gain[None], w_out)
+    )(
+        node, source, dense, dense_other, token, token_other, hidden, cot, cot_other, attended,
+        gain[None], w_out,
+    )
+
+
+def dispatch_kernel(node_ref, place_ref, own_ref, other_ref, sent_ref):
+    size = sent_ref.shape[0]
+    node = node_ref[0]
+    slot = pl.program_id(0) * size + lax.broadcasted_iota(jnp.int32, (size, 1), 0)
+    total = None
+    for at, ref in ((node, own_ref), (1 - node, other_ref)):
+        place = place_ref[pl.ds(at, 1), :]
+        part = dot((place == slot).astype(F32).astype(BF16), ref[...])
+        total = part if total is None else total + part
+    sent_ref[...] = total.astype(BF16)
+
+
+def dispatch_rows(node, place, own, other, slots):
+    rows = place.shape[1]
+    half = own.shape[1] // 2
+    size = 256
+    if own.shape[0] == rows:
+        first = spec((rows, half), lambda i, n: (0, n[0]))
+        second = first
+    else:
+        first = spec((rows, half), lambda i, n: (n[0], n[0]))
+        second = spec((rows, half), lambda i, n: (1 - n[0], n[0]))
+    return pl.pallas_call(
+        dispatch_kernel,
+        grid_spec=pltpu.PrefetchScalarGridSpec(
+            num_scalar_prefetch=1,
+            grid=(slots // size,),
+            in_specs=[fixed(place.shape), first, second],
+            out_specs=spec((size, half), lambda i, n: (i, 0)),
+        ),
+        out_shape=struct((slots, half), BF16),
+        cost_estimate=pl.CostEstimate(
+            flops=4 * slots * rows * half, bytes_accessed=4 * slots * half, transcendentals=0
+        ),
+        compiler_params=pltpu.CompilerParams(vmem_limit_bytes=16 << 20),
+        name="dispatch",
+    )(node, place, own, other)
+
+
+def combine_kernel(place_ref, got_ref, out_ref):
+    size = place_ref.shape[0]
+    slot = lax.broadcasted_iota(jnp.int32, (size, got_ref.shape[0]), 1)
+    onehot = (place_ref[...] == slot).astype(F32).astype(BF16)
+    out_ref[...] = dot(onehot, got_ref[...]).astype(BF16)
+
+
+def combine_rows(place, got):
+    rows = place.shape[0]
+    size = 256
+    return pl.pallas_call(
+        combine_kernel,
+        grid=(rows // size,),
+        in_specs=[spec((size, 1), lambda i: (i, 0)), fixed(got.shape)],
+        out_specs=spec((size, got.shape[1]), lambda i: (i, 0)),
+        out_shape=struct((rows, got.shape[1]), BF16),
+        cost_estimate=pl.CostEstimate(
+            flops=2 * rows * got.shape[0] * got.shape[1],
+            bytes_accessed=4 * rows * got.shape[1],
+            transcendentals=0,
+        ),
+        compiler_params=pltpu.CompilerParams(vmem_limit_bytes=16 << 20),
+        name="combine",
+    )(place, got)
 
 
 def branch_kernel(dense, experts, parts, node_ref, *refs):
     if dense:
-        x_refs, c_refs, refs = refs[:1], refs[1:2], refs[2:]
+        x_refs, c_refs, refs = refs[:1], refs[1:3], refs[3:]
     else:
         x_refs, c_refs, refs = refs[:2], refs[2:4], refs[4:]
     side_ref, wc_ref, wct_ref, up_ref, dn_ref = refs[:5]
@@ -401,8 +494,7 @@
         xt_ref, g_ref, a_ref, acc_ref, dxa_ref, act_ref, dpre_ref, gt_ref = refs[4 + 2 * parts :]
     else:
         out_refs, dx_refs, gsm_ref = refs[:2], refs[2:4], refs[4]
-        gup_ref, gdn_ref = refs[5:7]
-        xt_ref, g_ref, a_ref, acc_ref, dxa_ref, act_ref, dpre_ref = refs[7:]
+        g_ref, act_ref, dpre_ref, a_ref, acc_ref, dxa_ref = refs[5:]
     halves = len(x_refs)
     rows, half = x_refs[0].shape
     width = halves * half
@@ -450,14 +542,18 @@
                 a_ref[at, :] = jnp.where(
                     is_router, picked - router, jnp.where(is_mix, second - mix, 0.0)
                 )
-            for n in range(halves):
-                scaled = (factor * c_refs[n][at, :].astype(F32)).astype(BF16)
-                g_ref[at, split[n]] = scaled
-                if dense:
-                    xt_ref[:, at] = dot_t(turn, x_refs[n][at, :]).astype(BF16)
-                    gt_ref[:, at] = dot_t(turn, scaled).astype(BF16)
-                else:
-                    xt_ref[split[n], at] = x_refs[n][at, :].T
+            if dense:
+                own = c_refs[0].shape[0]
+                place = at.start // own
+                inside = pl.ds(pl.multiple_of(at.start - place * own, small), small)
+                cot = row_pick(node, place, c_refs[0][inside, :], c_refs[1][inside, :])
+                scaled = (factor * cot.astype(F32)).astype(BF16)
+                g_ref[at, :] = scaled
+                xt_ref[:, at] = dot_t(turn, x_refs[0][at, :]).astype(BF16)
+                gt_ref[:, at] = dot_t(turn, scaled).astype(BF16)
+            else:
+                for n in range(halves):
+                    g_ref[at, split[n]] = (factor * c_refs[n][at, :].astype(F32)).astype(BF16)
             acc_ref[at, :] = jnp.zeros((small, width), F32)
             dxa_ref[at, :] = jnp.zeros((small, width), F32)
 
@@ -493,13 +589,6 @@
                 gdn_refs[part][at, :] = dot(gt_ref[rows_at, :], act_ref[...]).astype(BF16)
 
             chunks(size, small, weights)
-    else:
-
-        def weights(at):
-            gup_ref[at, :] = dot(xt_ref[at, :], dpre_ref[...])
-
-        chunks(width, small, weights)
-        gdn_ref[...] = dot_n(act_ref[...], g_ref[...])
 
     @pl.when(step == pl.num_programs(0) - 1)
     def _():
@@ -533,37 +622,39 @@
     rows, half = xs[0].shape
     width = len(xs) * half
     hidden = up.shape[1]
-    block = 256
+    block = 512
     column = lambda size: spec((size, block), lambda f, n: (0, f))
     up_spec = column(width)
     down_spec = up_spec if dense else spec((block, width), lambda f, n: (f, 0))
     outs = [(fixed((rows, half)), struct((rows, half), BF16))] * (2 * len(xs))
     outs = outs + [(fixed((LANES, width)), struct((LANES, width), F32))]
-    scratch = [
-        pltpu.VMEM((width, rows), BF16),
-        pltpu.VMEM((rows, width), BF16),
+    sums = [
         pltpu.VMEM((rows, LANES), F32),
         pltpu.VMEM((rows, width), F32),
         pltpu.VMEM((rows, width), F32),
-        pltpu.VMEM((rows, block), BF16),
-        pltpu.VMEM((rows, block), BF16),
     ]
     if dense:
         outs = outs + [(fixed((rows, LANES)), struct((rows, LANES), F32))]
         size = width // parts
         outs = outs + [(column(size), struct((size, hidden), BF16))] * (2 * parts)
-        scratch = scratch + [pltpu.VMEM((width, rows), BF16)]
+        scratch = [
+            pltpu.VMEM((width, rows), BF16),
+            pltpu.VMEM((rows, width), BF16),
+            *sums,
+            pltpu.VMEM((rows, block), BF16),
+            pltpu.VMEM((rows, block), BF16),
+            pltpu.VMEM((width, rows), BF16),
+        ]
     else:
-        outs = outs + [
-            (up_spec, struct(up.shape, F32)),
-            (down_spec, struct(down.shape, F32)),
-        ]
+        outs = outs + [(fixed((rows, width)), struct((rows, width), BF16))]
+        outs = outs + [(column(rows), struct((rows, hidden), BF16))] * 2
+        scratch = sums
     return pl.pallas_call(
         functools.partial(branch_kernel, dense, experts, parts),
         grid_spec=pltpu.PrefetchScalarGridSpec(
             num_scalar_prefetch=1,
             grid=(hidden // block,),
-            in_specs=[fixed((rows, half))] * (2 * len(xs))
+            in_specs=[fixed(one.shape) for one in [*xs, *cs]]
             + [
                 fixed(side.shape),
                 fixed((width, LANES)),
@@ -576,13 +667,63 @@
         ),
         out_shape=[shape for _, shape in outs],
         cost_estimate=pl.CostEstimate(
-            flops=12 * rows * width * hidden,
+            flops=(12 if dense else 8) * rows * width * hidden,
             bytes_accessed=12 * width * hidden + 8 * rows * width,
             transcendentals=rows * hidden,
         ),
         compiler_params=pltpu.CompilerParams(vmem_limit_bytes=58 << 20),
         name="dense_branch" if dense else "expert_branch",
     )(node, *xs, *cs, side, head, head_t, up, down)
+
+
+def expert_weights_kernel(node_ref, own_ref, other_ref, g_ref, act_ref, dpre_ref, gup_ref, gdn_ref, xt_ref):
+    rows, half = own_ref.shape
+    node = node_ref[0]
+
+    @pl.when(pl.program_id(0) == 0)
+    def _():
+        for at, ref in ((node, own_ref), (1 - node, other_ref)):
+            place = pl.ds(pl.multiple_of(at * half, half), half)
+
+            def turn(rows_at):
+                xt_ref[place, rows_at] = ref[rows_at, :].T
+
+            chunks(rows, 256, turn)
+
+    def weights(at):
+        gup_ref[at, :] = dot(xt_ref[at, :], dpre_ref[...])
+
+    chunks(2 * half, 256, weights)
+    gdn_ref[...] = dot_n(act_ref[...], g_ref[...])
+
+
+def expert_weights(node, own, other, g, act, dpre):
+    rows, half = own.shape
+    width = 2 * half
+    hidden = act.shape[1]
+    block = 512
+    column = spec((rows, block), lambda f, n: (0, f))
+    return pl.pallas_call(
+        expert_weights_kernel,
+        grid_spec=pltpu.PrefetchScalarGridSpec(
+            num_scalar_prefetch=1,
+            grid=(hidden // block,),
+            in_specs=[fixed(own.shape), fixed(own.shape), fixed(g.shape), column, column],
+            out_specs=[
+                spec((width, block), lambda f, n: (0, f)),
+                spec((block, width), lambda f, n: (f, 0)),
+            ],
+            scratch_shapes=[pltpu.VMEM((width, rows), BF16)],
+        ),
+        out_shape=[struct((width, hidden), F32), struct((hidden, width), F32)],
+        cost_estimate=pl.CostEstimate(
+            flops=4 * rows * width * hidden,
+            bytes_accessed=8 * width * hidden + 4 * rows * hidden,
+            transcendentals=0,
+        ),
+        compiler_params=pltpu.CompilerParams(vmem_limit_bytes=48 << 20),
+        name="expert_weights",
+    )(node, own, other, g, act, dpre)
 
 
 def tail_kernel(
@@ -745,12 +886,14 @@
             tables.append(table)
         return jnp.array(tables, jnp.int32)[node, member]
 
-    def reduce(self, parts):
+    def reduce(self, parts, gates=(None, None, None)):
         for stage, size in enumerate(self.sizes):
             came = [
                 lax.ppermute(parts[by], ("node", "expert"), self.shift(stage, by))
                 for by in range(1, size)
             ]
+            if gates[stage] is not None:
+                came = [after(other, gates[stage]) for other in came]
             pieces = self.sizes[stage + 1] if stage < 2 else 1
             rows = parts[0].shape[0] // pieces
             sums = []
@@ -808,8 +951,6 @@
 
     own_tokens, own_cot = tokens[0], cotangent[0]
     other_tokens, other_cot = swap(own_tokens), swap(own_cot)
-    seq_cot = in_order(own_cot, other_cot, 0)
-    seq_tokens = in_order(own_tokens, other_tokens, 0)
 
     group_routes = routes.reshape(-1)
     route_onehot = group_routes[:, None] == jnp.arange(experts)[None, :]
@@ -818,31 +959,27 @@
     earlier = (row_at[:, None] > row_at[None, :]).astype(BF16)
     order = jnp.sum(jnp.where(route_onehot, dot(earlier, ones), 0.0), axis=1).astype(jnp.int32)
     place = jnp.where(order < capacity, group_routes * capacity + order, slots)
-    slot_onehot = (place[:, None] == jnp.arange(slots)[None, :]).astype(BF16)
-
-    def dispatch(rows):
-        part = lax.dynamic_slice_in_dim(rows, node * half, half, 1)
-        sent = dot_n(slot_onehot, part).astype(BF16).reshape(experts, capacity, half)
-        got = lax.all_to_all(sent, "expert", split_axis=0, concat_axis=0, tiled=True)
-        got = got.reshape(slots, half)
-        return [got, swap(got)]
+    place_rows = place.reshape(2, own_rows)
+    place_column = place.reshape(seq, 1)
+
+    def exchange(value):
+        value = value.reshape(experts, capacity, half)
+        got = lax.all_to_all(value, "expert", split_axis=0, concat_axis=0, tiled=True)
+        return got.reshape(slots, half)
 
     def give_back(mine, other):
         total = (mine.astype(F32) + swap(other).astype(F32)).astype(BF16)
-        got = lax.all_to_all(
-            total.reshape(experts, capacity, half), "expert", split_axis=0, concat_axis=0, tiled=True
-        )
-        return dot(slot_onehot, got.reshape(slots, half))
-
-    expert_cot = dispatch(seq_cot)
+        return total, exchange(total)
+
+    got_cot = exchange(dispatch_rows(scalar, place_rows, own_cot, other_cot, slots))
 
     qkv, normed_low = front(scalar, own_tokens, other_tokens, ln1_gain, w_qkv)
     attended_own, lse = attend(qkv, pairs)
     hidden, inner_low = middle(
-        scalar, seq_tokens, attended_own, swap(attended_own), w_out, ln2_gain
-    )
-
-    expert_rows = dispatch(inner_low)
+        scalar, own_tokens, other_tokens, attended_own, swap(attended_own), w_out, ln2_gain
+    )
+
+    got_rows = exchange(dispatch_rows(scalar, place_rows, inner_low, inner_low, slots))
     head = jnp.concatenate(
         [w_router, w_mix, jnp.zeros((width, LANES - experts - 2), BF16)], axis=1
     )
@@ -853,36 +990,28 @@
         return (order_of[:, None] * block + jnp.arange(block)[None, :]).reshape(-1, 1)
 
     results = branch(
-        scalar, [inner_low], [seq_cot], sources(width // members), head, head_t, w_up, w_down,
-        experts, parts,
+        scalar, [inner_low], [own_cot, other_cot], sources(width // members), head, head_t, w_up,
+        w_down, experts, parts,
     )
     dense_out, dense_dx, small_dense, probs = results[:4]
     grad_up, grad_down = results[4 : 4 + parts], results[4 + parts :]
-    out_keep, out_send, dx_keep, dx_send, small_expert, grad_expert_up, grad_expert_down = branch(
-        scalar, expert_rows, expert_cot, picked, head, head_t, expert_up[0], expert_down[0],
-        experts, parts,
-    )
-    grad_w_up = grid.reduce(grad_up)
-    grad_w_down = grid.reduce(grad_down)
-
-    token_dx = give_back(dx_keep, dx_send).astype(BF16)
+    got_rows = after(got_rows, small_dense)
+    expert_rows = [got_rows, swap(got_rows)]
+    out_keep, out_send, dx_keep, dx_send, small_expert, expert_g, expert_act, expert_dpre = branch(
+        scalar, expert_rows, [got_cot, swap(got_cot)], picked, head, head_t, expert_up[0],
+        expert_down[0], experts, parts,
+    )
+
+    sent_dx, got_dx = give_back(dx_keep, dx_send)
+    _, got_out = give_back(out_keep, after(out_send, sent_dx))
+    token_dx = combine_rows(place_column, got_dx)
     results = middle_back(
         scalar, sources(half // members), dense_dx, swap(dense_dx), token_dx, swap(token_dx),
-        hidden, seq_cot, attended_own, ln2_gain, w_out, parts,
+        hidden, own_cot, other_cot, attended_own, ln2_gain, w_out, parts,
     )
     hidden_grad, attended_grad, ln2_row = results[:3]
-    grad_w_out = grid.reduce(results[3:])
+    grad_w_out = results[3:]
     dq, dk, dv = attend_back(qkv, attended_own, attended_grad, lse)
-
-    token_out = give_back(out_keep, out_send)
-    gate = jnp.sum(jnp.where(route_onehot, probs[:, :experts], 0.0), axis=1, keepdims=True)
-    scaled = gate * probs[:, experts + 1 : experts + 2] * token_out
-    total_out = dense_out.astype(F32) + in_order(scaled, jnp.zeros_like(scaled), 1)
-    total_out = total_out.astype(BF16)
-    out_mine = lax.dynamic_slice_in_dim(total_out, own_start, own_rows, 0)
-    out_other = swap(lax.dynamic_slice_in_dim(total_out, own_rows - own_start, own_rows, 0))
-    hidden_own = lax.dynamic_slice_in_dim(hidden, own_start, own_rows, 0)
-    mixed_out = (hidden_own + out_mine.astype(F32) + out_other.astype(F32)).astype(BF16)
 
     small = small_dense + small_expert
     small = small + jnp.where(jnp.arange(LANES)[:, None] == experts + 3, ln2_row[0:1], 0.0)
@@ -900,6 +1029,25 @@
     input_grad = lax.dynamic_slice_in_dim(hidden_grad, own_start, own_rows, 0) + norm_backward(
         normed_grad, base_one, inverse_one, ln1_gain
     )
+    gate = results[0]
+    grad_expert_up, grad_expert_down = expert_weights(
+        scalar, *expert_rows, after(expert_g, gate), expert_act, expert_dpre
+    )
+    late = grad_expert_up
+    grad_w_up = grid.reduce(grad_up, (sent_dx, ln2_row, late))
+    grad_w_down = grid.reduce(grad_down, (sent_dx, ln2_row, late))
+    grad_w_out = grid.reduce(grad_w_out, (gate, late, None))
+
+    token_out = combine_rows(place_column, after(got_out, late)).astype(F32)
+    chance = jnp.sum(jnp.where(route_onehot, probs[:, :experts], 0.0), axis=1, keepdims=True)
+    scaled = chance * probs[:, experts + 1 : experts + 2] * token_out
+    total_out = dense_out.astype(F32) + in_order(scaled, jnp.zeros_like(scaled), 1)
+    total_out = total_out.astype(BF16)
+    out_mine = lax.dynamic_slice_in_dim(total_out, own_start, own_rows, 0)
+    out_other = swap(lax.dynamic_slice_in_dim(total_out, own_rows - own_start, own_rows, 0))
+    hidden_own = lax.dynamic_slice_in_dim(hidden, own_start, own_rows, 0)
+    mixed_out = (hidden_own + out_mine.astype(F32) + out_other.astype(F32)).astype(BF16)
+
     last = grid.reduce(results[2:]).reshape(2, block, -1)
     kept = lax.dynamic_index_in_dim(last, node, 0, False)
     other = swap(lax.dynamic_index_in_dim(last, 1 - node, 0, False).astype(BF16)).astype(F32)

time: 494 us -> 477 us (0.966)
  the two profiles are of different devices: /device:TPU:11 before, /device:TPU:0 now
where the time goes in v3:
time: 477 us; the launch traced here: 471 us
  Pallas kernels  212 us (44%)
  waiting for transfers between devices  94 us (20%)
  starting transfers between devices  80.6 us (17%)
  other arithmetic  45.1 us (9%)
  local copies, waits for them, and re-layouts  35.8 us (8%)
    pallas_call x2, Pallas kernels, branch(): pl.pallas_call(functools.partial(branch_kernel, dense, experts, parts), g...  92.4 us
    ppermute x20, waiting for transfers between devices, reduce(): lax.ppermute(parts[by], ('node', 'expert'), self.shift(stage, by))  81 us
    all_to_all x4, starting transfers between devices, exchange(): lax.all_to_all(value, 'expert', split_axis=0, concat_axis=0, tiled=True)  40.4 us
    ppermute x20, starting transfers between devices, reduce(): lax.ppermute(parts[by], ('node', 'expert'), self.shift(stage, by))  38.2 us
    pallas_call x1, Pallas kernels, tail(): pl.pallas_call(functools.partial(tail_kernel, parts, ln_lane), grid_spec=...  23.3 us
    unnamed x91, local copies, waits for them, and re-layouts  23.1 us
    pallas_call x1, Pallas kernels, expert_weights(): pl.pallas_call(expert_weights_kernel, grid_spec=pltpu.PrefetchScalarGridS...  22.5 us
    pallas_call x1, Pallas kernels, attend_back(): pl.pallas_call(attend_back_kernel, grid=(pairs,), in_specs=head_specs(seq...  19.2 us
  transfers between devices with their start and end apart: 36, of which 16 were waited for; matrix products, arithmetic and copies ran while one was open for 11% of the time, Pallas kernels for 35%

profile of v3, /device:TPU:0, one launch (start us, length us, event | category | flops | bytes accessed | tf_op | source)
XLA Modules:
  0.0 470.5 jit_solution(5273958364054691207)
XLA Ops:
  3.7 3.9 dispatch.3
  7.7 8.4 %all-to-all-start.1 = ((bf16[16,96,512]{2,1,0:T(8,128)(2,1)}), bf16[16,96,512]{2,1,0:T(8,128)(2,1)}, u32[]{:S(2)}, u32[]{:S(2)}) async-start(bf16[16,96,512]{2,1,0:T(8,128)(2,1)} %bitcast.13), calls=%async_computation.1 | async-start | bytes 3145728 | tf_op jit(solution)/shard_map/all_to_all | solution.py:967
  16.1 3.1 copy-done.22
  19.3 8.2 %front.1 = (bf16[1024,1536]{1,0:T(8,128)(2,1)S(1)}, bf16[1024,1024]{1,0:T(8,128)(2,1)S(1)}) custom-call(s32[1]{0:T(128)} %bitcast.node_ref, bf16[512,1024]{1,0:T(8,128)(2,1)S(1)} %bitcast.58, bf16[512,1024]{1,0:T(8,128)(2,1)S(1)} %collective-permute-done.other_ref.tok_other_ref, f32[1,1024]{1,0:T(1,128)S(1)} %bitcast.65, bf16[1024,3072]{1,0:T(8,128)(2,1)S(1)} %copy-done.22), custom_call_target="tpu_custom_call" | custom-call | flops 3221225472 | bytes 7340032 | tf_op jit(solution)/shard_map/front/pallas_call | solution.py:112
  27.5 15.0 %attend.1 = (bf16[1024,512]{1,0:T(8,128)(2,1)}, f32[4,8,1024]{2,1,0:T(8,128)S(1)}) custom-call(bf16[1024,1536]{1,0:T(8,128)(2,1)S(1)} %get-tuple-element.64.q_ref.k_ref.v_ref, bf16[1024,1536]{1,0:T(8,128)(2,1)S(1)} %get-tuple-element.64.q_ref.k_ref.v_ref, bf16[1024,1536]{1,0:T(8,128)(2,1)S(1)} %get-tuple-element.64.q_ref.k_ref.v_ref), custom_call_target="tpu_custom_call" | custom-call | flops 4294967296 | bytes 4194304 | tf_op jit(solution)/shard_map/attend/pallas_call | solution.py:178
  42.5 3.0 collective-permute-done.1.other_ref
  46.8 5.1 %middle.1 = (f32[1024,1024]{1,0:T(8,128)S(1)}, bf16[1024,1024]{1,0:T(8,128)(2,1)S(1)}) custom-call(s32[1]{0:T(128)} %bitcast.node_ref, bf16[512,1024]{1,0:T(8,128)(2,1)S(1)} %bitcast.59, bf16[512,1024]{1,0:T(8,128)(2,1)S(1)} %copy-done.26, bf16[1024,512]{1,0:T(8,128)(2,1)} %get-tuple-element.65.own_ref.attended_ref.out_ref, ...), custom_call_target="tpu_custom_call" | custom-call | flops 2147483648 | bytes 12582912 | tf_op jit(solution)/shard_map/middle/pallas_call | solution.py:292
  59.0 7.3 %all-to-all-start = ((bf16[16,96,512]{2,1,0:T(8,128)(2,1)}), bf16[16,96,512]{2,1,0:T(8,128)(2,1)}, u32[]{:S(2)}, u32[]{:S(2)}) async-start(bf16[16,96,512]{2,1,0:T(8,128)(2,1)} %bitcast.60), calls=%async_computation | async-start | bytes 3145728 | tf_op jit(solution)/shard_map/all_to_all | solution.py:967
  71.4 47.5 %dense_branch.1 = (bf16[1024,1024]{1,0:T(8,128)(2,1)}, bf16[1024,1024]{1,0:T(8,128)(2,1)}, f32[128,1024]{1,0:T(8,128)}, f32[1024,128]{1,0:T(8,128)}, bf16[512,20...) custom-call(s32[1]{0:T(128)} %bitcast.node_ref, ...), custom_call_target="tpu_custom_call" | custom-call | flops 25769803776 | bytes 33554432 | tf_op jit(solution)/shard_map/dense_branch/pallas_call | solution.py:652
  126.0 44.9 %expert_branch.1 = (bf16[1536,512]{1,0:T(8,128)(2,1)}, bf16[1536,512]{1,0:T(8,128)(2,1)}, bf16[1536,512]{1,0:T(8,128)(2,1)}, bf16[1536,512]{1,0:T(8,128)(2,1)}, ...) custom-call(s32[1]{0:T(128)} %bitcast.node_ref, ...), custom_call_target="tpu_custom_call" | custom-call | flops 25769803776 | bytes 37748736 | tf_op jit(solution)/shard_map/expert_branch/pallas_call | solution.py:652
  171.1 3.5 collective-permute-done.5
  174.6 3.0 add_convert_fusion.2
  177.6 18.9 %all-to-all-start.3 = ((bf16[16,96,512]{2,1,0:T(8,128)(2,1)}), bf16[16,96,512]{2,1,0:T(8,128)(2,1)}, u32[]{:S(2)}, u32[]{:S(2)}) async-start(bf16[16,96,512]{2,1,0:T(8,128)(2,1)} %bitcast.72), calls=%async_computation.3 | async-start | bytes 3145728 | tf_op jit(solution)/shard_map/all_to_all | solution.py:967
  214.8 46.2 %collective-permute-done.27 = bf16[512,2048]{1,0:T(8,128)(2,1)} collective-permute-done((bf16[512,2048]{1,0:T(8,128)(2,1)}, bf16[512,2048]{1,0:T(8,128)(2,1)}, u32[]{:S(2)}, u32[]{:S(2)}) %collective-permute-start.27) | collective-permute-done | bytes 2097184 | tf_op jit(solution)/shard_map/ppermute | solution.py:892
  261.0 4.5 add_convert_fusion.5
  268.3 4.9 %combine.2.token_ref = bf16[1024,512]{1,0:T(8,128)(2,1)} custom-call(s32[1024,1]{1,0:T(8,128)S(1)} %copy-done.15, bf16[1536,512]{1,0:T(8,128)(2,1)} %bitcast.21.got_ref), custom_call_target="tpu_custom_call" | custom-call | flops 1610612736 | bytes 2097152 | tf_op jit(solution)/shard_map/combine/pallas_call | solution.py:468
  273.2 3.8 add_convert_fusion.3
  277.2 3.0 add_convert_fusion.1
  280.2 5.8 %all-to-all-start.2 = ((bf16[16,96,512]{2,1,0:T(8,128)(2,1)}), bf16[16,96,512]{2,1,0:T(8,128)(2,1)}, u32[]{:S(2)}, u32[]{:S(2)}) async-start(bf16[16,96,512]{2,1,0:T(8,128)(2,1)} %bitcast.71), calls=%async_computation.2 | async-start | bytes 3145728 | tf_op jit(solution)/shard_map/all_to_all | solution.py:967
  292.3 10.6 %middle_back.1 = (f32[1024,1024]{1,0:T(8,128)S(1)}, bf16[1024,512]{1,0:T(8,128)(2,1)S(1)}, f32[8,1024]{1,0:T(8,128)S(1)}, bf16[256,1024]{1,0:T(8,128)(2,1)S(1)}, bf16[256,1024]{1,0:T(8,128)(2,1)}) custom-call(s32[1]{0:T(128)} %bitcast.node_ref, s32[512,1]{1,0:T(8,128)S(1)} %add.346.source_ref, bf16[1024,1024]{1,0:T(8,128)(2,1)S(1)} %copy-done.5, ...), custom_call_target="tpu_custom_call" | custom-call | flops 2147483648 | bytes 18874368 | tf_op jit(solution)/shard_map/middle_back/pallas_call | solution.py:381
  305.0 19.2 %attend_back.1 = (bf16[1024,512]{1,0:T(8,128)(2,1)S(1)}, bf16[1024,512]{1,0:T(8,128)(2,1)S(1)}, bf16[1024,512]{1,0:T(8,128)(2,1)S(1)}) custom-call(bf16[1024,1536]{1,0:T(8,128)(2,1)S(1)} %copy-done.29, bf16[1024,1536]{1,0:T(8,128)(2,1)S(1)} %copy-done.29, bf16[1024,1536]{1,0:T(8,128)(2,1)S(1)} %copy-done.29, ...), custom_call_target="tpu_custom_call" | custom-call | flops 10737418240 | bytes 8388608 | tf_op jit(solution)/shard_map/attend_back/pallas_call | solution.py:247
  326.0 23.3 %tail.1 = (f32[512,1024]{1,0:T(8,128)S(1)}, bf16[512,1024]{1,0:T(8,128)(2,1)}, bf16[512,1792]{1,0:T(8,128)(2,1)S(1)}, bf16[512,1792]{1,0:T(8,128)(2,1)}) custom-call(s32[1]{0:T(128)} %bitcast.node_ref, s32[1024,1]{1,0:T(8,128)S(1)} %copy-done.19, bf16[1024,1024]{1,0:T(8,128)(2,1)S(1)} %copy-done.31, f32[1,1024]{1,0:T(1,128)S(1)} %bitcast.66, ...), custom_call_target="tpu_custom_call" | custom-call | flops 6442450944 | bytes 16777216 | tf_op jit(solution)/shard_map/tail/pallas_call | solution.py:812
  362.4 12.1 %collective-permute-start.30 = (bf16[64,2048]{1,0:T(8,128)(2,1)S(1)}, bf16[64,2048]{1,0:T(8,128)(2,1)S(1)}, u32[]{:S(2)}, u32[]{:S(2)}) collective-permute-start(bf16[64,2048]{1,0:T(8,128)(2,1)S(1)} %get-tuple-element.126), channel_id=1, source_target_pairs={{0,8},{1,9},{2,10},{3,11},{4,12},{5,13},{6,14},{7,15},{8,0},{9,1},... | collective-permute-start | bytes 786440 | tf_op jit(solution)/shard_map/ppermute | solution.py:892
  374.5 22.5 %expert_weights.1 = (f32[1024,2048]{1,0:T(8,128)}, f32[2048,1024]{1,0:T(8,128)}) custom-call(s32[1]{0:T(128)} %bitcast.node_ref, bf16[1536,512]{1,0:T(8,128)(2,1)} %bitcast.12.refs_0_.own_ref, bf16[1536,512]{1,0:T(8,128)(2,1)S(1)} %copy-done.24, bf16[1536,1024]{1,0:T(8,128)(2,1)} %get-tuple-element.88.g_ref, bf16[1536,2048]{1,0:T(8,128)(2,1)} %get-tuple-element.89.act_ref, ...), custom_call_target="tpu_custom_call" | custom-call | flops 12884901888 | bytes 29360128 | tf_op jit(solution)/shard_map/expert_weights/pallas_call | solution.py:706
  404.2 4.0 combine.3
  413.0 6.8 %collective-permute-done.18 = bf16[128,1024]{1,0:T(8,128)(2,1)S(1)} collective-permute-done((bf16[128,1024]{1,0:T(8,128)(2,1)S(1)}, bf16[128,1024]{1,0:T(8,128)(2,1)S(1)}, u32[]{:S(2)}, u32[]{:S(2)}) %collective-permute-start.18) | collective-permute-done | bytes 262176 | tf_op jit(solution)/shard_map/ppermute | solution.py:892
  419.9 3.8 collective-permute-start.21
  435.2 3.6 fusion.9
  438.8 6.2 %collective-permute-done.12 = bf16[256,1792]{1,0:T(8,128)(2,1)S(1)} collective-permute-done((bf16[256,1792]{1,0:T(8,128)(2,1)S(1)}, bf16[256,1792]{1,0:T(8,128)(2,1)S(1)}, u32[]{:S(2)}, u32[]{:S(2)}) %collective-permute-start.12) | collective-permute-done | bytes 917536 | tf_op jit(solution)/shard_map/ppermute | solution.py:892
  445.2 3.8 collective-permute-start.15
  450.6 5.0 %collective-permute-done.13 = bf16[64,1792]{1,0:T(8,128)(2,1)S(1)} collective-permute-done((bf16[64,1792]{1,0:T(8,128)(2,1)S(1)}, bf16[64,1792]{1,0:T(8,128)(2,1)S(1)}, u32[]{:S(2)}, u32[]{:S(2)}) %collective-permute-start.13) | collective-permute-done | bytes 229408 | tf_op jit(solution)/shard_map/ppermute | solution.py:892
  455.9 9.0 %collective-permute-done.14 = bf16[64,1792]{1,0:T(8,128)(2,1)S(1)} collective-permute-done((bf16[64,1792]{1,0:T(8,128)(2,1)S(1)}, bf16[64,1792]{1,0:T(8,128)(2,1)S(1)}, u32[]{:S(2)}, u32[]{:S(2)}) %collective-permute-start.14) | collective-permute-done | bytes 229408 | tf_op jit(solution)/shard_map/ppermute | solution.py:892
  (214 shorter events, 99.1 us)
Async XLA Ops:
  1.2 14.9 %collective-permute-start = (bf16[512,1024]{1,0:T(8,128)(2,1)}, bf16[512,1024]{1,0:T(8,128)(2,1)S(1)}, u32[]{:S(2)}, u32[]{:S(2)}) collective-permute-start(bf16[512,1024]{1,0:T(8,128)(2,1)} %bitcast.57), channel_id=1, source_target_pairs={{0,16},{16,0},{1,17},{17,1},{2,18},{18,2},{3,19},{19,3},{4,20},{20... | collective-permute-start | bytes 3145736 | tf_op jit(solution)/shard_map/ppermute | solution.py:943
  7.7 51.4 %all-to-all-start.1 = ((bf16[16,96,512]{2,1,0:T(8,128)(2,1)}), bf16[16,96,512]{2,1,0:T(8,128)(2,1)}, u32[]{:S(2)}, u32[]{:S(2)}) async-start(bf16[16,96,512]{2,1,0:T(8,128)(2,1)} %bitcast.13), calls=%async_computation.1 | async-start | bytes 3145728 | tf_op jit(solution)/shard_map/all_to_all | solution.py:967
  59.0 60.0 %all-to-all-start = ((bf16[16,96,512]{2,1,0:T(8,128)(2,1)}), bf16[16,96,512]{2,1,0:T(8,128)(2,1)}, u32[]{:S(2)}, u32[]{:S(2)}) async-start(bf16[16,96,512]{2,1,0:T(8,128)(2,1)} %bitcast.60), calls=%async_computation | async-start | bytes 3145728 | tf_op jit(solution)/shard_map/all_to_all | solution.py:967
  118.9 3.8 collective-permute-start.4
  119.0 5.8 %collective-permute-start.3 = (bf16[1536,512]{1,0:T(8,128)(2,1)}, bf16[1536,512]{1,0:T(8,128)(2,1)S(1)}, u32[]{:S(2)}, u32[]{:S(2)}) collective-permute-start(bf16[1536,512]{1,0:T(8,128)(2,1)} %bitcast.12.refs_0_.own_ref), channel_id=1, source_target_pairs={{0,16},{16,0},{1,17},{17,1},{2,18},{18,2},{3,19},{19,3},{4,20},{20... | collective-permute-start | bytes 4718600 | tf_op jit(solution)/shard_map/ppermute | solution.py:943
  177.6 89.7 %all-to-all-start.3 = ((bf16[16,96,512]{2,1,0:T(8,128)(2,1)}), bf16[16,96,512]{2,1,0:T(8,128)(2,1)}, u32[]{:S(2)}, u32[]{:S(2)}) async-start(bf16[16,96,512]{2,1,0:T(8,128)(2,1)} %bitcast.72), calls=%async_computation.3 | async-start | bytes 3145728 | tf_op jit(solution)/shard_map/all_to_all | solution.py:967
  196.5 64.5 %collective-permute-start.22 = (bf16[512,2048]{1,0:T(8,128)(2,1)}, bf16[512,2048]{1,0:T(8,128)(2,1)}, u32[]{:S(2)}, u32[]{:S(2)}) collective-permute-start(bf16[512,2048]{1,0:T(8,128)(2,1)} %get-tuple-element.102), channel_id=1, source_target_pairs={{0,1},{1,0},{2,3},{3,2},{4,5},{5,4},{6,7},{7,6},{8,9},{9,8},{10,11... | collective-permute-start | bytes 6291464 | tf_op jit(solution)/shard_map/ppermute | solution.py:892
  198.6 62.4 %collective-permute-start.27 = (bf16[512,2048]{1,0:T(8,128)(2,1)}, bf16[512,2048]{1,0:T(8,128)(2,1)}, u32[]{:S(2)}, u32[]{:S(2)}) collective-permute-start(bf16[512,2048]{1,0:T(8,128)(2,1)} %get-tuple-element.109), channel_id=1, source_target_pairs={{0,1},{1,0},{2,3},{3,2},{4,5},{5,4},{6,7},{7,6},{8,9},{9,8},{10,11... | collective-permute-start | bytes 6291464 | tf_op jit(solution)/shard_map/ppermute | solution.py:892
  204.9 72.3 %collective-permute-start.6 = (bf16[1536,512]{1,0:T(8,128)(2,1)}, bf16[1536,512]{1,0:T(8,128)(2,1)}, u32[]{:S(2)}, u32[]{:S(2)}) collective-permute-start(bf16[1536,512]{1,0:T(8,128)(2,1)} %get-tuple-element.76), channel_id=1, source_target_pairs={{0,16},{16,0},{1,17},{17,1},{2,18},{18,2},{3,19},{19,3},{4,20},{20... | collective-permute-start | bytes 4718600 | tf_op jit(solution)/shard_map/ppermute | solution.py:943
  208.4 77.6 %collective-permute-start.7 = (bf16[1024,1024]{1,0:T(8,128)(2,1)}, bf16[1024,1024]{1,0:T(8,128)(2,1)}, u32[]{:S(2)}, u32[]{:S(2)}) collective-permute-start(bf16[1024,1024]{1,0:T(8,128)(2,1)} %get-tuple-element.80.dense_ref), channel_id=1, source_target_pairs={{0,16},{16,0},{1,17},{17,1},{2,18},{18,2},{3,19},{19,3},{4,20},{20... | collective-permute-start | bytes 6291464 | tf_op jit(solution)/shard_map/ppermute | solution.py:943
  265.5 83.8 %collective-permute-start.23 = (bf16[256,2048]{1,0:T(8,128)(2,1)}, bf16[256,2048]{1,0:T(8,128)(2,1)}, u32[]{:S(2)}, u32[]{:S(2)}) collective-permute-start(bf16[256,2048]{1,0:T(8,128)(2,1)} %get-tuple-element.120), channel_id=1, source_target_pairs={{0,2},{1,3},{2,0},{3,1},{4,6},{5,7},{6,4},{7,5},{8,10},{9,11},{10,... | collective-permute-start | bytes 3145736 | tf_op jit(solution)/shard_map/ppermute | solution.py:892
  273.2 12.8 %collective-permute-start.8 = (bf16[1024,512]{1,0:T(8,128)(2,1)}, bf16[1024,512]{1,0:T(8,128)(2,1)}, u32[]{:S(2)}, u32[]{:S(2)}) collective-permute-start(bf16[1024,512]{1,0:T(8,128)(2,1)} %combine.2.token_ref), channel_id=1, source_target_pairs={{0,16},{16,0},{1,17},{17,1},{2,18},{18,2},{3,19},{19,3},{4,20},{20... | collective-permute-start | bytes 3145736 | tf_op jit(solution)/shard_map/ppermute | solution.py:943
  277.0 79.3 %collective-permute-start.28 = (bf16[256,2048]{1,0:T(8,128)(2,1)}, bf16[256,2048]{1,0:T(8,128)(2,1)}, u32[]{:S(2)}, u32[]{:S(2)}) collective-permute-start(bf16[256,2048]{1,0:T(8,128)(2,1)} %get-tuple-element.118), channel_id=1, source_target_pairs={{0,2},{1,3},{2,0},{3,1},{4,6},{5,7},{6,4},{7,5},{8,10},{9,11},{10,... | collective-permute-start | bytes 3145736 | tf_op jit(solution)/shard_map/ppermute | solution.py:892
  280.2 123.0 %all-to-all-start.2 = ((bf16[16,96,512]{2,1,0:T(8,128)(2,1)}), bf16[16,96,512]{2,1,0:T(8,128)(2,1)}, u32[]{:S(2)}, u32[]{:S(2)}) async-start(bf16[16,96,512]{2,1,0:T(8,128)(2,1)} %bitcast.71), calls=%async_computation.2 | async-start | bytes 3145728 | tf_op jit(solution)/shard_map/all_to_all | solution.py:967
  351.4 11.1 %collective-permute-start.24 = (bf16[64,2048]{1,0:T(8,128)(2,1)S(1)}, bf16[64,2048]{1,0:T(8,128)(2,1)S(1)}, u32[]{:S(2)}, u32[]{:S(2)}) collective-permute-start(bf16[64,2048]{1,0:T(8,128)(2,1)S(1)} %get-tuple-element.127), channel_id=1, source_target_pairs={{0,4},{1,5},{2,6},{3,7},{4,8},{5,9},{6,10},{7,11},{8,12},{9,13},{1... | collective-permute-start | bytes 786440 | tf_op jit(solution)/shard_map/ppermute | solution.py:892
  353.3 43.7 %collective-permute-start.26 = (bf16[64,2048]{1,0:T(8,128)(2,1)S(1)}, bf16[64,2048]{1,0:T(8,128)(2,1)S(1)}, u32[]{:S(2)}, u32[]{:S(2)}) collective-permute-start(bf16[64,2048]{1,0:T(8,128)(2,1)S(1)} %get-tuple-element.128), channel_id=1, source_target_pairs={{0,12},{1,13},{2,14},{3,15},{4,0},{5,1},{6,2},{7,3},{8,4},{9,5},{1... | collective-permute-start | bytes 786440 | tf_op jit(solution)/shard_map/ppermute | solution.py:892
  355.3 43.2 %collective-permute-start.25 = (bf16[64,2048]{1,0:T(8,128)(2,1)S(1)}, bf16[64,2048]{1,0:T(8,128)(2,1)S(1)}, u32[]{:S(2)}, u32[]{:S(2)}) collective-permute-start(bf16[64,2048]{1,0:T(8,128)(2,1)S(1)} %get-tuple-element.129), channel_id=1, source_target_pairs={{0,8},{1,9},{2,10},{3,11},{4,12},{5,13},{6,14},{7,15},{8,0},{9,1},... | collective-permute-start | bytes 786440 | tf_op jit(solution)/shard_map/ppermute | solution.py:892
  357.6 41.0 %collective-permute-start.29 = (bf16[64,2048]{1,0:T(8,128)(2,1)S(1)}, bf16[64,2048]{1,0:T(8,128)(2,1)S(1)}, u32[]{:S(2)}, u32[]{:S(2)}) collective-permute-start(bf16[64,2048]{1,0:T(8,128)(2,1)S(1)} %get-tuple-element.124), channel_id=1, source_target_pairs={{0,4},{1,5},{2,6},{3,7},{4,8},{5,9},{6,10},{7,11},{8,12},{9,13},{1... | collective-permute-start | bytes 786440 | tf_op jit(solution)/shard_map/ppermute | solution.py:892
  359.1 40.1 %collective-permute-start.31 = (bf16[64,2048]{1,0:T(8,128)(2,1)S(1)}, bf16[64,2048]{1,0:T(8,128)(2,1)S(1)}, u32[]{:S(2)}, u32[]{:S(2)}) collective-permute-start(bf16[64,2048]{1,0:T(8,128)(2,1)S(1)} %get-tuple-element.125), channel_id=1, source_target_pairs={{0,12},{1,13},{2,14},{3,15},{4,0},{5,1},{6,2},{7,3},{8,4},{9,5},{1... | collective-permute-start | bytes 786440 | tf_op jit(solution)/shard_map/ppermute | solution.py:892
  362.4 38.3 %collective-permute-start.30 = (bf16[64,2048]{1,0:T(8,128)(2,1)S(1)}, bf16[64,2048]{1,0:T(8,128)(2,1)S(1)}, u32[]{:S(2)}, u32[]{:S(2)}) collective-permute-start(bf16[64,2048]{1,0:T(8,128)(2,1)S(1)} %get-tuple-element.126), channel_id=1, source_target_pairs={{0,8},{1,9},{2,10},{3,11},{4,12},{5,13},{6,14},{7,15},{8,0},{9,1},... | collective-permute-start | bytes 786440 | tf_op jit(solution)/shard_map/ppermute | solution.py:892
  397.0 11.4 %collective-permute-start.17 = (bf16[256,1024]{1,0:T(8,128)(2,1)}, bf16[256,1024]{1,0:T(8,128)(2,1)}, u32[]{:S(2)}, u32[]{:S(2)}) collective-permute-start(bf16[256,1024]{1,0:T(8,128)(2,1)} %get-tuple-element.98), channel_id=1, source_target_pairs={{0,1},{1,0},{2,3},{3,2},{4,5},{5,4},{6,7},{7,6},{8,9},{9,8},{10,11... | collective-permute-start | bytes 1572872 | tf_op jit(solution)/shard_map/ppermute | solution.py:892
  398.6 34.6 %collective-permute-start.10 = (bf16[512,1024]{1,0:T(8,128)(2,1)}, bf16[512,1024]{1,0:T(8,128)(2,1)}, u32[]{:S(2)}, u32[]{:S(2)}) collective-permute-start(bf16[512,1024]{1,0:T(8,128)(2,1)} %get-tuple-element.94), channel_id=1, source_target_pairs={{0,16},{16,0},{1,17},{17,1},{2,18},{18,2},{3,19},{19,3},{4,20},{20... | collective-permute-start | bytes 3145736 | tf_op jit(solution)/shard_map/ppermute | solution.py:943
  398.6 31.0 %collective-permute-start.11 = (bf16[512,1792]{1,0:T(8,128)(2,1)}, bf16[512,1792]{1,0:T(8,128)(2,1)}, u32[]{:S(2)}, u32[]{:S(2)}) collective-permute-start(bf16[512,1792]{1,0:T(8,128)(2,1)} %get-tuple-element.96), channel_id=1, source_target_pairs={{0,1},{1,0},{2,3},{3,2},{4,5},{5,4},{6,7},{7,6},{8,9},{9,8},{10,11... | collective-permute-start | bytes 5505032 | tf_op jit(solution)/shard_map/ppermute | solution.py:892
  410.5 9.2 %collective-permute-start.18 = (bf16[128,1024]{1,0:T(8,128)(2,1)S(1)}, bf16[128,1024]{1,0:T(8,128)(2,1)S(1)}, u32[]{:S(2)}, u32[]{:S(2)}) collective-permute-start(bf16[128,1024]{1,0:T(8,128)(2,1)S(1)} %get-tuple-element.133), channel_id=1, source_target_pairs={{0,2},{1,3},{2,0},{3,1},{4,6},{5,7},{6,4},{7,5},{8,10},{9,11},{10,... | collective-permute-start | bytes 786440 | tf_op jit(solution)/shard_map/ppermute | solution.py:892
  419.8 6.6 %collective-permute-start.19 = (bf16[32,1024]{1,0:T(8,128)(2,1)S(1)}, bf16[32,1024]{1,0:T(8,128)(2,1)S(1)}, u32[]{:S(2)}, u32[]{:S(2)}) collective-permute-start(bf16[32,1024]{1,0:T(8,128)(2,1)S(1)} %get-tuple-element.135), channel_id=1, source_target_pairs={{0,4},{1,5},{2,6},{3,7},{4,8},{5,9},{6,10},{7,11},{8,12},{9,13},{1... | collective-permute-start | bytes 196616 | tf_op jit(solution)/shard_map/ppermute | solution.py:892
  419.9 6.5 %collective-permute-start.21 = (bf16[32,1024]{1,0:T(8,128)(2,1)S(1)}, bf16[32,1024]{1,0:T(8,128)(2,1)S(1)}, u32[]{:S(2)}, u32[]{:S(2)}) collective-permute-start(bf16[32,1024]{1,0:T(8,128)(2,1)S(1)} %get-tuple-element.136), channel_id=1, source_target_pairs={{0,12},{1,13},{2,14},{3,15},{4,0},{5,1},{6,2},{7,3},{8,4},{9,5},{1... | collective-permute-start | bytes 196616 | tf_op jit(solution)/shard_map/ppermute | solution.py:892
  423.7 5.2 %collective-permute-start.20 = (bf16[32,1024]{1,0:T(8,128)(2,1)S(1)}, bf16[32,1024]{1,0:T(8,128)(2,1)S(1)}, u32[]{:S(2)}, u32[]{:S(2)}) collective-permute-start(bf16[32,1024]{1,0:T(8,128)(2,1)S(1)} %get-tuple-element.137), channel_id=1, source_target_pairs={{0,8},{1,9},{2,10},{3,11},{4,12},{5,13},{6,14},{7,15},{8,0},{9,1},... | collective-permute-start | bytes 196616 | tf_op jit(solution)/shard_map/ppermute | solution.py:892
  426.4 22.6 %collective-permute-start.9 = (bf16[512,1024]{1,0:T(8,128)(2,1)S(1)}, bf16[512,1024]{1,0:T(8,128)(2,1)S(1)}, u32[]{:S(2)}, u32[]{:S(2)}) collective-permute-start(bf16[512,1024]{1,0:T(8,128)(2,1)S(1)} %constant_dynamic-slice_fusion.2), channel_id=1, source_target_pairs={{0,16},{16,0},{1,17},{17,1},{2,18},{18,2},{3,19},{19,3},{4,20},{20... | collective-permute-start | bytes 3145736 | tf_op jit(solution)/shard_map/ppermute | solution.py:943
  431.5 13.5 %collective-permute-start.12 = (bf16[256,1792]{1,0:T(8,128)(2,1)S(1)}, bf16[256,1792]{1,0:T(8,128)(2,1)S(1)}, u32[]{:S(2)}, u32[]{:S(2)}) collective-permute-start(bf16[256,1792]{1,0:T(8,128)(2,1)S(1)} %get-tuple-element.123), channel_id=1, source_target_pairs={{0,2},{1,3},{2,0},{3,1},{4,6},{5,7},{6,4},{7,5},{8,10},{9,11},{10,... | collective-permute-start | bytes 2752520 | tf_op jit(solution)/shard_map/ppermute | solution.py:892
  445.1 10.4 %collective-permute-start.13 = (bf16[64,1792]{1,0:T(8,128)(2,1)S(1)}, bf16[64,1792]{1,0:T(8,128)(2,1)S(1)}, u32[]{:S(2)}, u32[]{:S(2)}) collective-permute-start(bf16[64,1792]{1,0:T(8,128)(2,1)S(1)} %get-tuple-element.130), channel_id=1, source_target_pairs={{0,4},{1,5},{2,6},{3,7},{4,8},{5,9},{6,10},{7,11},{8,12},{9,13},{1... | collective-permute-start | bytes 688136 | tf_op jit(solution)/shard_map/ppermute | solution.py:892
  445.2 10.7 %collective-permute-start.15 = (bf16[64,1792]{1,0:T(8,128)(2,1)S(1)}, bf16[64,1792]{1,0:T(8,128)(2,1)S(1)}, u32[]{:S(2)}, u32[]{:S(2)}) collective-permute-start(bf16[64,1792]{1,0:T(8,128)(2,1)S(1)} %get-tuple-element.131), channel_id=1, source_target_pairs={{0,12},{1,13},{2,14},{3,15},{4,0},{5,1},{6,2},{7,3},{8,4},{9,5},{1... | collective-permute-start | bytes 688136 | tf_op jit(solution)/shard_map/ppermute | solution.py:892
  449.0 15.9 %collective-permute-start.14 = (bf16[64,1792]{1,0:T(8,128)(2,1)S(1)}, bf16[64,1792]{1,0:T(8,128)(2,1)S(1)}, u32[]{:S(2)}, u32[]{:S(2)}) collective-permute-start(bf16[64,1792]{1,0:T(8,128)(2,1)S(1)} %get-tuple-element.132), channel_id=1, source_target_pairs={{0,8},{1,9},{2,10},{3,11},{4,12},{5,13},{6,14},{7,15},{8,0},{9,1},... | collective-permute-start | bytes 688136 | tf_op jit(solution)/shard_map/ppermute | solution.py:892
  (49 other events, 418.7 us)

commit v4 on v3

--- a/solution.py
+++ b/solution.py
@@ -9,6 +9,7 @@
 
 
 HEAD_DIM = 64
+LIMIT = 60 << 20
 EPS = 1e-05
 LANES = 128
 LOG2E = 1.4426950408889634
@@ -77,12 +78,15 @@
     return jnp.where(index == node, own, other)
 
 
-def permutation(source, columns):
-    lane = lax.broadcasted_iota(jnp.int32, (source.shape[0], columns), 1)
-    return (source == lane).astype(F32).astype(BF16)
-
-
-WIDE = 256
+def permutation(order_ref, start, count, block, columns, copies=1):
+    lane = lax.broadcasted_iota(jnp.int32, (block, columns), 1)
+    row = lax.broadcasted_iota(jnp.int32, (block, columns), 0)
+    pieces = []
+    for index in range(count // block):
+        place = start // block + index
+        first = order_ref[place // copies] * block + (place % copies) * (columns // copies)
+        pieces.append((row + first == lane).astype(F32))
+    return jnp.concatenate(pieces, axis=0).astype(BF16)
 
 
 def front_kernel(node_ref, own_ref, other_ref, gain_ref, w_ref, qkv_ref, normed_ref):
@@ -107,29 +111,28 @@
 
 def front(node, own, other, gain, w_qkv):
     rows, width = own.shape
-    blocks = width // WIDE
-    half = blocks // 2
+    half = width // 2
     return pl.pallas_call(
         front_kernel,
         grid_spec=pltpu.PrefetchScalarGridSpec(
             num_scalar_prefetch=1,
-            grid=(3 * half,),
+            grid=(3,),
             in_specs=[
                 fixed(own.shape),
                 fixed(own.shape),
                 fixed((1, width)),
-                spec((width, WIDE), lambda i, n: (0, (i % 3) * blocks + n[0] * half + i // 3)),
+                spec((width, half), lambda i, n: (0, 2 * i + n[0])),
             ],
             out_specs=[
-                spec((2 * rows, WIDE), lambda i, n: (0, i)),
+                spec((2 * rows, half), lambda i, n: (0, i)),
                 fixed((2 * rows, width)),
             ],
         ),
-        out_shape=[struct((2 * rows, 3 * width // 2), BF16), struct((2 * rows, width), BF16)],
+        out_shape=[struct((2 * rows, 3 * half), BF16), struct((2 * rows, width), BF16)],
         cost_estimate=pl.CostEstimate(
             flops=6 * rows * width * width, bytes_accessed=14 * rows * width, transcendentals=0
         ),
-        compiler_params=pltpu.CompilerParams(vmem_limit_bytes=32 << 20),
+        compiler_params=pltpu.CompilerParams(vmem_limit_bytes=28 << 20),
         name="front",
     )(node, own, other, gain[None], w_qkv)
 
@@ -137,8 +140,8 @@
 QB = 256
 
 
-def head_specs(seq):
-    return [spec((seq, LANES), lambda j, at=at: (0, (j // 2) * 6 + at + j % 2)) for at in (0, 2, 4)]
+def head_specs(seq, pairs):
+    return [spec((seq, LANES), lambda j, at=at: (0, at * pairs + j)) for at in range(3)]
 
 
 def attend_kernel(q_ref, k_ref, v_ref, out_ref, lse_ref, ot_ref):
@@ -178,19 +181,21 @@
     return pl.pallas_call(
         attend_kernel,
         grid=(pairs,),
-        in_specs=head_specs(seq),
+        in_specs=head_specs(seq, pairs),
         out_specs=[
             spec((seq, LANES), lambda j: (0, j)),
             spec((1, 8, seq), lambda j: (j, 0, 0)),
         ],
         out_shape=[struct((seq, pairs * LANES), BF16), struct((pairs, 8, seq), F32)],
-        scratch_shapes=[pltpu.VMEM((LANES, seq), F32)],
+        scratch_shapes=[
+            pltpu.VMEM((LANES, seq), F32),
+        ],
         cost_estimate=pl.CostEstimate(
             flops=pairs * 8 * seq * seq * LANES,
             bytes_accessed=pairs * seq * LANES * 8,
             transcendentals=pairs * seq * seq,
         ),
-        compiler_params=pltpu.CompilerParams(vmem_limit_bytes=32 << 20),
+        compiler_params=pltpu.CompilerParams(vmem_limit_bytes=14 << 20),
         name="attend",
     )(qkv, qkv, qkv)
 
@@ -247,7 +252,7 @@
     return pl.pallas_call(
         attend_back_kernel,
         grid=(pairs,),
-        in_specs=head_specs(seq) + [one, one, spec((1, 8, seq), lambda j: (j, 0, 0))],
+        in_specs=head_specs(seq, pairs) + [one, one, spec((1, 8, seq), lambda j: (j, 0, 0))],
         out_specs=[one] * 3,
         out_shape=[struct(attended.shape, BF16)] * 3,
         scratch_shapes=[
@@ -260,7 +265,7 @@
             bytes_accessed=pairs * seq * LANES * 16,
             transcendentals=pairs * seq * seq,
         ),
-        compiler_params=pltpu.CompilerParams(vmem_limit_bytes=32 << 20),
+        compiler_params=pltpu.CompilerParams(vmem_limit_bytes=20 << 20),
         name="attend_back",
     )(qkv, qkv, qkv, attended, grad, lse)
 
@@ -308,15 +313,16 @@
         cost_estimate=pl.CostEstimate(
             flops=2 * seq * width * width, bytes_accessed=12 * seq * width, transcendentals=0
         ),
-        compiler_params=pltpu.CompilerParams(vmem_limit_bytes=24 << 20),
+        compiler_params=pltpu.CompilerParams(vmem_limit_bytes=20 << 20),
         name="middle",
     )(node, tokens, tokens_other, own, other, w_out, gain[None])
 
 
 def middle_back_kernel(
     parts,
+    block,
     node_ref,
-    source_ref,
+    order_ref,
     dense_ref,
     dense_other_ref,
     token_ref,
@@ -358,7 +364,8 @@
     grad_ref[...] = hidden_grad
     low = hidden_grad.astype(BF16)
     attended_grad_ref[...] = dot_t(low, w_ref[...]).astype(BF16)
-    turned = dot_t(permutation(source_ref[...], half), attended_ref[...]).astype(BF16)
+    turn = permutation(order_ref, 0, half, block, half)
+    turned = dot_t(turn, attended_ref[...]).astype(BF16)
     acc_ref[...] += dot(turned, low)
 
     @pl.when(step == pl.num_programs(0) - 1)
@@ -369,22 +376,21 @@
 
 
 def middle_back(
-    node, source, dense, dense_other, token, token_other, hidden, cot, cot_other, attended, gain, w_out, parts
+    node, order, dense, dense_other, token, token_other, hidden, cot, cot_other, attended, gain, w_out, parts
 ):
     seq, width = hidden.shape
     half = width // 2
     rows = 256
     steps = seq // rows
-    half_row = spec((rows, width), lambda i, n: (i % (steps // 2), 0))
-    row = lambda columns: spec((rows, columns), lambda i, n: (i, 0))
+    half_row = spec((rows, width), lambda i, n, o: (i % (steps // 2), 0))
+    row = lambda columns: spec((rows, columns), lambda i, n, o: (i, 0))
     result = (half // parts, width)
     return pl.pallas_call(
-        functools.partial(middle_back_kernel, parts),
+        functools.partial(middle_back_kernel, parts, half // order.shape[0]),
         grid_spec=pltpu.PrefetchScalarGridSpec(
-            num_scalar_prefetch=1,
+            num_scalar_prefetch=2,
             grid=(seq // rows,),
             in_specs=[
-                fixed(source.shape),
                 row(width),
                 row(width),
                 row(half),
@@ -394,7 +400,7 @@
                 half_row,
                 row(half),
                 fixed((1, width)),
-                spec((half, width), lambda i, n: (n[0], 0)),
+                spec((half, width), lambda i, n, o: (n[0], 0)),
             ],
             out_specs=[row(width), row(half), fixed((8, width))] + [fixed(result)] * parts,
             scratch_shapes=[pltpu.VMEM((rows, width), F32), pltpu.VMEM((half, width), F32)],
@@ -408,10 +414,10 @@
         cost_estimate=pl.CostEstimate(
             flops=2 * seq * width * width, bytes_accessed=18 * seq * width, transcendentals=0
         ),
-        compiler_params=pltpu.CompilerParams(vmem_limit_bytes=32 << 20),
+        compiler_params=pltpu.CompilerParams(vmem_limit_bytes=28 << 20),
         name="middle_back",
     )(
-        node, source, dense, dense_other, token, token_other, hidden, cot, cot_other, attended,
+        node, order, dense, dense_other, token, token_other, hidden, cot, cot_other, attended,
         gain[None], w_out,
     )
 
@@ -450,7 +456,7 @@
         cost_estimate=pl.CostEstimate(
             flops=4 * slots * rows * half, bytes_accessed=4 * slots * half, transcendentals=0
         ),
-        compiler_params=pltpu.CompilerParams(vmem_limit_bytes=16 << 20),
+        compiler_params=pltpu.CompilerParams(vmem_limit_bytes=14 << 20),
         name="dispatch",
     )(node, place, own, other)
 
@@ -476,22 +482,22 @@
             bytes_accessed=4 * rows * got.shape[1],
             transcendentals=0,
         ),
-        compiler_params=pltpu.CompilerParams(vmem_limit_bytes=16 << 20),
+        compiler_params=pltpu.CompilerParams(vmem_limit_bytes=12 << 20),
         name="combine",
     )(place, got)
 
 
-def branch_kernel(dense, experts, parts, node_ref, *refs):
+def branch_kernel(dense, experts, parts, unit, node_ref, order_ref, *refs):
     if dense:
         x_refs, c_refs, refs = refs[:1], refs[1:3], refs[3:]
     else:
         x_refs, c_refs, refs = refs[:2], refs[2:4], refs[4:]
-    side_ref, wc_ref, wct_ref, up_ref, dn_ref = refs[:5]
-    refs = refs[5:]
+    side_ref, wct_ref, up_ref, dn_ref = refs[:4]
+    refs = refs[4:]
     if dense:
         out_refs, dx_refs, gsm_ref, probs_ref = refs[:1], refs[1:2], refs[2], refs[3]
-        gup_refs, gdn_refs = refs[4 : 4 + parts], refs[4 + parts : 4 + 2 * parts]
-        xt_ref, g_ref, a_ref, acc_ref, dxa_ref, act_ref, dpre_ref, gt_ref = refs[4 + 2 * parts :]
+        grad_refs = refs[4 : 4 + parts]
+        xt_ref, g_ref, a_ref, acc_ref, dxa_ref, act_ref, dpre_ref, gt_ref = refs[4 + parts :]
     else:
         out_refs, dx_refs, gsm_ref = refs[:2], refs[2:4], refs[4]
         g_ref, act_ref, dpre_ref, a_ref, acc_ref, dxa_ref = refs[5:]
@@ -517,13 +523,10 @@
         is_mix = (lane >= experts) & (lane < experts + 2)
         first = (lane == experts).astype(F32)
         second = (lane == experts + 1).astype(F32)
-        if dense:
-            turn = permutation(side_ref[...], width)
-        else:
-            picked = side_ref[...]
+        picked = side_ref[...]
 
         def prepare(at):
-            logits = sum(dot(x_refs[n][at, :], wc_ref[split[n], :]) for n in range(halves))
+            logits = sum(dot_t(x_refs[n][at, :], wct_ref[:, split[n]]) for n in range(halves))
 
             def soft(mask):
                 masked = jnp.where(mask, logits, -1e30)
@@ -549,8 +552,6 @@
                 cot = row_pick(node, place, c_refs[0][inside, :], c_refs[1][inside, :])
                 scaled = (factor * cot.astype(F32)).astype(BF16)
                 g_ref[at, :] = scaled
-                xt_ref[:, at] = dot_t(turn, x_refs[0][at, :]).astype(BF16)
-                gt_ref[:, at] = dot_t(turn, scaled).astype(BF16)
             else:
                 for n in range(halves):
                     g_ref[at, split[n]] = (factor * c_refs[n][at, :].astype(F32)).astype(BF16)
@@ -558,6 +559,16 @@
             dxa_ref[at, :] = jnp.zeros((small, width), F32)
 
         chunks(rows, small, prepare)
+        if dense:
+
+            def transpose(at):
+                turn = permutation(order_ref, at.start, small, unit, width)
+                for index in range(rows // big):
+                    some = slice(index * big, (index + 1) * big)
+                    xt_ref[at, some] = dot_t(turn, x_refs[0][some, :]).astype(BF16)
+                    gt_ref[at, some] = dot_t(turn, g_ref[some, :]).astype(BF16)
+
+            chunks(width, small, transpose)
 
     def forward(at):
         pre = sum(dot(x_refs[n][at, :], up_ref[split[n], :]) for n in range(halves))
@@ -583,10 +594,15 @@
         for part in range(parts):
 
             def weights(at):
-                start = pl.multiple_of(part * size + at.start, small)
-                rows_at = pl.ds(start, small)
-                gup_refs[part][at, :] = dot(xt_ref[rows_at, :], dpre_ref[...]).astype(BF16)
-                gdn_refs[part][at, :] = dot(gt_ref[rows_at, :], act_ref[...]).astype(BF16)
+                rows_at = pl.ds(pl.multiple_of(part * size + at.start, small), small)
+                pair = (
+                    dot(xt_ref[rows_at, :], dpre_ref[...]).astype(BF16),
+                    dot(gt_ref[rows_at, :], act_ref[...]).astype(BF16),
+                )
+                for index in range(2 * small // unit):
+                    to = pl.multiple_of(2 * at.start + index * unit, unit)
+                    place = index // 2 * unit
+                    grad_refs[part][pl.ds(to, unit), :] = pair[index % 2][place : place + unit]
 
             chunks(size, small, weights)
 
@@ -617,15 +633,15 @@
         chunks(rows, small, finish)
 
 
-def branch(node, xs, cs, side, head, head_t, up, down, experts, parts):
+def branch(node, order, xs, cs, side, head_t, up, down, experts, parts):
     dense = len(xs) == 1
     rows, half = xs[0].shape
     width = len(xs) * half
     hidden = up.shape[1]
     block = 512
-    column = lambda size: spec((size, block), lambda f, n: (0, f))
+    column = lambda size: spec((size, block), lambda f, n, o: (0, f))
     up_spec = column(width)
-    down_spec = up_spec if dense else spec((block, width), lambda f, n: (f, 0))
+    down_spec = up_spec if dense else spec((block, width), lambda f, n, o: (f, 0))
     outs = [(fixed((rows, half)), struct((rows, half), BF16))] * (2 * len(xs))
     outs = outs + [(fixed((LANES, width)), struct((LANES, width), F32))]
     sums = [
@@ -635,8 +651,8 @@
     ]
     if dense:
         outs = outs + [(fixed((rows, LANES)), struct((rows, LANES), F32))]
-        size = width // parts
-        outs = outs + [(column(size), struct((size, hidden), BF16))] * (2 * parts)
+        size = 2 * width // parts
+        outs = outs + [(column(size), struct((size, hidden), BF16))] * parts
         scratch = [
             pltpu.VMEM((width, rows), BF16),
             pltpu.VMEM((rows, width), BF16),
@@ -650,14 +666,13 @@
         outs = outs + [(column(rows), struct((rows, hidden), BF16))] * 2
         scratch = sums
     return pl.pallas_call(
-        functools.partial(branch_kernel, dense, experts, parts),
+        functools.partial(branch_kernel, dense, experts, parts, width // order.shape[0]),
         grid_spec=pltpu.PrefetchScalarGridSpec(
-            num_scalar_prefetch=1,
+            num_scalar_prefetch=2,
             grid=(hidden // block,),
             in_specs=[fixed(one.shape) for one in [*xs, *cs]]
             + [
                 fixed(side.shape),
-                fixed((width, LANES)),
                 fixed((LANES, width)),
                 up_spec,
                 down_spec,
@@ -671,12 +686,12 @@
             bytes_accessed=12 * width * hidden + 8 * rows * width,
             transcendentals=rows * hidden,
         ),
-        compiler_params=pltpu.CompilerParams(vmem_limit_bytes=58 << 20),
+        compiler_params=pltpu.CompilerParams(vmem_limit_bytes=LIMIT),
         name="dense_branch" if dense else "expert_branch",
-    )(node, *xs, *cs, side, head, head_t, up, down)
-
-
-def expert_weights_kernel(node_ref, own_ref, other_ref, g_ref, act_ref, dpre_ref, gup_ref, gdn_ref, xt_ref):
+    )(node, order, *xs, *cs, side, head_t, up, down)
+
+
+def expert_up_kernel(node_ref, own_ref, other_ref, dpre_ref, grad_ref, xt_ref):
     rows, half = own_ref.shape
     node = node_ref[0]
 
@@ -691,46 +706,69 @@
             chunks(rows, 256, turn)
 
     def weights(at):
-        gup_ref[at, :] = dot(xt_ref[at, :], dpre_ref[...])
+        grad_ref[at, :] = dot(xt_ref[at, :], dpre_ref[...])
 
     chunks(2 * half, 256, weights)
-    gdn_ref[...] = dot_n(act_ref[...], g_ref[...])
-
-
-def expert_weights(node, own, other, g, act, dpre):
+
+
+def expert_down_kernel(act_ref, g_ref, grad_ref):
+    grad_ref[...] = dot_n(act_ref[...], g_ref[...])
+
+
+def expert_up_grad(node, own, other, dpre):
     rows, half = own.shape
-    width = 2 * half
-    hidden = act.shape[1]
+    hidden = dpre.shape[1]
     block = 512
-    column = spec((rows, block), lambda f, n: (0, f))
     return pl.pallas_call(
-        expert_weights_kernel,
+        expert_up_kernel,
         grid_spec=pltpu.PrefetchScalarGridSpec(
             num_scalar_prefetch=1,
             grid=(hidden // block,),
-            in_specs=[fixed(own.shape), fixed(own.shape), fixed(g.shape), column, column],
-            out_specs=[
-                spec((width, block), lambda f, n: (0, f)),
-                spec((block, width), lambda f, n: (f, 0)),
+            in_specs=[
+                fixed(own.shape),
+                fixed(own.shape),
+                spec((rows, block), lambda f, n: (0, f)),
             ],
-            scratch_shapes=[pltpu.VMEM((width, rows), BF16)],
-        ),
-        out_shape=[struct((width, hidden), F32), struct((hidden, width), F32)],
+            out_specs=spec((2 * half, block), lambda f, n: (0, f)),
+            scratch_shapes=[pltpu.VMEM((2 * half, rows), BF16)],
+        ),
+        out_shape=struct((2 * half, hidden), F32),
         cost_estimate=pl.CostEstimate(
-            flops=4 * rows * width * hidden,
-            bytes_accessed=8 * width * hidden + 4 * rows * hidden,
+            flops=4 * rows * half * hidden,
+            bytes_accessed=8 * half * hidden + 2 * rows * hidden,
             transcendentals=0,
         ),
-        compiler_params=pltpu.CompilerParams(vmem_limit_bytes=48 << 20),
-        name="expert_weights",
-    )(node, own, other, g, act, dpre)
+        compiler_params=pltpu.CompilerParams(vmem_limit_bytes=36 << 20),
+        name="expert_up_grad",
+    )(node, own, other, dpre)
+
+
+def expert_down_grad(act, g):
+    rows, hidden = act.shape
+    width = g.shape[1]
+    block = 256
+    return pl.pallas_call(
+        expert_down_kernel,
+        grid=(hidden // block,),
+        in_specs=[spec((rows, block), lambda f: (0, f)), fixed(g.shape)],
+        out_specs=spec((block, width), lambda f: (f, 0)),
+        out_shape=struct((hidden, width), F32),
+        cost_estimate=pl.CostEstimate(
+            flops=2 * rows * width * hidden,
+            bytes_accessed=4 * width * hidden + 2 * rows * hidden,
+            transcendentals=0,
+        ),
+        compiler_params=pltpu.CompilerParams(vmem_limit_bytes=28 << 20),
+        name="expert_down_grad",
+    )(act, g)
 
 
 def tail_kernel(
     parts,
     ln_lane,
+    block,
     node_ref,
-    source_ref,
+    order_ref,
     x_ref,
     gain_ref,
     small_ref,
@@ -752,17 +790,17 @@
 
     @pl.when(step == 0)
     def _():
-        turn = permutation(source_ref[...], width)
-
         def prepare(at):
-            xt_ref[:, at] = dot_t(turn, x_ref[at, :]).astype(BF16)
-            acc_ref[at, :] = jnp.zeros((256, width), F32)
-
-        chunks(seq, 256, prepare)
+            turn = permutation(order_ref, at.start, 256, block, width, 2)
+            for index in range(seq // 512):
+                some = slice(index * 512, (index + 1) * 512)
+                xt_ref[at, some] = dot_t(turn, x_ref[some, :]).astype(BF16)
+
+        chunks(width, 256, prepare)
 
     for which, ref in enumerate((dq_ref, dk_ref, dv_ref)):
 
-        @pl.when((step < last) & (step % 3 == which))
+        @pl.when(step == which)
         def _():
             for part in range(parts):
 
@@ -773,7 +811,8 @@
                 chunks(size, 256, weights)
 
             def back(at):
-                acc_ref[at, :] += dot_t(ref[at, :], w_ref[...])
+                piece = dot_t(ref[at, :], w_ref[...])
+                acc_ref[at, :] = acc_ref[at, :] + piece if which else piece
 
             chunks(seq, 256, back)
 
@@ -781,61 +820,58 @@
     def _():
         gain = gain_ref[...]
         node = node_ref[0]
-        total = jnp.zeros((1, width), F32)
-        for piece in range(seq // 256):
-            rows = slice(piece * 256, (piece + 1) * 256)
-            total = total + jnp.sum(
-                acc_ref[rows] * (x_ref[rows, :].astype(F32) / gain), axis=0, keepdims=True
+
+        def column_sum(index, total):
+            rows = pl.ds(pl.multiple_of(index * 256, 256), 256)
+            return total + jnp.sum(
+                acc_ref[rows, :] * x_ref[rows, :].astype(F32), axis=0, keepdims=True
             )
+
+        total = lax.fori_loop(0, seq // 256, column_sum, jnp.zeros((1, width), F32)) / gain
         row = lax.broadcasted_iota(jnp.int32, (LANES, 1), 0)
         small = (small_ref[...] + jnp.where(row == ln_lane, total, 0.0)).astype(BF16)
-        turned = dot_t(permutation(source_ref[...], width), small).astype(BF16)
         for part in range(parts):
-            part_refs[part][:, 0:LANES] = turned[part * size : (part + 1) * size]
-            part_refs[part][:, LANES:WIDE] = jnp.zeros((size, WIDE - LANES), BF16)
+
+            def turn(at):
+                rows = permutation(order_ref, part * size + at.start, 256, block, width, 2)
+                part_refs[part][at, 0:LANES] = dot_t(rows, small).astype(BF16)
+
+            chunks(size, 256, turn)
         keep_ref[...] = acc_ref[pl.ds(pl.multiple_of(node * own, own), own), :]
         send_ref[...] = acc_ref[pl.ds(pl.multiple_of((1 - node) * own, own), own), :].astype(BF16)
 
 
-def tail(node, source, normed, gain, small, dq, dk, dv, w_qkv, parts, ln_lane):
+def tail(node, order, normed, gain, small, dq, dk, dv, w_qkv, parts, ln_lane):
     seq, width = normed.shape
-    blocks = width // WIDE
-    half = blocks // 2
-    steps = 3 * half
-    grad_spec = spec((seq, WIDE), lambda i, n: (0, jnp.minimum(i // 3, half - 1)))
-
-    def column(i, n):
-        i = jnp.minimum(i, steps - 1)
-        return (0, (i % 3) * blocks + n[0] * half + i // 3)
-
-    part = (width // parts, WIDE)
+    half = width // 2
+    steps = 3
+    part = (width // parts, half)
     return pl.pallas_call(
-        functools.partial(tail_kernel, parts, ln_lane),
+        functools.partial(tail_kernel, parts, ln_lane, half // order.shape[0]),
         grid_spec=pltpu.PrefetchScalarGridSpec(
-            num_scalar_prefetch=1,
+            num_scalar_prefetch=2,
             grid=(steps + 1,),
             in_specs=[
-                fixed(source.shape),
                 fixed(normed.shape),
                 fixed((1, width)),
                 fixed((LANES, width)),
-                grad_spec,
-                grad_spec,
-                grad_spec,
-                spec((width, WIDE), column),
+                fixed((seq, half)),
+                fixed((seq, half)),
+                fixed((seq, half)),
+                spec((width, half), lambda i, n, o: (0, 2 * jnp.minimum(i, steps - 1) + n[0])),
             ],
             out_specs=[fixed((seq // 2, width)), fixed((seq // 2, width))]
-            + [spec(part, lambda i, n: (0, i))] * parts,
+            + [spec(part, lambda i, n, o: (0, i))] * parts,
             scratch_shapes=[pltpu.VMEM((width, seq), BF16), pltpu.VMEM((seq, width), F32)],
         ),
         out_shape=[struct((seq // 2, width), F32), struct((seq // 2, width), BF16)]
-        + [struct((width // parts, (steps + 1) * WIDE), BF16)] * parts,
+        + [struct((width // parts, steps * half + LANES), BF16)] * parts,
         cost_estimate=pl.CostEstimate(
             flops=6 * seq * width * width, bytes_accessed=16 * seq * width, transcendentals=0
         ),
         compiler_params=pltpu.CompilerParams(vmem_limit_bytes=32 << 20),
         name="tail",
-    )(node, source, normed, gain[None], small, dq, dk, dv, w_qkv)
+    )(node, order, normed, gain[None], small, dq, dk, dv, w_qkv)
 
 
 class Grid:
@@ -886,25 +922,25 @@
             tables.append(table)
         return jnp.array(tables, jnp.int32)[node, member]
 
-    def reduce(self, parts, gates=(None, None, None)):
-        for stage, size in enumerate(self.sizes):
-            came = [
-                lax.ppermute(parts[by], ("node", "expert"), self.shift(stage, by))
-                for by in range(1, size)
-            ]
-            if gates[stage] is not None:
-                came = [after(other, gates[stage]) for other in came]
-            pieces = self.sizes[stage + 1] if stage < 2 else 1
-            rows = parts[0].shape[0] // pieces
-            sums = []
-            for piece in range(pieces):
-                at = slice(piece * rows, (piece + 1) * rows)
-                total = parts[0][at].astype(F32)
-                for other in came:
-                    total = total + other[at].astype(F32)
-                sums.append(total.astype(BF16) if stage < 2 else total)
-            parts = sums
-        return parts[0]
+    def send(self, parts, stage):
+        return [
+            lax.ppermute(parts[by], ("node", "expert"), self.shift(stage, by))
+            for by in range(1, self.sizes[stage])
+        ]
+
+    def add(self, parts, came, stage, *gates):
+        if gates:
+            came = [after(other, *gates) for other in came]
+        pieces = self.sizes[stage + 1] if stage < 2 else 1
+        rows = parts[0].shape[0] // pieces
+        sums = []
+        for piece in range(pieces):
+            at = slice(piece * rows, (piece + 1) * rows)
+            total = parts[0][at].astype(F32)
+            for other in came:
+                total = total + other[at].astype(F32)
+            sums.append(total.astype(BF16) if stage < 2 else total)
+        return sums
 
 
 def shards(
@@ -980,81 +1016,86 @@
     )
 
     got_rows = exchange(dispatch_rows(scalar, place_rows, inner_low, inner_low, slots))
-    head = jnp.concatenate(
+    head_t = jnp.concatenate(
         [w_router, w_mix, jnp.zeros((width, LANES - experts - 2), BF16)], axis=1
-    )
-    head_t = head.T
+    ).T
     picked = (jnp.arange(LANES) == member).astype(F32)[None]
-
-    def sources(block):
-        return (order_of[:, None] * block + jnp.arange(block)[None, :]).reshape(-1, 1)
-
     results = branch(
-        scalar, [inner_low], [own_cot, other_cot], sources(width // members), head, head_t, w_up,
-        w_down, experts, parts,
+        scalar, order_of, [inner_low], [own_cot, other_cot], picked, head_t, w_up, w_down,
+        experts, parts,
     )
     dense_out, dense_dx, small_dense, probs = results[:4]
-    grad_up, grad_down = results[4 : 4 + parts], results[4 + parts :]
+    pair0 = results[4:]
+    came = grid.send(pair0, 0)
     got_rows = after(got_rows, small_dense)
     expert_rows = [got_rows, swap(got_rows)]
     out_keep, out_send, dx_keep, dx_send, small_expert, expert_g, expert_act, expert_dpre = branch(
-        scalar, expert_rows, [got_cot, swap(got_cot)], picked, head, head_t, expert_up[0],
+        scalar, order_of, expert_rows, [got_cot, swap(got_cot)], picked, head_t, expert_up[0],
         expert_down[0], experts, parts,
     )
 
     sent_dx, got_dx = give_back(dx_keep, dx_send)
+    pair1 = grid.add(pair0, came, 0, sent_dx)
+    came = grid.send(pair1, 1)
     _, got_out = give_back(out_keep, after(out_send, sent_dx))
-    token_dx = combine_rows(place_column, got_dx)
+    grad_expert_down = expert_down_grad(expert_act, after(expert_g, sent_dx))
+    token_dx = combine_rows(place_column, after(got_dx, pair1, grad_expert_down))
     results = middle_back(
-        scalar, sources(half // members), dense_dx, swap(dense_dx), token_dx, swap(token_dx),
-        hidden, own_cot, other_cot, attended_own, ln2_gain, w_out, parts,
+        scalar, order_of, dense_dx, swap(dense_dx), token_dx, swap(token_dx), hidden, own_cot,
+        other_cot, attended_own, ln2_gain, w_out, parts,
     )
     hidden_grad, attended_grad, ln2_row = results[:3]
-    grad_w_out = results[3:]
+    out0 = results[3:]
+    out_came = grid.send(out0, 0)
+    pair2 = grid.add(pair1, came, 1, ln2_row)
+    came = grid.send(pair2, 2)
     dq, dk, dv = attend_back(qkv, attended_own, attended_grad, lse)
 
     small = small_dense + small_expert
     small = small + jnp.where(jnp.arange(LANES)[:, None] == experts + 3, ln2_row[0:1], 0.0)
-    block = width // (2 * members)
-    source = (
-        order_of[:, None, None] * block
-        + jnp.arange(2)[None, :, None] * half
-        + jnp.arange(block)[None, None, :]
-    ).reshape(-1, 1)
     results = tail(
-        scalar, source, normed_low, ln1_gain, small, dq, dk, dv, w_qkv, parts, experts + 2
-    )
-    normed_grad = results[0] + swap(results[1]).astype(F32)
-    _, base_one, inverse_one = layer_norm(own_tokens.astype(F32), ln1_gain)
-    input_grad = lax.dynamic_slice_in_dim(hidden_grad, own_start, own_rows, 0) + norm_backward(
-        normed_grad, base_one, inverse_one, ln1_gain
-    )
-    gate = results[0]
-    grad_expert_up, grad_expert_down = expert_weights(
-        scalar, *expert_rows, after(expert_g, gate), expert_act, expert_dpre
-    )
-    late = grad_expert_up
-    grad_w_up = grid.reduce(grad_up, (sent_dx, ln2_row, late))
-    grad_w_down = grid.reduce(grad_down, (sent_dx, ln2_row, late))
-    grad_w_out = grid.reduce(grad_w_out, (gate, late, None))
-
-    token_out = combine_rows(place_column, after(got_out, late)).astype(F32)
+        scalar, order_of, normed_low, ln1_gain, small, dq, dk, dv, w_qkv, parts, experts + 2
+    )
+    grad_keep, grad_send, last0 = results[0], results[1], results[2:]
+    last_came = grid.send(last0, 0)
+    out1 = grid.add(out0, out_came, 0, grad_keep)
+    out_came = grid.send(out1, 1)
+    grad_expert_up = expert_up_grad(scalar, *expert_rows, after(expert_dpre, grad_keep))
+
+    token_out = combine_rows(place_column, after(got_out, grad_expert_up)).astype(F32)
     chance = jnp.sum(jnp.where(route_onehot, probs[:, :experts], 0.0), axis=1, keepdims=True)
     scaled = chance * probs[:, experts + 1 : experts + 2] * token_out
     total_out = dense_out.astype(F32) + in_order(scaled, jnp.zeros_like(scaled), 1)
     total_out = total_out.astype(BF16)
     out_mine = lax.dynamic_slice_in_dim(total_out, own_start, own_rows, 0)
     out_other = swap(lax.dynamic_slice_in_dim(total_out, own_rows - own_start, own_rows, 0))
+    out2 = grid.add(out1, out_came, 1, grad_expert_up)
+    out_came = grid.send(out2, 2)
+
+    last1 = grid.add(last0, last_came, 0, grad_expert_up, total_out)
+    last_came = grid.send(last1, 1)
+
+    unit = width // members
+    both = grid.add(pair2, came, 2, last1)[0]
+    grad_w_up, grad_w_down = both[:unit], both[unit:]
     hidden_own = lax.dynamic_slice_in_dim(hidden, own_start, own_rows, 0)
+    out_other = after(out_other, last1)
     mixed_out = (hidden_own + out_mine.astype(F32) + out_other.astype(F32)).astype(BF16)
-
-    last = grid.reduce(results[2:]).reshape(2, block, -1)
+    last2 = grid.add(last1, last_came, 1, mixed_out, both)
+    last_came = grid.send(last2, 2)
+    grad_w_out = grid.add(out2, out_came, 2, last2)[0]
+    normed_grad = grad_keep + after(swap(grad_send), last2).astype(F32)
+    _, base_one, inverse_one = layer_norm(own_tokens.astype(F32), ln1_gain)
+    input_grad = lax.dynamic_slice_in_dim(hidden_grad, own_start, own_rows, 0) + norm_backward(
+        normed_grad, base_one, inverse_one, ln1_gain
+    )
+    block = width // (2 * members)
+    last = grid.add(last2, last_came, 2, input_grad, grad_w_out)[0].reshape(2, block, -1)
     kept = lax.dynamic_index_in_dim(last, node, 0, False)
     other = swap(lax.dynamic_index_in_dim(last, 1 - node, 0, False).astype(BF16)).astype(F32)
 
     def columns(rows):
-        rows = rows[:, : 3 * half].reshape(block, half // WIDE, 3, WIDE)
-        return rows.transpose(0, 2, 1, 3).reshape(block, 3, half)
+        return rows[:, : 3 * half].reshape(block, 3, half)
 
     grad_w_qkv = in_order(columns(kept), columns(other), 2).reshape(block, 3 * width)
     small = kept[:, 3 * half :] + other[:, 3 * half :]

time: 477 us -> 414 us (0.87)
  waiting for transfers between devices: 94 us -> 70.3 us
  starting transfers between devices: 80.6 us -> 57 us
  other arithmetic: 45.1 us -> 36.1 us
    ppermute x20 -> x15, waiting for transfers between devices: 81 us -> 58.9 us  [send(): lax.ppermute(parts[by], ('node', 'expert'), self.shift(stage, by))]
    ppermute x20 -> x15, starting transfers between devices: 38.2 us -> 26.1 us  [send(): lax.ppermute(parts[by], ('node', 'expert'), self.shift(stage, by))]
    all_to_all x4, starting transfers between devices: 40.4 us -> 28.9 us  [exchange(): lax.all_to_all(value, 'expert', split_axis=0, concat_axis=0, tiled=True)]
    reshape x2 -> x0, other arithmetic: 5.13 us -> none  [the longest x1 3.57 us: shards(): input_grad.reshape(tokens.shape)]
    convert_element_type x8 -> x7, other arithmetic: 15 us -> 12.6 us  [the longest x6 11.1 us: add(): sums.append(total.astype(BF16) if stage < 2 else total)]
    unnamed x91 -> x92, local copies, waits for them, and re-layouts: 23.1 us -> 25.3 us
    pallas_call x6 -> x7, Pallas kernels: 164 us -> 163 us  [the longest x2 94.2 us: branch(): pl.pallas_call(functools.partial(branch_kernel, dense, experts, parts, wi...]
  transfers between devices with their start and end apart: 36 -> 31, of which waited for: 16 -> 11; matrix products, arithmetic and copies ran while one was open for 11% -> 11% of each run, Pallas kernels for 35% -> 40%
where the time goes in v4:
time: 414 us; the launch traced here: 408 us
  Pallas kernels  208 us (50%)
  waiting for transfers between devices  70.3 us (17%)
  starting transfers between devices  57 us (14%)
  other arithmetic  36.1 us (9%)
  local copies, waits for them, and re-layouts  33.6 us (8%)
    pallas_call x2, Pallas kernels, branch(): pl.pallas_call(functools.partial(branch_kernel, dense, experts, parts, wi...  94.2 us
    ppermute x15, waiting for transfers between devices, send(): lax.ppermute(parts[by], ('node', 'expert'), self.shift(stage, by))  58.9 us
    all_to_all x4, starting transfers between devices, exchange(): lax.all_to_all(value, 'expert', split_axis=0, concat_axis=0, tiled=True)  28.9 us
    ppermute x15, starting transfers between devices, send(): lax.ppermute(parts[by], ('node', 'expert'), self.shift(stage, by))  26.1 us
    unnamed x92, local copies, waits for them, and re-layouts  25.3 us
    pallas_call x1, Pallas kernels, tail(): pl.pallas_call(functools.partial(tail_kernel, parts, ln_lane, half // ord...  18.6 us
    pallas_call x1, Pallas kernels, attend_back(): pl.pallas_call(attend_back_kernel, grid=(pairs,), in_specs=head_specs(seq...  18.3 us
    pallas_call x1, Pallas kernels, expert_up_grad(): pl.pallas_call(expert_up_kernel, grid_spec=pltpu.PrefetchScalarGridSpec(n...  14.3 us
  transfers between devices with their start and end apart: 31, of which 11 were waited for; matrix products, arithmetic and copies ran while one was open for 11% of the time, Pallas kernels for 40%

profile of v4, /device:TPU:0, one launch (start us, length us, event | category | flops | bytes accessed | tf_op | source)
XLA Modules:
  0.0 407.7 jit_solution(7708370245257874016)
XLA Ops:
  3.7 3.9 dispatch.3
  7.7 8.4 %all-to-all-start.1 = ((bf16[16,96,512]{2,1,0:T(8,128)(2,1)}), bf16[16,96,512]{2,1,0:T(8,128)(2,1)}, u32[]{:S(2)}, u32[]{:S(2)}) async-start(bf16[16,96,512]{2,1,0:T(8,128)(2,1)} %bitcast.13), calls=%async_computation.1 | async-start | bytes 3145728 | tf_op jit(solution)/shard_map/all_to_all | solution.py:1003
  16.1 3.1 copy-done.23
  19.3 6.8 %front.1 = (bf16[1024,1536]{1,0:T(8,128)(2,1)S(1)}, bf16[1024,1024]{1,0:T(8,128)(2,1)S(1)}) custom-call(s32[1]{0:T(128)} %bitcast.node_ref, bf16[512,1024]{1,0:T(8,128)(2,1)S(1)} %bitcast.47, bf16[512,1024]{1,0:T(8,128)(2,1)S(1)} %collective-permute-done.other_ref.tok_other_ref, f32[1,1024]{1,0:T(1,128)S(1)} %bitcast.54, bf16[1024,3072]{1,0:T(8,128)(2,1)S(1)} %copy-done.23), custom_call_target="tpu_custom_call" | custom-call | flops 3221225472 | bytes 7340032 | tf_op jit(solution)/shard_map/front/pallas_call | solution.py:115
  26.2 14.2 %attend.1 = (bf16[1024,512]{1,0:T(8,128)(2,1)S(1)}, f32[4,8,1024]{2,1,0:T(8,128)S(1)}) custom-call(bf16[1024,1536]{1,0:T(8,128)(2,1)S(1)} %get-tuple-element.67.q_ref.k_ref.v_ref, bf16[1024,1536]{1,0:T(8,128)(2,1)S(1)} %get-tuple-element.67.q_ref.k_ref.v_ref, bf16[1024,1536]{1,0:T(8,128)(2,1)S(1)} %get-tuple-element.67.q_ref.k_ref.v_ref), custom_call_target="tpu_custom_call" | custom-call | flops 4294967296 | bytes 4194304 | tf_op jit(solution)/shard_map/attend/pallas_call | solution.py:181
  43.2 4.0 middle.1
  54.4 7.5 %all-to-all-start = ((bf16[16,96,512]{2,1,0:T(8,128)(2,1)}), bf16[16,96,512]{2,1,0:T(8,128)(2,1)}, u32[]{:S(2)}, u32[]{:S(2)}) async-start(bf16[16,96,512]{2,1,0:T(8,128)(2,1)} %bitcast.49), calls=%async_computation | async-start | bytes 3145728 | tf_op jit(solution)/shard_map/all_to_all | solution.py:1003
  64.6 48.3 %dense_branch.1 = (bf16[1024,1024]{1,0:T(8,128)(2,1)}, bf16[1024,1024]{1,0:T(8,128)(2,1)}, f32[128,1024]{1,0:T(8,128)}, f32[1024,128]{1,0:T(8,128)}, bf16[1024,2...) custom-call(s32[1]{0:T(128)} %bitcast.node_ref, s32[16]{0:T(128)} %fusion.14.order_ref, bf16[1024,1024]{1,0:T(8,128)(2,1)} %copy-done.26, ...), custom_call_target="tpu_custom_call" | custom-call | flops 25769803776 | bytes 33554432 | tf_op jit(solution)/shard_map/dense_branch/pallas_call | solution.py:668
  113.4 3.2 collective-permute-done.4.refs_3_
  118.9 45.9 %expert_branch.1 = (bf16[1536,512]{1,0:T(8,128)(2,1)}, bf16[1536,512]{1,0:T(8,128)(2,1)}, bf16[1536,512]{1,0:T(8,128)(2,1)}, bf16[1536,512]{1,0:T(8,128)(2,1)}, ...) custom-call(s32[1]{0:T(128)} %bitcast.node_ref, ...), custom_call_target="tpu_custom_call" | custom-call | flops 25769803776 | bytes 37748736 | tf_op jit(solution)/shard_map/expert_branch/pallas_call | solution.py:668
  168.5 3.1 add_convert_fusion.4
  171.6 7.0 %all-to-all-start.3 = ((bf16[16,96,512]{2,1,0:T(8,128)(2,1)}), bf16[16,96,512]{2,1,0:T(8,128)(2,1)}, u32[]{:S(2)}, u32[]{:S(2)}) async-start(bf16[16,96,512]{2,1,0:T(8,128)(2,1)} %bitcast.61), calls=%async_computation.3 | async-start | bytes 3145728 | tf_op jit(solution)/shard_map/all_to_all | solution.py:1003
  184.2 2.8 copy-done.30
  187.0 10.1 %expert_down_grad.1 = f32[2048,1024]{1,0:T(8,128)} custom-call(bf16[1536,2048]{1,0:T(8,128)(2,1)S(1)} %copy-done.30, bf16[1536,1024]{1,0:T(8,128)(2,1)S(1)} %copy-done.33), custom_call_target="tpu_custom_call" | custom-call | flops 6442450944 | bytes 14680064 | tf_op jit(solution)/shard_map/expert_down_grad/pallas_call | solution.py:750
  197.0 31.5 %collective-permute-done.8 = bf16[1024,2048]{1,0:T(8,128)(2,1)} collective-permute-done((bf16[1024,2048]{1,0:T(8,128)(2,1)}, bf16[1024,2048]{1,0:T(8,128)(2,1)}, u32[]{:S(2)}, u32[]{:S(2)}) %collective-permute-start.8) | collective-permute-done | bytes 4194336 | tf_op jit(solution)/shard_map/ppermute | solution.py:927
  228.5 4.8 %add_convert_fusion.1 = (bf16[512,2048]{1,0:T(8,128)(2,1)}, bf16[512,2048]{1,0:T(8,128)(2,1)}) fusion(bf16[1024,2048]{1,0:T(8,128)(2,1)} %collective-permute-done.8, bf16[1024,2048]{1,0:T(8,128)(2,1)S(1)} %copy-done.35), kind=kLoop, calls=%fused_computation.1 | loop fusion | flops 8388608 | bytes 12582912 | tf_op jit(solution)/shard_map/convert_element_type | solution.py:942
  234.3 4.7 %combine.2.token_ref = bf16[1024,512]{1,0:T(8,128)(2,1)} custom-call(s32[1024,1]{1,0:T(8,128)S(1)} %copy-done.16, bf16[1536,512]{1,0:T(8,128)(2,1)} %bitcast.20.got_ref), custom_call_target="tpu_custom_call" | custom-call | flops 1610612736 | bytes 2097152 | tf_op jit(solution)/shard_map/combine/pallas_call | solution.py:474
  245.2 3.5 add_convert_fusion.3
  248.7 5.9 %all-to-all-start.2 = ((bf16[16,96,512]{2,1,0:T(8,128)(2,1)}), bf16[16,96,512]{2,1,0:T(8,128)(2,1)}, u32[]{:S(2)}, u32[]{:S(2)}) async-start(bf16[16,96,512]{2,1,0:T(8,128)(2,1)} %bitcast.60), calls=%async_computation.2 | async-start | bytes 3145728 | tf_op jit(solution)/shard_map/all_to_all | solution.py:1003
  260.5 11.6 %middle_back.1 = (f32[1024,1024]{1,0:T(8,128)S(1)}, bf16[1024,512]{1,0:T(8,128)(2,1)S(1)}, f32[8,1024]{1,0:T(8,128)S(1)}, bf16[256,1024]{1,0:T(8,128)(2,1)S(1)}, bf16[256,1024]{1,0:T(8,128)(2,1)}) custom-call(s32[1]{0:T(128)} %bitcast.node_ref, s32[16]{0:T(128)S(1)} %copy-done.22, bf16[1024,1024]{1,0:T(8,128)(2,1)} %get-tuple-element.83.dense_ref, ...), custom_call_target="tpu_custom_call" | custom-call | flops 2147483648 | bytes 18874368 | tf_op jit(solution)/shard_map/middle_back/pallas_call | solution.py:388
  274.4 18.3 %attend_back.1 = (bf16[1024,512]{1,0:T(8,128)(2,1)S(1)}, bf16[1024,512]{1,0:T(8,128)(2,1)S(1)}, bf16[1024,512]{1,0:T(8,128)(2,1)S(1)}) custom-call(bf16[1024,1536]{1,0:T(8,128)(2,1)S(1)} %copy-done.28, bf16[1024,1536]{1,0:T(8,128)(2,1)S(1)} %copy-done.28, bf16[1024,1536]{1,0:T(8,128)(2,1)S(1)} %copy-done.28, bf16[1024,512]{1,0:T(8,128)(2,1)S(1)} %copy-done.15, ...), custom_call_target="tpu_custom_call" | custom-call | flops 10737418240 | bytes 8388608 | tf_op jit(solution)/shard_map/attend_back/pallas_call | solution.py:252
  292.7 18.6 %tail.1 = (f32[512,1024]{1,0:T(8,128)S(1)}, bf16[512,1024]{1,0:T(8,128)(2,1)}, bf16[512,1664]{1,0:T(8,128)(2,1)S(1)}, bf16[512,1664]{1,0:T(8,128)(2,1)}) custom-call(s32[1]{0:T(128)} %bitcast.node_ref, s32[16]{0:T(128)S(1)} %copy-done.22, bf16[1024,1024]{1,0:T(8,128)(2,1)S(1)} %copy-done.32, f32[1,1024]{1,0:T(1,128)S(1)} %bitcast.55, ...), custom_call_target="tpu_custom_call" | custom-call | flops 6442450944 | bytes 16777216 | tf_op jit(solution)/shard_map/tail/pallas_call | solution.py:849
  313.3 2.9 add_convert_fusion.10
  316.2 3.5 collective-permute-start.17
  320.5 2.8 copy-done.29
  323.3 14.3 %expert_up_grad.1 = f32[1024,2048]{1,0:T(8,128)} custom-call(s32[1]{0:T(128)} %bitcast.node_ref, bf16[1536,512]{1,0:T(8,128)(2,1)} %bitcast.12.refs_0_.own_ref, bf16[1536,512]{1,0:T(8,128)(2,1)} %collective-permute-done.3.refs_1_.other_ref, bf16[1536,2048]{1,0:T(8,128)(2,1)S(1)} %copy-done.29), custom_call_target="tpu_custom_call" | custom-call | flops 6442450944 | bytes 14680064 | tf_op jit(solution)/shard_map/expert_up_grad/pallas_call | solution.py:722
  338.6 4.0 combine.3
  347.0 4.3 %collective-permute-done.20 = bf16[128,1024]{1,0:T(8,128)(2,1)S(1)} collective-permute-done((bf16[128,1024]{1,0:T(8,128)(2,1)S(1)}, bf16[128,1024]{1,0:T(8,128)(2,1)S(1)}, u32[]{:S(2)}, u32[]{:S(2)}) %collective-permute-start.20) | collective-permute-done | bytes 262176 | tf_op jit(solution)/shard_map/ppermute | solution.py:927
  358.4 9.5 %collective-permute-done.15 = bf16[128,2048]{1,0:T(8,128)(2,1)S(1)} collective-permute-done((bf16[128,2048]{1,0:T(8,128)(2,1)S(1)}, bf16[128,2048]{1,0:T(8,128)(2,1)S(1)}, u32[]{:S(2)}, u32[]{:S(2)}) %collective-permute-start.15) | collective-permute-done | bytes 524320 | tf_op jit(solution)/shard_map/ppermute | solution.py:927
  375.9 4.7 %collective-permute-done.13 = bf16[256,1664]{1,0:T(8,128)(2,1)S(1)} collective-permute-done((bf16[256,1664]{1,0:T(8,128)(2,1)S(1)}, bf16[256,1664]{1,0:T(8,128)(2,1)S(1)}, u32[]{:S(2)}, u32[]{:S(2)}) %collective-permute-start.13) | collective-permute-done | bytes 852000 | tf_op jit(solution)/shard_map/ppermute | solution.py:927
  388.8 3.4 fusion.8
  393.0 8.9 %collective-permute-done.24 = bf16[64,1664]{1,0:T(8,128)(2,1)S(1)} collective-permute-done((bf16[64,1664]{1,0:T(8,128)(2,1)S(1)}, bf16[64,1664]{1,0:T(8,128)(2,1)S(1)}, u32[]{:S(2)}, u32[]{:S(2)}) %collective-permute-start.24) | collective-permute-done | bytes 213024 | tf_op jit(solution)/shard_map/ppermute | solution.py:927
  (193 shorter events, 80.5 us)
Async XLA Ops:
  0.7 3.1 collective-permute-start.2
  1.2 14.9 %collective-permute-start = (bf16[512,1024]{1,0:T(8,128)(2,1)}, bf16[512,1024]{1,0:T(8,128)(2,1)S(1)}, u32[]{:S(2)}, u32[]{:S(2)}) collective-permute-start(bf16[512,1024]{1,0:T(8,128)(2,1)} %bitcast.46), channel_id=1, source_target_pairs={{0,16},{16,0},{1,17},{17,1},{2,18},{18,2},{3,19},{19,3},{4,20},{20... | collective-permute-start | bytes 3145736 | tf_op jit(solution)/shard_map/ppermute | solution.py:979
  7.7 46.8 %all-to-all-start.1 = ((bf16[16,96,512]{2,1,0:T(8,128)(2,1)}), bf16[16,96,512]{2,1,0:T(8,128)(2,1)}, u32[]{:S(2)}, u32[]{:S(2)}) async-start(bf16[16,96,512]{2,1,0:T(8,128)(2,1)} %bitcast.13), calls=%async_computation.1 | async-start | bytes 3145728 | tf_op jit(solution)/shard_map/all_to_all | solution.py:1003
  40.5 2.7 collective-permute-start.1
  54.4 58.4 %all-to-all-start = ((bf16[16,96,512]{2,1,0:T(8,128)(2,1)}), bf16[16,96,512]{2,1,0:T(8,128)(2,1)}, u32[]{:S(2)}, u32[]{:S(2)}) async-start(bf16[16,96,512]{2,1,0:T(8,128)(2,1)} %bitcast.49), calls=%async_computation | async-start | bytes 3145728 | tf_op jit(solution)/shard_map/all_to_all | solution.py:1003
  112.9 3.8 collective-permute-start.4
  112.9 6.0 %collective-permute-start.3 = (bf16[1536,512]{1,0:T(8,128)(2,1)}, bf16[1536,512]{1,0:T(8,128)(2,1)}, u32[]{:S(2)}, u32[]{:S(2)}) collective-permute-start(bf16[1536,512]{1,0:T(8,128)(2,1)} %bitcast.12.refs_0_.own_ref), channel_id=1, source_target_pairs={{0,16},{16,0},{1,17},{17,1},{2,18},{18,2},{3,19},{19,3},{4,20},{20... | collective-permute-start | bytes 4718600 | tf_op jit(solution)/shard_map/ppermute | solution.py:979
  164.8 3.7 collective-permute-start.5
  165.0 63.6 %collective-permute-start.8 = (bf16[1024,2048]{1,0:T(8,128)(2,1)}, bf16[1024,2048]{1,0:T(8,128)(2,1)}, u32[]{:S(2)}, u32[]{:S(2)}) collective-permute-start(bf16[1024,2048]{1,0:T(8,128)(2,1)} %get-tuple-element.85), channel_id=1, source_target_pairs={{0,1},{1,0},{2,3},{3,2},{4,5},{5,4},{6,7},{7,6},{8,9},{9,8},{10,11... | collective-permute-start | bytes 12582920 | tf_op jit(solution)/shard_map/ppermute | solution.py:927
  171.6 61.7 %all-to-all-start.3 = ((bf16[16,96,512]{2,1,0:T(8,128)(2,1)}), bf16[16,96,512]{2,1,0:T(8,128)(2,1)}, u32[]{:S(2)}, u32[]{:S(2)}) async-start(bf16[16,96,512]{2,1,0:T(8,128)(2,1)} %bitcast.61), calls=%async_computation.3 | async-start | bytes 3145728 | tf_op jit(solution)/shard_map/all_to_all | solution.py:1003
  183.7 70.9 %collective-permute-start.7 = (bf16[1024,1024]{1,0:T(8,128)(2,1)}, bf16[1024,1024]{1,0:T(8,128)(2,1)}, u32[]{:S(2)}, u32[]{:S(2)}) collective-permute-start(bf16[1024,1024]{1,0:T(8,128)(2,1)} %get-tuple-element.83.dense_ref), channel_id=1, source_target_pairs={{0,16},{16,0},{1,17},{17,1},{2,18},{18,2},{3,19},{19,3},{4,20},{20... | collective-permute-start | bytes 6291464 | tf_op jit(solution)/shard_map/ppermute | solution.py:979
  183.7 61.5 %collective-permute-start.6 = (bf16[1536,512]{1,0:T(8,128)(2,1)}, bf16[1536,512]{1,0:T(8,128)(2,1)}, u32[]{:S(2)}, u32[]{:S(2)}) collective-permute-start(bf16[1536,512]{1,0:T(8,128)(2,1)} %get-tuple-element.79), channel_id=1, source_target_pairs={{0,16},{16,0},{1,17},{17,1},{2,18},{18,2},{3,19},{19,3},{4,20},{20... | collective-permute-start | bytes 4718600 | tf_op jit(solution)/shard_map/ppermute | solution.py:979
  187.0 41.6 %copy-start.35 = (bf16[1024,2048]{1,0:T(8,128)(2,1)S(1)}, bf16[1024,2048]{1,0:T(8,128)(2,1)}, u32[]{:S(2)}) copy-start(bf16[1024,2048]{1,0:T(8,128)(2,1)} %get-tuple-element.84) | copy-start | bytes 12582916
  239.1 15.6 %collective-permute-start.9 = (bf16[1024,512]{1,0:T(8,128)(2,1)}, bf16[1024,512]{1,0:T(8,128)(2,1)}, u32[]{:S(2)}, u32[]{:S(2)}) collective-permute-start(bf16[1024,512]{1,0:T(8,128)(2,1)} %combine.2.token_ref), channel_id=1, source_target_pairs={{0,16},{16,0},{1,17},{17,1},{2,18},{18,2},{3,19},{19,3},{4,20},{20... | collective-permute-start | bytes 3145736 | tf_op jit(solution)/shard_map/ppermute | solution.py:979
  243.1 70.2 %collective-permute-start.14 = (bf16[512,2048]{1,0:T(8,128)(2,1)}, bf16[512,2048]{1,0:T(8,128)(2,1)}, u32[]{:S(2)}, u32[]{:S(2)}) collective-permute-start(bf16[512,2048]{1,0:T(8,128)(2,1)} %get-tuple-element.124), channel_id=1, source_target_pairs={{0,2},{1,3},{2,0},{3,1},{4,6},{5,7},{6,4},{7,5},{8,10},{9,11},{10,... | collective-permute-start | bytes 6291464 | tf_op jit(solution)/shard_map/ppermute | solution.py:927
  248.7 88.9 %all-to-all-start.2 = ((bf16[16,96,512]{2,1,0:T(8,128)(2,1)}), bf16[16,96,512]{2,1,0:T(8,128)(2,1)}, u32[]{:S(2)}, u32[]{:S(2)}) async-start(bf16[16,96,512]{2,1,0:T(8,128)(2,1)} %bitcast.60), calls=%async_computation.2 | async-start | bytes 3145728 | tf_op jit(solution)/shard_map/all_to_all | solution.py:1003
  311.3 41.1 %collective-permute-start.11 = (bf16[512,1664]{1,0:T(8,128)(2,1)}, bf16[512,1664]{1,0:T(8,128)(2,1)}, u32[]{:S(2)}, u32[]{:S(2)}) collective-permute-start(bf16[512,1664]{1,0:T(8,128)(2,1)} %get-tuple-element.101), channel_id=1, source_target_pairs={{0,1},{1,0},{2,3},{3,2},{4,5},{5,4},{6,7},{7,6},{8,9},{9,8},{10,11... | collective-permute-start | bytes 5111816 | tf_op jit(solution)/shard_map/ppermute | solution.py:927
  313.3 70.2 %collective-permute-start.12 = (bf16[512,1024]{1,0:T(8,128)(2,1)}, bf16[512,1024]{1,0:T(8,128)(2,1)}, u32[]{:S(2)}, u32[]{:S(2)}) collective-permute-start(bf16[512,1024]{1,0:T(8,128)(2,1)} %get-tuple-element.105), channel_id=1, source_target_pairs={{0,16},{16,0},{1,17},{17,1},{2,18},{18,2},{3,19},{19,3},{4,20},{20... | collective-permute-start | bytes 3145736 | tf_op jit(solution)/shard_map/ppermute | solution.py:979
  316.2 38.3 %collective-permute-start.17 = (bf16[128,2048]{1,0:T(8,128)(2,1)}, bf16[128,2048]{1,0:T(8,128)(2,1)}, u32[]{:S(2)}, u32[]{:S(2)}) collective-permute-start(bf16[128,2048]{1,0:T(8,128)(2,1)} %get-tuple-element.127), channel_id=1, source_target_pairs={{0,12},{1,13},{2,14},{3,15},{4,0},{5,1},{6,2},{7,3},{8,4},{9,5},{1... | collective-permute-start | bytes 1572872 | tf_op jit(solution)/shard_map/ppermute | solution.py:927
  319.7 37.6 %collective-permute-start.16 = (bf16[128,2048]{1,0:T(8,128)(2,1)}, bf16[128,2048]{1,0:T(8,128)(2,1)}, u32[]{:S(2)}, u32[]{:S(2)}) collective-permute-start(bf16[128,2048]{1,0:T(8,128)(2,1)} %get-tuple-element.128), channel_id=1, source_target_pairs={{0,8},{1,9},{2,10},{3,11},{4,12},{5,13},{6,14},{7,15},{8,0},{9,1},... | collective-permute-start | bytes 1572872 | tf_op jit(solution)/shard_map/ppermute | solution.py:927
  319.7 23.1 %collective-permute-start.19 = (bf16[256,1024]{1,0:T(8,128)(2,1)}, bf16[256,1024]{1,0:T(8,128)(2,1)}, u32[]{:S(2)}, u32[]{:S(2)}) collective-permute-start(bf16[256,1024]{1,0:T(8,128)(2,1)} %get-tuple-element.113), channel_id=1, source_target_pairs={{0,1},{1,0},{2,3},{3,2},{4,5},{5,4},{6,7},{7,6},{8,9},{9,8},{10,11... | collective-permute-start | bytes 1572872 | tf_op jit(solution)/shard_map/ppermute | solution.py:927
  344.8 6.4 %collective-permute-start.20 = (bf16[128,1024]{1,0:T(8,128)(2,1)S(1)}, bf16[128,1024]{1,0:T(8,128)(2,1)S(1)}, u32[]{:S(2)}, u32[]{:S(2)}) collective-permute-start(bf16[128,1024]{1,0:T(8,128)(2,1)S(1)} %get-tuple-element.137), channel_id=1, source_target_pairs={{0,2},{1,3},{2,0},{3,1},{4,6},{5,7},{6,4},{7,5},{8,10},{9,11},{10,... | collective-permute-start | bytes 786440 | tf_op jit(solution)/shard_map/ppermute | solution.py:927
  351.3 16.6 %collective-permute-start.15 = (bf16[128,2048]{1,0:T(8,128)(2,1)S(1)}, bf16[128,2048]{1,0:T(8,128)(2,1)S(1)}, u32[]{:S(2)}, u32[]{:S(2)}) collective-permute-start(bf16[128,2048]{1,0:T(8,128)(2,1)S(1)} %copy-done.37), channel_id=1, source_target_pairs={{0,4},{1,5},{2,6},{3,7},{4,8},{5,9},{6,10},{7,11},{8,12},{9,13},{1... | collective-permute-start | bytes 1572872 | tf_op jit(solution)/shard_map/ppermute | solution.py:927
  352.4 18.2 %collective-permute-start.10 = (bf16[512,1024]{1,0:T(8,128)(2,1)S(1)}, bf16[512,1024]{1,0:T(8,128)(2,1)S(1)}, u32[]{:S(2)}, u32[]{:S(2)}) collective-permute-start(bf16[512,1024]{1,0:T(8,128)(2,1)S(1)} %constant_dynamic-slice_fusion.2), channel_id=1, source_target_pairs={{0,16},{16,0},{1,17},{17,1},{2,18},{18,2},{3,19},{19,3},{4,20},{20... | collective-permute-start | bytes 3145736 | tf_op jit(solution)/shard_map/ppermute | solution.py:979
  354.5 30.3 %collective-permute-start.23 = (bf16[32,1024]{1,0:T(8,128)(2,1)S(1)}, bf16[32,1024]{1,0:T(8,128)(2,1)S(1)}, u32[]{:S(2)}, u32[]{:S(2)}) collective-permute-start(bf16[32,1024]{1,0:T(8,128)(2,1)S(1)} %get-tuple-element.140), channel_id=1, source_target_pairs={{0,12},{1,13},{2,14},{3,15},{4,0},{5,1},{6,2},{7,3},{8,4},{9,5},{1... | collective-permute-start | bytes 196616 | tf_op jit(solution)/shard_map/ppermute | solution.py:927
  357.3 29.5 %collective-permute-start.22 = (bf16[32,1024]{1,0:T(8,128)(2,1)S(1)}, bf16[32,1024]{1,0:T(8,128)(2,1)S(1)}, u32[]{:S(2)}, u32[]{:S(2)}) collective-permute-start(bf16[32,1024]{1,0:T(8,128)(2,1)S(1)} %get-tuple-element.141), channel_id=1, source_target_pairs={{0,8},{1,9},{2,10},{3,11},{4,12},{5,13},{6,14},{7,15},{8,0},{9,1},... | collective-permute-start | bytes 196616 | tf_op jit(solution)/shard_map/ppermute | solution.py:927
  367.9 12.7 %collective-permute-start.13 = (bf16[256,1664]{1,0:T(8,128)(2,1)S(1)}, bf16[256,1664]{1,0:T(8,128)(2,1)S(1)}, u32[]{:S(2)}, u32[]{:S(2)}) collective-permute-start(bf16[256,1664]{1,0:T(8,128)(2,1)S(1)} %get-tuple-element.129), channel_id=1, source_target_pairs={{0,2},{1,3},{2,0},{3,1},{4,6},{5,7},{6,4},{7,5},{8,10},{9,11},{10,... | collective-permute-start | bytes 2555912 | tf_op jit(solution)/shard_map/ppermute | solution.py:927
  370.7 16.1 %collective-permute-start.21 = (bf16[32,1024]{1,0:T(8,128)(2,1)S(1)}, bf16[32,1024]{1,0:T(8,128)(2,1)S(1)}, u32[]{:S(2)}, u32[]{:S(2)}) collective-permute-start(bf16[32,1024]{1,0:T(8,128)(2,1)S(1)} %get-tuple-element.139), channel_id=1, source_target_pairs={{0,4},{1,5},{2,6},{3,7},{4,8},{5,9},{6,10},{7,11},{8,12},{9,13},{1... | collective-permute-start | bytes 196616 | tf_op jit(solution)/shard_map/ppermute | solution.py:927
  380.9 12.1 %collective-permute-start.25 = (bf16[64,1664]{1,0:T(8,128)(2,1)S(1)}, bf16[64,1664]{1,0:T(8,128)(2,1)S(1)}, u32[]{:S(2)}, u32[]{:S(2)}) collective-permute-start(bf16[64,1664]{1,0:T(8,128)(2,1)S(1)} %get-tuple-element.131), channel_id=1, source_target_pairs={{0,12},{1,13},{2,14},{3,15},{4,0},{5,1},{6,2},{7,3},{8,4},{9,5},{1... | collective-permute-start | bytes 638984 | tf_op jit(solution)/shard_map/ppermute | solution.py:927
  383.5 18.4 %collective-permute-start.24 = (bf16[64,1664]{1,0:T(8,128)(2,1)S(1)}, bf16[64,1664]{1,0:T(8,128)(2,1)S(1)}, u32[]{:S(2)}, u32[]{:S(2)}) collective-permute-start(bf16[64,1664]{1,0:T(8,128)(2,1)S(1)} %get-tuple-element.132), channel_id=1, source_target_pairs={{0,8},{1,9},{2,10},{3,11},{4,12},{5,13},{6,14},{7,15},{8,0},{9,1},... | collective-permute-start | bytes 638984 | tf_op jit(solution)/shard_map/ppermute | solution.py:927
  384.8 17.1 %collective-permute-start.18 = (bf16[64,1664]{1,0:T(8,128)(2,1)S(1)}, bf16[64,1664]{1,0:T(8,128)(2,1)S(1)}, u32[]{:S(2)}, u32[]{:S(2)}) collective-permute-start(bf16[64,1664]{1,0:T(8,128)(2,1)S(1)} %get-tuple-element.133), channel_id=1, source_target_pairs={{0,4},{1,5},{2,6},{3,7},{4,8},{5,9},{6,10},{7,11},{8,12},{9,13},{1... | collective-permute-start | bytes 638984 | tf_op jit(solution)/shard_map/ppermute | solution.py:927
  402.3 1.8 collective-permute-start.26
  (44 other events, 368.1 us)

commit v5 on v4

--- a/solution.py
+++ b/solution.py
@@ -78,15 +78,22 @@
     return jnp.where(index == node, own, other)
 
 
-def permutation(order_ref, start, count, block, columns, copies=1):
+def permutation(order, start, count, block, columns, copies=1):
     lane = lax.broadcasted_iota(jnp.int32, (block, columns), 1)
     row = lax.broadcasted_iota(jnp.int32, (block, columns), 0)
     pieces = []
     for index in range(count // block):
         place = start // block + index
-        first = order_ref[place // copies] * block + (place % copies) * (columns // copies)
+        first = order(place // copies) * block + (place % copies) * (columns // copies)
         pieces.append((row + first == lane).astype(F32))
     return jnp.concatenate(pieces, axis=0).astype(BF16)
+
+
+def half_rows(shape, steps):
+    return [
+        spec(shape, lambda i, n, at=at: (jnp.clip(i - abs(at - n[0]) * steps, 0, steps - 1), 0))
+        for at in range(2)
+    ]
 
 
 def front_kernel(node_ref, own_ref, other_ref, gain_ref, w_ref, qkv_ref, normed_ref):
@@ -201,7 +208,7 @@
 
 
 def attend_back_kernel(
-    q_ref, k_ref, v_ref, out_ref, grad_ref, lse_ref, dq_ref, dk_ref, dv_ref, dqt_ref, dka_ref, dva_ref
+    q_ref, k_ref, v_ref, out_ref, grad_ref, lse_ref, packed_ref, dqt_ref, dka_ref, dva_ref
 ):
     seq = q_ref.shape[0]
     scale = HEAD_DIM ** (-0.5)
@@ -240,9 +247,9 @@
                 part = dot(k_t[rows, start:stop], score_grad)
                 acc = part if acc is None else acc + part
             dqt_ref[rows, lo:hi] = acc
-    dq_ref[...] = (dqt_ref[...].T * scale).astype(BF16)
-    dk_ref[...] = (dka_ref[...] * scale).astype(BF16)
-    dv_ref[...] = dva_ref[...].astype(BF16)
+    packed_ref[0] = (dqt_ref[...].T * scale).astype(BF16)
+    packed_ref[1] = (dka_ref[...] * scale).astype(BF16)
+    packed_ref[2] = dva_ref[...].astype(BF16)
 
 
 def attend_back(qkv, attended, grad, lse):
@@ -253,8 +260,8 @@
         attend_back_kernel,
         grid=(pairs,),
         in_specs=head_specs(seq, pairs) + [one, one, spec((1, 8, seq), lambda j: (j, 0, 0))],
-        out_specs=[one] * 3,
-        out_shape=[struct(attended.shape, BF16)] * 3,
+        out_specs=spec((3, seq, LANES), lambda j: (0, 0, j)),
+        out_shape=struct((3, *attended.shape), BF16),
         scratch_shapes=[
             pltpu.VMEM((LANES, seq), F32),
             pltpu.VMEM((seq, LANES), F32),
@@ -271,58 +278,94 @@
 
 
 def middle_kernel(
-    node_ref, tok_ref, tok_other_ref, own_ref, other_ref, w_ref, gain_ref, hidden_ref, normed_ref
+    row_steps,
+    node_ref,
+    tok_ref,
+    tok_other_ref,
+    own_ref,
+    other_ref,
+    w_ref,
+    gain_ref,
+    place_ref,
+    hidden_ref,
+    normed_ref,
+    sent_ref,
+    half_ref,
 ):
-    half = own_ref.shape[1]
+    rows, half = own_ref.shape
     node = node_ref[0]
-    index = pl.program_id(0) // (pl.num_programs(0) // 2)
-    tok = row_pick(node, index, tok_ref[...], tok_other_ref[...])
+    step = pl.program_id(0)
     mine = pl.ds(pl.multiple_of(node * half, half), half)
     theirs = pl.ds(pl.multiple_of((1 - node) * half, half), half)
-    hidden = tok.astype(F32) + (
-        dot(own_ref[...], w_ref[mine, :]) + dot(other_ref[...], w_ref[theirs, :])
-    )
-    normed, _, _ = layer_norm(hidden, gain_ref[...])
-    hidden_ref[...] = hidden
-    normed_ref[...] = normed.astype(BF16)
-
-
-def middle(node, tokens, tokens_other, own, other, w_out, gain):
+
+    @pl.when(step < row_steps)
+    def _():
+        tok = row_pick(node, step // (row_steps // 2), tok_ref[...], tok_other_ref[...])
+        hidden = tok.astype(F32) + (
+            dot(own_ref[...], w_ref[mine, :]) + dot(other_ref[...], w_ref[theirs, :])
+        )
+        normed, _, _ = layer_norm(hidden, gain_ref[...])
+        hidden_ref[...] = hidden
+        normed_ref[...] = normed.astype(BF16)
+        half_ref[pl.ds(pl.multiple_of(step * rows, rows), rows), :] = normed_ref[:, mine]
+
+    @pl.when(step >= row_steps)
+    def _():
+        size = sent_ref.shape[0]
+        first = (step - row_steps) * size
+        slot = first + lax.broadcasted_iota(jnp.int32, (size, 1), 0)
+        onehot = (place_ref[...] == slot).astype(F32).astype(BF16)
+        sent_ref[...] = dot(onehot, half_ref[...]).astype(BF16)
+
+
+def middle(node, tokens, tokens_other, own, other, w_out, gain, place, slots):
     width = tokens.shape[1]
     seq = 2 * tokens.shape[0]
     rows = 256
+    size = 512
     steps = seq // rows
-    half_row = spec((rows, width), lambda i, n: (i % (steps // 2), 0))
-    row = lambda columns: spec((rows, columns), lambda i, n: (i, 0))
+    mine, theirs = half_rows((rows, width), steps // 2)
+    row = lambda columns: spec((rows, columns), lambda i, n: (jnp.minimum(i, steps - 1), 0))
     return pl.pallas_call(
-        middle_kernel,
+        functools.partial(middle_kernel, steps),
         grid_spec=pltpu.PrefetchScalarGridSpec(
             num_scalar_prefetch=1,
-            grid=(seq // rows,),
+            grid=(steps + slots // size,),
             in_specs=[
-                half_row,
-                half_row,
+                mine,
+                theirs,
                 row(width // 2),
                 row(width // 2),
                 fixed(w_out.shape),
                 fixed((1, width)),
+                fixed(place.shape),
             ],
-            out_specs=[row(width), row(width)],
-        ),
-        out_shape=[struct((seq, width), F32), struct((seq, width), BF16)],
+            out_specs=[
+                row(width),
+                row(width),
+                spec((size, width // 2), lambda i, n: (jnp.maximum(i - steps, 0), 0)),
+            ],
+            scratch_shapes=[pltpu.VMEM((seq, width // 2), BF16)],
+        ),
+        out_shape=[
+            struct((seq, width), F32),
+            struct((seq, width), BF16),
+            struct((slots, width // 2), BF16),
+        ],
         cost_estimate=pl.CostEstimate(
-            flops=2 * seq * width * width, bytes_accessed=12 * seq * width, transcendentals=0
-        ),
-        compiler_params=pltpu.CompilerParams(vmem_limit_bytes=20 << 20),
+            flops=2 * seq * width * width + seq * slots * width,
+            bytes_accessed=12 * seq * width,
+            transcendentals=0,
+        ),
+        compiler_params=pltpu.CompilerParams(vmem_limit_bytes=24 << 20),
         name="middle",
-    )(node, tokens, tokens_other, own, other, w_out, gain[None])
+    )(node, tokens, tokens_other, own, other, w_out, gain[None], place)
 
 
 def middle_back_kernel(
     parts,
-    block,
+    grid,
     node_ref,
-    order_ref,
     dense_ref,
     dense_other_ref,
     token_ref,
@@ -339,7 +382,7 @@
     *refs,
 ):
     weight_refs = refs[:parts]
-    inner_ref, acc_ref = refs[parts:]
+    inner_ref, acc_ref, turn_ref = refs[parts:]
     half = token_ref.shape[1]
     node = node_ref[0]
     step = pl.program_id(0)
@@ -348,6 +391,8 @@
     def _():
         ln_ref[...] = jnp.zeros_like(ln_ref)
         acc_ref[...] = jnp.zeros_like(acc_ref)
+        order = functools.partial(grid.place, node_ref[0], node_ref[1])
+        turn_ref[...] = permutation(order, 0, half, half // grid.members, half)
 
     inner_ref[...] = dense_ref[...].astype(F32) + dense_other_ref[...].astype(F32)
     inner_ref[:, pl.ds(pl.multiple_of(node * half, half), half)] += token_ref[...].astype(F32)
@@ -361,11 +406,14 @@
     index = step // (pl.num_programs(0) // 2)
     cot = row_pick(node, index, cot_ref[...], cot_other_ref[...])
     hidden_grad = cot.astype(F32) + norm_backward(inner, base, inverse, gain)
-    grad_ref[...] = hidden_grad
+
+    @pl.when(index == node)
+    def _():
+        grad_ref[...] = hidden_grad
+
     low = hidden_grad.astype(BF16)
     attended_grad_ref[...] = dot_t(low, w_ref[...]).astype(BF16)
-    turn = permutation(order_ref, 0, half, block, half)
-    turned = dot_t(turn, attended_ref[...]).astype(BF16)
+    turned = dot_t(turn_ref[...], attended_ref[...]).astype(BF16)
     acc_ref[...] += dot(turned, low)
 
     @pl.when(step == pl.num_programs(0) - 1)
@@ -376,19 +424,19 @@
 
 
 def middle_back(
-    node, order, dense, dense_other, token, token_other, hidden, cot, cot_other, attended, gain, w_out, parts
+    node, grid, dense, dense_other, token, token_other, hidden, cot, cot_other, attended, gain, w_out, parts
 ):
     seq, width = hidden.shape
     half = width // 2
     rows = 256
     steps = seq // rows
-    half_row = spec((rows, width), lambda i, n, o: (i % (steps // 2), 0))
-    row = lambda columns: spec((rows, columns), lambda i, n, o: (i, 0))
+    mine, theirs = half_rows((rows, width), steps // 2)
+    row = lambda columns: spec((rows, columns), lambda i, n: (i, 0))
     result = (half // parts, width)
     return pl.pallas_call(
-        functools.partial(middle_back_kernel, parts, half // order.shape[0]),
+        functools.partial(middle_back_kernel, parts, grid),
         grid_spec=pltpu.PrefetchScalarGridSpec(
-            num_scalar_prefetch=2,
+            num_scalar_prefetch=1,
             grid=(seq // rows,),
             in_specs=[
                 row(width),
@@ -396,17 +444,21 @@
                 row(half),
                 row(half),
                 row(width),
-                half_row,
-                half_row,
+                mine,
+                theirs,
                 row(half),
                 fixed((1, width)),
-                spec((half, width), lambda i, n, o: (n[0], 0)),
+                spec((half, width), lambda i, n: (n[0], 0)),
             ],
-            out_specs=[row(width), row(half), fixed((8, width))] + [fixed(result)] * parts,
-            scratch_shapes=[pltpu.VMEM((rows, width), F32), pltpu.VMEM((half, width), F32)],
+            out_specs=[mine, row(half), fixed((8, width))] + [fixed(result)] * parts,
+            scratch_shapes=[
+                pltpu.VMEM((rows, width), F32),
+                pltpu.VMEM((half, width), F32),
+                pltpu.VMEM((half, half), BF16),
+            ],
         ),
         out_shape=[
-            struct((seq, width), F32),
+            struct((seq // 2, width), F32),
             struct((seq, half), BF16),
             struct((8, width), F32),
         ]
@@ -414,10 +466,10 @@
         cost_estimate=pl.CostEstimate(
             flops=2 * seq * width * width, bytes_accessed=18 * seq * width, transcendentals=0
         ),
-        compiler_params=pltpu.CompilerParams(vmem_limit_bytes=28 << 20),
+        compiler_params=pltpu.CompilerParams(vmem_limit_bytes=LIMIT),
         name="middle_back",
     )(
-        node, order, dense, dense_other, token, token_other, hidden, cot, cot_other, attended,
+        node, dense, dense_other, token, token_other, hidden, cot, cot_other, attended,
         gain[None], w_out,
     )
 
@@ -438,18 +490,13 @@
     rows = place.shape[1]
     half = own.shape[1] // 2
     size = 256
-    if own.shape[0] == rows:
-        first = spec((rows, half), lambda i, n: (0, n[0]))
-        second = first
-    else:
-        first = spec((rows, half), lambda i, n: (n[0], n[0]))
-        second = spec((rows, half), lambda i, n: (1 - n[0], n[0]))
+    column = spec((rows, half), lambda i, n: (0, n[0]))
     return pl.pallas_call(
         dispatch_kernel,
         grid_spec=pltpu.PrefetchScalarGridSpec(
             num_scalar_prefetch=1,
             grid=(slots // size,),
-            in_specs=[fixed(place.shape), first, second],
+            in_specs=[fixed(place.shape), column, column],
             out_specs=spec((size, half), lambda i, n: (i, 0)),
         ),
         out_shape=struct((slots, half), BF16),
@@ -487,9 +534,56 @@
     )(place, got)
 
 
-def branch_kernel(dense, experts, parts, unit, node_ref, order_ref, *refs):
+def combine_out_kernel(node_ref, place_ref, got_ref, dense_ref, share_ref, out_ref, sum_ref):
+    size = place_ref.shape[0]
+    half = got_ref.shape[1]
+    node = node_ref[0]
+    slot = lax.broadcasted_iota(jnp.int32, (size, got_ref.shape[0]), 1)
+    onehot = (place_ref[...] == slot).astype(F32).astype(BF16)
+    sum_ref[...] = dense_ref[...].astype(F32)
+    sum_ref[:, pl.ds(pl.multiple_of(node * half, half), half)] += share_ref[:, 0:1] * dot(
+        onehot, got_ref[...]
+    )
+    out_ref[...] = sum_ref[...].astype(BF16)
+
+
+def combine_out(node, place, got, dense, share):
+    rows, width = dense.shape
+    size = 256
+    steps = rows // size
+
+    def chunk(i, n):
+        mine = i // (steps // 2) == 0
+        return (jnp.where(mine, n[0], 1 - n[0]) * (steps // 2) + i % (steps // 2), 0)
+
+    return pl.pallas_call(
+        combine_out_kernel,
+        grid_spec=pltpu.PrefetchScalarGridSpec(
+            num_scalar_prefetch=1,
+            grid=(steps,),
+            in_specs=[
+                spec((size, 1), chunk),
+                fixed(got.shape),
+                spec((size, width), chunk),
+                spec((size, LANES), chunk),
+            ],
+            out_specs=spec((size, width), lambda i, n: (i, 0)),
+            scratch_shapes=[pltpu.VMEM((size, width), F32)],
+        ),
+        out_shape=struct((rows, width), BF16),
+        cost_estimate=pl.CostEstimate(
+            flops=2 * rows * got.shape[0] * got.shape[1],
+            bytes_accessed=4 * rows * width,
+            transcendentals=0,
+        ),
+        compiler_params=pltpu.CompilerParams(vmem_limit_bytes=20 << 20),
+        name="combine_out",
+    )(node, place, got, dense, share)
+
+
+def branch_kernel(dense, experts, parts, layout, node_ref, *refs):
     if dense:
-        x_refs, c_refs, refs = refs[:1], refs[1:3], refs[3:]
+        x_refs, c_refs, route_ref, refs = refs[:1], refs[1:3], refs[3], refs[4:]
     else:
         x_refs, c_refs, refs = refs[:2], refs[2:4], refs[4:]
     side_ref, wct_ref, up_ref, dn_ref = refs[:4]
@@ -507,8 +601,10 @@
     step = pl.program_id(0)
     small = 256
     big = 512
+    unit = width // layout.members
     node = node_ref[0]
     if dense:
+        order = functools.partial(layout.place, node, node_ref[1])
         split = [slice(0, width)]
     else:
         split = [
@@ -536,7 +632,10 @@
             mix = soft(is_mix)
             if dense:
                 factor = jnp.sum(mix * first, axis=1, keepdims=True)
-                probs_ref[at, :] = jnp.where(is_router, soft(is_router), mix)
+                chosen = lane == route_ref[at, :]
+                gate = jnp.sum(jnp.where(chosen, soft(is_router), 0.0), axis=1, keepdims=True)
+                share = gate * jnp.sum(mix * second, axis=1, keepdims=True)
+                probs_ref[at, :] = jnp.where(lane == 0, share, factor)
                 a_ref[at, :] = jnp.where(is_mix, first - mix, 0.0)
             else:
                 router = soft(is_router)
@@ -562,7 +661,7 @@
         if dense:
 
             def transpose(at):
-                turn = permutation(order_ref, at.start, small, unit, width)
+                turn = permutation(order, at.start, small, unit, width)
                 for index in range(rows // big):
                     some = slice(index * big, (index + 1) * big)
                     xt_ref[at, some] = dot_t(turn, x_refs[0][some, :]).astype(BF16)
@@ -620,11 +719,7 @@
                 gsm_ref[:, split[n]] += dot(turned, x_refs[n][at, :])
                 part = acc_ref[at, split[n]]
                 if dense:
-                    mixes = probs_ref[at, :]
-                    lane = lax.broadcasted_iota(jnp.int32, (1, LANES), 1)
-                    part = part * jnp.sum(
-                        jnp.where(lane == experts, mixes, 0.0), axis=1, keepdims=True
-                    )
+                    part = part * probs_ref[at, 1:2]
                 out_refs[n][at, :] = part.astype(BF16)
                 dx_refs[n][at, :] = (dxa_ref[at, split[n]] + dot(low, wct_ref[:, split[n]])).astype(
                     BF16
@@ -633,15 +728,15 @@
         chunks(rows, small, finish)
 
 
-def branch(node, order, xs, cs, side, head_t, up, down, experts, parts):
+def branch(node, layout, xs, cs, side, head_t, up, down, experts, parts):
     dense = len(xs) == 1
     rows, half = xs[0].shape
     width = len(xs) * half
     hidden = up.shape[1]
     block = 512
-    column = lambda size: spec((size, block), lambda f, n, o: (0, f))
+    column = lambda size: spec((size, block), lambda f, n: (0, f))
     up_spec = column(width)
-    down_spec = up_spec if dense else spec((block, width), lambda f, n, o: (f, 0))
+    down_spec = up_spec if dense else spec((block, width), lambda f, n: (f, 0))
     outs = [(fixed((rows, half)), struct((rows, half), BF16))] * (2 * len(xs))
     outs = outs + [(fixed((LANES, width)), struct((LANES, width), F32))]
     sums = [
@@ -666,9 +761,9 @@
         outs = outs + [(column(rows), struct((rows, hidden), BF16))] * 2
         scratch = sums
     return pl.pallas_call(
-        functools.partial(branch_kernel, dense, experts, parts, width // order.shape[0]),
+        functools.partial(branch_kernel, dense, experts, parts, layout),
         grid_spec=pltpu.PrefetchScalarGridSpec(
-            num_scalar_prefetch=2,
+            num_scalar_prefetch=1,
             grid=(hidden // block,),
             in_specs=[fixed(one.shape) for one in [*xs, *cs]]
             + [
@@ -688,7 +783,7 @@
         ),
         compiler_params=pltpu.CompilerParams(vmem_limit_bytes=LIMIT),
         name="dense_branch" if dense else "expert_branch",
-    )(node, order, *xs, *cs, side, head_t, up, down)
+    )(node, *xs, *cs, side, head_t, up, down)
 
 
 def expert_up_kernel(node_ref, own_ref, other_ref, dpre_ref, grad_ref, xt_ref):
@@ -738,7 +833,7 @@
             bytes_accessed=8 * half * hidden + 2 * rows * hidden,
             transcendentals=0,
         ),
-        compiler_params=pltpu.CompilerParams(vmem_limit_bytes=36 << 20),
+        compiler_params=pltpu.CompilerParams(vmem_limit_bytes=LIMIT),
         name="expert_up_grad",
     )(node, own, other, dpre)
 
@@ -763,58 +858,77 @@
     )(act, g)
 
 
+def turn_kernel(grid, node_ref, x_ref, out_ref):
+    rows, width = out_ref.shape[0], x_ref.shape[1]
+    order = functools.partial(grid.place, node_ref[0], node_ref[1])
+    start = pl.program_id(0) * rows
+    rows_of = permutation(order, start, rows, width // (2 * grid.members), width, 2)
+    out_ref[...] = dot_t(rows_of, x_ref[...]).astype(BF16)
+
+
+def turn(node, grid, x):
+    seq, width = x.shape
+    rows = 256
+    return pl.pallas_call(
+        functools.partial(turn_kernel, grid),
+        grid_spec=pltpu.PrefetchScalarGridSpec(
+            num_scalar_prefetch=1,
+            grid=(width // rows,),
+            in_specs=[fixed(x.shape)],
+            out_specs=spec((rows, seq), lambda i, n: (i, 0)),
+        ),
+        out_shape=struct((width, seq), BF16),
+        cost_estimate=pl.CostEstimate(
+            flops=2 * seq * width * width, bytes_accessed=4 * seq * width, transcendentals=0
+        ),
+        compiler_params=pltpu.CompilerParams(vmem_limit_bytes=16 << 20),
+        name="turn",
+    )(node, x)
+
+
 def tail_kernel(
     parts,
     ln_lane,
-    block,
+    grid,
     node_ref,
-    order_ref,
     x_ref,
+    xt_ref,
     gain_ref,
     small_ref,
-    dq_ref,
-    dk_ref,
-    dv_ref,
+    packed_ref,
     w_ref,
     keep_ref,
     send_ref,
     *refs,
 ):
     part_refs = refs[:parts]
-    xt_ref, acc_ref = refs[parts:]
+    acc_ref = refs[parts]
     seq, width = x_ref.shape
     size = width // parts
     own = keep_ref.shape[0]
+    order = functools.partial(grid.place, node_ref[0], node_ref[1])
+    block = width // (2 * grid.members)
     step = pl.program_id(0)
     last = pl.num_programs(0) - 1
 
-    @pl.when(step == 0)
+    @pl.when(step < last)
     def _():
-        def prepare(at):
-            turn = permutation(order_ref, at.start, 256, block, width, 2)
-            for index in range(seq // 512):
-                some = slice(index * 512, (index + 1) * 512)
-                xt_ref[at, some] = dot_t(turn, x_ref[some, :]).astype(BF16)
-
-        chunks(width, 256, prepare)
-
-    for which, ref in enumerate((dq_ref, dk_ref, dv_ref)):
-
-        @pl.when(step == which)
+        for part in range(parts):
+
+            def weights(at):
+                rows_at = pl.ds(pl.multiple_of(part * size + at.start, 256), 256)
+                part_refs[part][at, :] = dot(xt_ref[rows_at, :], packed_ref[0]).astype(BF16)
+
+            chunks(size, 256, weights)
+
+        @pl.when(step == 0)
         def _():
-            for part in range(parts):
-
-                def weights(at):
-                    rows_at = pl.ds(pl.multiple_of(part * size + at.start, 256), 256)
-                    part_refs[part][at, :] = dot(xt_ref[rows_at, :], ref[...]).astype(BF16)
-
-                chunks(size, 256, weights)
-
-            def back(at):
-                piece = dot_t(ref[at, :], w_ref[...])
-                acc_ref[at, :] = acc_ref[at, :] + piece if which else piece
-
-            chunks(seq, 256, back)
+            acc_ref[...] = jnp.zeros_like(acc_ref)
+
+        def back(at):
+            acc_ref[at, :] += dot_t(packed_ref[0, at, :], w_ref[...])
+
+        chunks(seq, 256, back)
 
     @pl.when(step == last)
     def _():
@@ -833,7 +947,7 @@
         for part in range(parts):
 
             def turn(at):
-                rows = permutation(order_ref, part * size + at.start, 256, block, width, 2)
+                rows = permutation(order, part * size + at.start, 256, block, width, 2)
                 part_refs[part][at, 0:LANES] = dot_t(rows, small).astype(BF16)
 
             chunks(size, 256, turn)
@@ -841,28 +955,27 @@
         send_ref[...] = acc_ref[pl.ds(pl.multiple_of((1 - node) * own, own), own), :].astype(BF16)
 
 
-def tail(node, order, normed, gain, small, dq, dk, dv, w_qkv, parts, ln_lane):
+def tail(node, grid, normed, turned, gain, small, packed, w_qkv, parts, ln_lane):
     seq, width = normed.shape
     half = width // 2
     steps = 3
     part = (width // parts, half)
     return pl.pallas_call(
-        functools.partial(tail_kernel, parts, ln_lane, half // order.shape[0]),
+        functools.partial(tail_kernel, parts, ln_lane, grid),
         grid_spec=pltpu.PrefetchScalarGridSpec(
-            num_scalar_prefetch=2,
+            num_scalar_prefetch=1,
             grid=(steps + 1,),
             in_specs=[
                 fixed(normed.shape),
+                fixed(turned.shape),
                 fixed((1, width)),
                 fixed((LANES, width)),
-                fixed((seq, half)),
-                fixed((seq, half)),
-                fixed((seq, half)),
-                spec((width, half), lambda i, n, o: (0, 2 * jnp.minimum(i, steps - 1) + n[0])),
+                spec((1, seq, half), lambda i, n: (jnp.minimum(i, steps - 1), 0, 0)),
+                spec((width, half), lambda i, n: (0, 2 * jnp.minimum(i, steps - 1) + n[0])),
             ],
             out_specs=[fixed((seq // 2, width)), fixed((seq // 2, width))]
-            + [spec(part, lambda i, n, o: (0, i))] * parts,
-            scratch_shapes=[pltpu.VMEM((width, seq), BF16), pltpu.VMEM((seq, width), F32)],
+            + [spec(part, lambda i, n: (0, i))] * parts,
+            scratch_shapes=[pltpu.VMEM((seq, width), F32)],
         ),
         out_shape=[struct((seq // 2, width), F32), struct((seq // 2, width), BF16)]
         + [struct((width // parts, steps * half + LANES), BF16)] * parts,
@@ -871,7 +984,7 @@
         ),
         compiler_params=pltpu.CompilerParams(vmem_limit_bytes=32 << 20),
         name="tail",
-    )(node, order, normed, gain[None], small, dq, dk, dv, w_qkv)
+    )(node, normed, turned, gain[None], small, packed, w_qkv)
 
 
 class Grid:
@@ -902,25 +1015,14 @@
                 pairs.append((node * self.members + member, node * self.members + target))
         return pairs
 
-    def order(self, node, member):
-        tables = []
-        for one in range(2):
-            table = []
-            for own in range(self.members):
-                base = self.digits(one, own)
-                row = []
-                for place in range(self.members):
-                    steps = (
-                        place // (self.first * self.third),
-                        (place // self.third) % self.first,
-                        place % self.third,
-                    )
-                    row.append(
-                        self.index(one, [(b + s) % k for b, s, k in zip(base, steps, self.sizes)])
-                    )
-                table.append(row)
-            tables.append(table)
-        return jnp.array(tables, jnp.int32)[node, member]
+    def place(self, node, member, place):
+        size, third = self.first, self.third
+        low, high = member % size, (member // size) % size
+        top = member // (size * size)
+        one = (jnp.where(node == 0, low, high) + place // (size * third)) % size
+        two = (jnp.where(node == 0, high, low) + (place // third) % size) % size
+        low, high = jnp.where(node == 0, one, two), jnp.where(node == 0, two, one)
+        return ((top + place % third) % third * size + high) * size + low
 
     def send(self, parts, stage):
         return [
@@ -970,10 +1072,9 @@
     slots = experts * capacity
     pairs = half // LANES
     own_start = node * own_rows
-    scalar = node.astype(jnp.int32).reshape(1)
+    scalar = jnp.stack([node, member]).astype(jnp.int32)
     grid = Grid(members)
     parts = grid.sizes[0]
-    order_of = grid.order(node, member)
 
     def swap(value):
         return lax.ppermute(value, "node", SWAP)
@@ -1011,37 +1112,39 @@
 
     qkv, normed_low = front(scalar, own_tokens, other_tokens, ln1_gain, w_qkv)
     attended_own, lse = attend(qkv, pairs)
-    hidden, inner_low = middle(
-        scalar, own_tokens, other_tokens, attended_own, swap(attended_own), w_out, ln2_gain
+    hidden, inner_low, sent_rows = middle(
+        scalar, own_tokens, other_tokens, attended_own, swap(attended_own), w_out, ln2_gain,
+        place.reshape(1, seq), slots,
     )
 
-    got_rows = exchange(dispatch_rows(scalar, place_rows, inner_low, inner_low, slots))
+    got_rows = exchange(sent_rows)
     head_t = jnp.concatenate(
         [w_router, w_mix, jnp.zeros((width, LANES - experts - 2), BF16)], axis=1
     ).T
     picked = (jnp.arange(LANES) == member).astype(F32)[None]
     results = branch(
-        scalar, order_of, [inner_low], [own_cot, other_cot], picked, head_t, w_up, w_down,
+        scalar, grid, [inner_low], [own_cot, other_cot, group_routes[:, None]], picked, head_t, w_up, w_down,
         experts, parts,
     )
-    dense_out, dense_dx, small_dense, probs = results[:4]
+    dense_out, dense_dx, small_dense, share = results[:4]
     pair0 = results[4:]
     came = grid.send(pair0, 0)
     got_rows = after(got_rows, small_dense)
     expert_rows = [got_rows, swap(got_rows)]
     out_keep, out_send, dx_keep, dx_send, small_expert, expert_g, expert_act, expert_dpre = branch(
-        scalar, order_of, expert_rows, [got_cot, swap(got_cot)], picked, head_t, expert_up[0],
+        scalar, grid, expert_rows, [got_cot, swap(got_cot)], picked, head_t, expert_up[0],
         expert_down[0], experts, parts,
     )
 
     sent_dx, got_dx = give_back(dx_keep, dx_send)
     pair1 = grid.add(pair0, came, 0, sent_dx)
     came = grid.send(pair1, 1)
-    _, got_out = give_back(out_keep, after(out_send, sent_dx))
     grad_expert_down = expert_down_grad(expert_act, after(expert_g, sent_dx))
-    token_dx = combine_rows(place_column, after(got_dx, pair1, grad_expert_down))
+    _, got_out = give_back(out_keep, after(out_send, grad_expert_down))
+    turned_low = turn(scalar, grid, after(normed_low, grad_expert_down))
+    token_dx = combine_rows(place_column, after(got_dx, pair1, turned_low))
     results = middle_back(
-        scalar, order_of, dense_dx, swap(dense_dx), token_dx, swap(token_dx), hidden, own_cot,
+        scalar, grid, dense_dx, swap(dense_dx), token_dx, swap(token_dx), hidden, own_cot,
         other_cot, attended_own, ln2_gain, w_out, parts,
     )
     hidden_grad, attended_grad, ln2_row = results[:3]
@@ -1049,48 +1152,44 @@
     out_came = grid.send(out0, 0)
     pair2 = grid.add(pair1, came, 1, ln2_row)
     came = grid.send(pair2, 2)
-    dq, dk, dv = attend_back(qkv, attended_own, attended_grad, lse)
+    packed = attend_back(qkv, attended_own, attended_grad, lse)
 
     small = small_dense + small_expert
     small = small + jnp.where(jnp.arange(LANES)[:, None] == experts + 3, ln2_row[0:1], 0.0)
     results = tail(
-        scalar, order_of, normed_low, ln1_gain, small, dq, dk, dv, w_qkv, parts, experts + 2
+        scalar, grid, normed_low, turned_low, ln1_gain, small, packed, w_qkv, parts, experts + 2
     )
     grad_keep, grad_send, last0 = results[0], results[1], results[2:]
     last_came = grid.send(last0, 0)
     out1 = grid.add(out0, out_came, 0, grad_keep)
     out_came = grid.send(out1, 1)
     grad_expert_up = expert_up_grad(scalar, *expert_rows, after(expert_dpre, grad_keep))
-
-    token_out = combine_rows(place_column, after(got_out, grad_expert_up)).astype(F32)
-    chance = jnp.sum(jnp.where(route_onehot, probs[:, :experts], 0.0), axis=1, keepdims=True)
-    scaled = chance * probs[:, experts + 1 : experts + 2] * token_out
-    total_out = dense_out.astype(F32) + in_order(scaled, jnp.zeros_like(scaled), 1)
-    total_out = total_out.astype(BF16)
-    out_mine = lax.dynamic_slice_in_dim(total_out, own_start, own_rows, 0)
-    out_other = swap(lax.dynamic_slice_in_dim(total_out, own_rows - own_start, own_rows, 0))
-    out2 = grid.add(out1, out_came, 1, grad_expert_up)
+    last1 = grid.add(last0, last_came, 0, grad_expert_up)
+    last_came = grid.send(last1, 1)
+
+    total_out = combine_out(scalar, place_column, after(got_out, last1), dense_out, share)
+    out_mine, out_other = total_out[:own_rows], swap(total_out[own_rows:])
+    out2 = grid.add(out1, out_came, 1, last1)
     out_came = grid.send(out2, 2)
 
-    last1 = grid.add(last0, last_came, 0, grad_expert_up, total_out)
-    last_came = grid.send(last1, 1)
+
+    last2 = grid.add(last1, last_came, 1, total_out, out2)
+    last_came = grid.send(last2, 2)
 
     unit = width // members
-    both = grid.add(pair2, came, 2, last1)[0]
+    both = grid.add(pair2, came, 2, last2)[0]
     grad_w_up, grad_w_down = both[:unit], both[unit:]
     hidden_own = lax.dynamic_slice_in_dim(hidden, own_start, own_rows, 0)
-    out_other = after(out_other, last1)
+    out_other = after(out_other, last2)
     mixed_out = (hidden_own + out_mine.astype(F32) + out_other.astype(F32)).astype(BF16)
-    last2 = grid.add(last1, last_came, 1, mixed_out, both)
-    last_came = grid.send(last2, 2)
     grad_w_out = grid.add(out2, out_came, 2, last2)[0]
     normed_grad = grad_keep + after(swap(grad_send), last2).astype(F32)
     _, base_one, inverse_one = layer_norm(own_tokens.astype(F32), ln1_gain)
-    input_grad = lax.dynamic_slice_in_dim(hidden_grad, own_start, own_rows, 0) + norm_backward(
+    input_grad = hidden_grad + norm_backward(
         normed_grad, base_one, inverse_one, ln1_gain
     )
     block = width // (2 * members)
-    last = grid.add(last2, last_came, 2, input_grad, grad_w_out)[0].reshape(2, block, -1)
+    last = grid.add(last2, last_came, 2, input_grad, grad_w_out, mixed_out, both)[0].reshape(2, block, -1)
     kept = lax.dynamic_index_in_dim(last, node, 0, False)
     other = swap(lax.dynamic_index_in_dim(last, 1 - node, 0, False).astype(BF16)).astype(F32)
 

time: 414 us -> 436 us (1.053)
  starting transfers between devices: 57 us -> 81.8 us
  waiting for transfers between devices: 70.3 us -> 57.3 us
  Pallas kernels: 208 us -> 214 us
    ppermute x15, starting transfers between devices: 26.1 us -> 51.1 us  [send(): lax.ppermute(parts[by], ('node', 'expert'), self.shift(stage, by))]
    pallas_call x5 -> x7, Pallas kernels: 128 us -> 141 us  [the longest x2 93.3 us: branch(): pl.pallas_call(functools.partial(branch_kernel, dense, experts, parts, la...]
    ppermute x15, waiting for transfers between devices: 58.9 us -> 46.5 us  [send(): lax.ppermute(parts[by], ('node', 'expert'), self.shift(stage, by))]
    pallas_call x2 -> x1, Pallas kernels: 8.71 us -> 3.37 us  [combine_rows(): pl.pallas_call(combine_kernel, grid=(rows // size,), in_specs=[spec((size...]
    unnamed x92 -> x100, local copies, waits for them, and re-layouts: 25.3 us -> 30 us
  transfers between devices with their start and end apart: 31 -> 31, of which waited for: 11 -> 9; matrix products, arithmetic and copies ran while one was open for 11% -> 9% of each run, Pallas kernels for 40% -> 39%
where the time goes in v5:
time: 436 us; the launch traced here: 427 us
  Pallas kernels  214 us (49%)
  starting transfers between devices  81.8 us (19%)
  waiting for transfers between devices  57.3 us (13%)
  local copies, waits for them, and re-layouts  36.8 us (8%)
  other arithmetic  34.6 us (8%)
    pallas_call x2, Pallas kernels, branch(): pl.pallas_call(functools.partial(branch_kernel, dense, experts, parts, la...  93.3 us
    ppermute x15, starting transfers between devices, send(): lax.ppermute(parts[by], ('node', 'expert'), self.shift(stage, by))  51.1 us
    ppermute x15, waiting for transfers between devices, send(): lax.ppermute(parts[by], ('node', 'expert'), self.shift(stage, by))  46.5 us
    unnamed x100, local copies, waits for them, and re-layouts  30 us
    all_to_all x4, starting transfers between devices, exchange(): lax.all_to_all(value, 'expert', split_axis=0, concat_axis=0, tiled=True)  28.7 us
    pallas_call x1, Pallas kernels, attend_back(): pl.pallas_call(attend_back_kernel, grid=(pairs,), in_specs=head_specs(seq...  18.2 us
    pallas_call x1, Pallas kernels, tail(): pl.pallas_call(functools.partial(tail_kernel, parts, ln_lane, grid), grid...  16.1 us
    pallas_call x1, Pallas kernels, expert_up_grad(): pl.pallas_call(expert_up_kernel, grid_spec=pltpu.PrefetchScalarGridSpec(n...  15.4 us
  transfers between devices with their start and end apart: 31, of which 9 were waited for; matrix products, arithmetic and copies ran while one was open for 9% of the time, Pallas kernels for 39%

profile of v5, /device:TPU:0, one launch (start us, length us, event | category | flops | bytes accessed | tf_op | source)
XLA Modules:
  0.0 427.3 jit_solution(9916941192925808119)
XLA Ops:
  4.9 4.5 %dispatch.1 = bf16[1536,512]{1,0:T(8,128)(2,1)} custom-call(s32[2]{0:T(128)S(1)} %pad_add_fusion.node_ref, s32[2,512]{1,0:T(2,128)S(1)} %compare_select_fusion.1.place_ref, bf16[512,1024]{1,0:T(8,128)(2,1)S(1)} %bitcast.55, bf16[512,1024]{1,0:T(8,128)(2,1)S(1)} %collective-permute-done.2.refs_2_.other_ref.cot_other_ref), custom_call_target="tpu_custom_call" | custom-call | flops 1610612736 | bytes 3145728 | tf_op jit(solution)/shard_map/dispatch/pallas_call | solution.py:494
  9.5 8.4 %all-to-all-start.1 = ((bf16[16,96,512]{2,1,0:T(8,128)(2,1)}), bf16[16,96,512]{2,1,0:T(8,128)(2,1)}, u32[]{:S(2)}, u32[]{:S(2)}) async-start(bf16[16,96,512]{2,1,0:T(8,128)(2,1)} %bitcast.14), calls=%async_computation.1 | async-start | bytes 3145728 | tf_op jit(solution)/shard_map/all_to_all | solution.py:1104
  20.7 7.3 %front.1 = (bf16[1024,1536]{1,0:T(8,128)(2,1)S(1)}, bf16[1024,1024]{1,0:T(8,128)(2,1)S(1)}) custom-call(s32[2]{0:T(128)S(1)} %pad_add_fusion.node_ref, bf16[512,1024]{1,0:T(8,128)(2,1)S(1)} %bitcast.49, bf16[512,1024]{1,0:T(8,128)(2,1)S(1)} %collective-permute-done.other_ref.tok_other_ref, f32[1,1024]{1,0:T(1,128)S(1)} %bitcast.56, ...), custom_call_target="tpu_custom_call" | custom-call | flops 3221225472 | bytes 7340032 | tf_op jit(solution)/shard_map/front/pallas_call | solution.py:122
  29.5 14.2 %attend.1 = (bf16[1024,512]{1,0:T(8,128)(2,1)S(1)}, f32[4,8,1024]{2,1,0:T(8,128)S(1)}) custom-call(bf16[1024,1536]{1,0:T(8,128)(2,1)S(1)} %get-tuple-element.66.q_ref.k_ref.v_ref, bf16[1024,1536]{1,0:T(8,128)(2,1)S(1)} %get-tuple-element.66.q_ref.k_ref.v_ref, bf16[1024,1536]{1,0:T(8,128)(2,1)S(1)} %get-tuple-element.66.q_ref.k_ref.v_ref), custom_call_target="tpu_custom_call" | custom-call | flops 4294967296 | bytes 4194304 | tf_op jit(solution)/shard_map/attend/pallas_call | solution.py:188
  46.5 7.9 %middle.1 = (f32[1024,1024]{1,0:T(8,128)S(1)}, bf16[1024,1024]{1,0:T(8,128)(2,1)S(1)}, bf16[1536,512]{1,0:T(8,128)(2,1)}) custom-call(s32[2]{0:T(128)S(1)} %pad_add_fusion.node_ref, bf16[512,1024]{1,0:T(8,128)(2,1)S(1)} %bitcast.50, bf16[512,1024]{1,0:T(8,128)(2,1)S(1)} %collective-permute-done.other_ref.tok_other_ref, ...), custom_call_target="tpu_custom_call" | custom-call | flops 3758096384 | bytes 12582912 | tf_op jit(solution)/shard_map/middle/pallas_call | solution.py:329
  58.7 7.5 %all-to-all-start = ((bf16[16,96,512]{2,1,0:T(8,128)(2,1)}), bf16[16,96,512]{2,1,0:T(8,128)(2,1)S(1)}, u32[]{:S(2)}, u32[]{:S(2)}) async-start(bf16[16,96,512]{2,1,0:T(8,128)(2,1)} %bitcast.10), calls=%async_computation | async-start | bytes 3145728 | tf_op jit(solution)/shard_map/all_to_all | solution.py:1104
  68.6 47.7 %dense_branch.1 = (bf16[1024,1024]{1,0:T(8,128)(2,1)}, bf16[1024,1024]{1,0:T(8,128)(2,1)}, f32[128,1024]{1,0:T(8,128)}, f32[1024,128]{1,0:T(8,128)}, bf16[1024,2...) custom-call(s32[2]{0:T(128)} %copy-done.15, bf16[1024,1024]{1,0:T(8,128)(2,1)} %copy-done.31, bf16[512,1024]{1,0:T(8,128)(2,1)} %bitcast.53, ...), custom_call_target="tpu_custom_call" | custom-call | flops 25769803776 | bytes 33554432 | tf_op jit(solution)/shard_map/dense_branch/pallas_call | solution.py:763
  116.8 3.2 collective-permute-done.4.refs_3_
  123.3 45.6 %expert_branch.1 = (bf16[1536,512]{1,0:T(8,128)(2,1)}, bf16[1536,512]{1,0:T(8,128)(2,1)}, bf16[1536,512]{1,0:T(8,128)(2,1)}, bf16[1536,512]{1,0:T(8,128)(2,1)}, ...) custom-call(s32[2]{0:T(128)} %copy-done.15, ...), custom_call_target="tpu_custom_call" | custom-call | flops 25769803776 | bytes 37748736 | tf_op jit(solution)/shard_map/expert_branch/pallas_call | solution.py:763
  172.6 3.1 add_convert_fusion.3
  175.7 7.0 %all-to-all-start.3 = ((bf16[16,96,512]{2,1,0:T(8,128)(2,1)}), bf16[16,96,512]{2,1,0:T(8,128)(2,1)S(1)}, u32[]{:S(2)}, u32[]{:S(2)}) async-start(bf16[16,96,512]{2,1,0:T(8,128)(2,1)} %bitcast.60), calls=%async_computation.3 | async-start | bytes 3145728 | tf_op jit(solution)/shard_map/all_to_all | solution.py:1104
  183.8 2.8 copy-done.24
  188.4 10.1 %expert_down_grad.1 = f32[2048,1024]{1,0:T(8,128)} custom-call(bf16[1536,2048]{1,0:T(8,128)(2,1)S(1)} %copy-done.24, bf16[1536,1024]{1,0:T(8,128)(2,1)S(1)} %copy-done.30), custom_call_target="tpu_custom_call" | custom-call | flops 6442450944 | bytes 14680064 | tf_op jit(solution)/shard_map/expert_down_grad/pallas_call | solution.py:845
  199.2 33.6 %collective-permute-done.8 = bf16[1024,2048]{1,0:T(8,128)(2,1)} collective-permute-done((bf16[1024,2048]{1,0:T(8,128)(2,1)}, bf16[1024,2048]{1,0:T(8,128)(2,1)}, u32[]{:S(2)}, u32[]{:S(2)}) %collective-permute-start.8) | collective-permute-done | bytes 4194336 | tf_op jit(solution)/shard_map/ppermute | solution.py:1029
  232.7 4.0 turn.1.xt_ref
  238.1 4.5 %add_convert_fusion = (bf16[512,2048]{1,0:T(8,128)(2,1)}, bf16[512,2048]{1,0:T(8,128)(2,1)}) fusion(bf16[1024,2048]{1,0:T(8,128)(2,1)} %collective-permute-done.8, bf16[1024,2048]{1,0:T(8,128)(2,1)S(1)} %copy-done.33), kind=kLoop, calls=%fused_computation | loop fusion | flops 8388608 | bytes 12582912 | tf_op jit(solution)/shard_map/convert_element_type | solution.py:1044
  242.6 3.4 combine.1.token_ref
  248.1 3.0 add_convert_fusion.2
  251.1 5.8 %all-to-all-start.2 = ((bf16[16,96,512]{2,1,0:T(8,128)(2,1)}), bf16[16,96,512]{2,1,0:T(8,128)(2,1)}, u32[]{:S(2)}, u32[]{:S(2)}) async-start(bf16[16,96,512]{2,1,0:T(8,128)(2,1)} %bitcast.18), calls=%async_computation.2 | async-start | bytes 3145728 | tf_op jit(solution)/shard_map/all_to_all | solution.py:1104
  257.9 14.6 %middle_back.1 = (f32[512,1024]{1,0:T(8,128)}, bf16[1024,512]{1,0:T(8,128)(2,1)}, f32[8,1024]{1,0:T(8,128)}, bf16[256,1024]{1,0:T(8,128)(2,1)}, bf16[256,1024]{1,0:T(8,128)(2,1)}) custom-call(s32[2]{0:T(128)} %copy-done.15, bf16[1024,1024]{1,0:T(8,128)(2,1)} %get-tuple-element.84.dense_ref, bf16[1024,1024]{1,0:T(8,128)(2,1)} %collective-permute-done.7.dense_other_ref, ...), custom_call_target="tpu_custom_call" | custom-call | flops 2147483648 | bytes 18874368 | tf_op jit(solution)/shard_map/middle_back/pallas_call | solution.py:436
  277.5 18.2 %attend_back.1.packed_ref = bf16[3,1024,512]{2,1,0:T(8,128)(2,1)S(1)} custom-call(bf16[1024,1536]{1,0:T(8,128)(2,1)S(1)} %copy-done.23, bf16[1024,1536]{1,0:T(8,128)(2,1)S(1)} %copy-done.23, bf16[1024,1536]{1,0:T(8,128)(2,1)S(1)} %copy-done.23, bf16[1024,512]{1,0:T(8,128)(2,1)S(1)} %copy-done.11, bf16[1024,512]{1,0:T(8,128)(2,1)S(1)} %copy-done.21, ...), custom_call_target="tpu_custom_call" | custom-call | flops 10737418240 | bytes 8388608 | tf_op jit(solution)/shard_map/attend_back/pallas_call | solution.py:259
  298.6 16.1 %tail.1 = (f32[512,1024]{1,0:T(8,128)S(1)}, bf16[512,1024]{1,0:T(8,128)(2,1)}, bf16[512,1664]{1,0:T(8,128)(2,1)S(1)}, bf16[512,1664]{1,0:T(8,128)(2,1)}) custom-call(s32[2]{0:T(128)S(1)} %copy-done.17, bf16[1024,1024]{1,0:T(8,128)(2,1)S(1)} %copy-done.27, bf16[1024,1024]{1,0:T(8,128)(2,1)S(1)} %copy-done.29, f32[1,1024]{1,0:T(1,128)S(1)} %bitcast.57, ...), custom_call_target="tpu_custom_call" | custom-call | flops 6442450944 | bytes 16777216 | tf_op jit(solution)/shard_map/tail/pallas_call | solution.py:963
  318.6 15.4 %expert_up_grad.1 = f32[1024,2048]{1,0:T(8,128)} custom-call(s32[2]{0:T(128)} %copy-done.15, bf16[1536,512]{1,0:T(8,128)(2,1)} %bitcast.69, bf16[1536,512]{1,0:T(8,128)(2,1)} %copy-done.48, bf16[1536,2048]{1,0:T(8,128)(2,1)} %get-tuple-element.96.dpre_ref), custom_call_target="tpu_custom_call" | custom-call | flops 6442450944 | bytes 14680064 | tf_op jit(solution)/shard_map/expert_up_grad/pallas_call | solution.py:817
  334.0 9.6 %collective-permute-done.13 = bf16[256,1024]{1,0:T(8,128)(2,1)} collective-permute-done((bf16[256,1024]{1,0:T(8,128)(2,1)}, bf16[256,1024]{1,0:T(8,128)(2,1)}, u32[]{:S(2)}, u32[]{:S(2)}) %collective-permute-start.13) | collective-permute-done | bytes 524320 | tf_op jit(solution)/shard_map/ppermute | solution.py:1029
  346.9 3.7 add_convert_fusion.5
  350.6 2.8 add_convert_fusion.9
  362.6 5.0 %combine_out.1 = bf16[1024,1024]{1,0:T(8,128)(2,1)S(1)} custom-call(s32[2]{0:T(128)S(1)} %copy-done.18, s32[1024,1]{1,0:T(8,128)S(1)} %copy-done.5, bf16[1536,512]{1,0:T(8,128)(2,1)} %bitcast.19.got_ref, bf16[1024,1024]{1,0:T(8,128)(2,1)S(1)} %copy-done.3, f32[1024,128]{1,0:T(8,128)S(1)} %copy-done.12), custom_call_target="tpu_custom_call" | custom-call | flops 1610612736 | bytes 4194304 | tf_op jit(solution)/shard_map/combine_out/pallas_call | solution.py:559
  367.7 2.9 collective-permute-start.19
  372.8 19.5 %collective-permute-start.23 = (bf16[128,2048]{1,0:T(8,128)(2,1)S(1)}, bf16[128,2048]{1,0:T(8,128)(2,1)S(1)}, u32[]{:S(2)}, u32[]{:S(2)}) collective-permute-start(bf16[128,2048]{1,0:T(8,128)(2,1)S(1)} %copy-done.41), channel_id=1, source_target_pairs={{0,12},{1,13},{2,14},{3,15},{4,0},{5,1},{6,2},{7,3},{8,4},{9,5},{1... | collective-permute-start | bytes 1572872 | tf_op jit(solution)/shard_map/ppermute | solution.py:1029
  394.4 3.4 fusion.8
  399.1 14.6 %collective-permute-start.25 = (bf16[64,1664]{1,0:T(8,128)(2,1)S(1)}, bf16[64,1664]{1,0:T(8,128)(2,1)S(1)}, u32[]{:S(2)}, u32[]{:S(2)}) collective-permute-start(bf16[64,1664]{1,0:T(8,128)(2,1)S(1)} %get-tuple-element.129), channel_id=1, source_target_pairs={{0,12},{1,13},{2,14},{3,15},{4,0},{5,1},{6,2},{7,3},{8,4},{9,5},{1... | collective-permute-start | bytes 638984 | tf_op jit(solution)/shard_map/ppermute | solution.py:1029
  418.1 3.4 collective-permute-done.24
  (196 shorter events, 73.2 us)
Async XLA Ops:
  0.6 3.1 collective-permute-start.2
  1.2 16.7 %collective-permute-start = (bf16[512,1024]{1,0:T(8,128)(2,1)}, bf16[512,1024]{1,0:T(8,128)(2,1)S(1)}, u32[]{:S(2)}, u32[]{:S(2)}) collective-permute-start(bf16[512,1024]{1,0:T(8,128)(2,1)} %bitcast.48), channel_id=1, source_target_pairs={{0,16},{16,0},{1,17},{17,1},{2,18},{18,2},{3,19},{19,3},{4,20},{20... | collective-permute-start | bytes 3145736 | tf_op jit(solution)/shard_map/ppermute | solution.py:1080
  9.5 49.2 %all-to-all-start.1 = ((bf16[16,96,512]{2,1,0:T(8,128)(2,1)}), bf16[16,96,512]{2,1,0:T(8,128)(2,1)}, u32[]{:S(2)}, u32[]{:S(2)}) async-start(bf16[16,96,512]{2,1,0:T(8,128)(2,1)} %bitcast.14), calls=%async_computation.1 | async-start | bytes 3145728 | tf_op jit(solution)/shard_map/all_to_all | solution.py:1104
  43.7 2.7 collective-permute-start.1
  58.7 57.6 %all-to-all-start = ((bf16[16,96,512]{2,1,0:T(8,128)(2,1)}), bf16[16,96,512]{2,1,0:T(8,128)(2,1)S(1)}, u32[]{:S(2)}, u32[]{:S(2)}) async-start(bf16[16,96,512]{2,1,0:T(8,128)(2,1)} %bitcast.10), calls=%async_computation | async-start | bytes 3145728 | tf_op jit(solution)/shard_map/all_to_all | solution.py:1104
  116.3 3.8 collective-permute-start.4
  116.3 5.8 %collective-permute-start.3 = (bf16[1536,512]{1,0:T(8,128)(2,1)S(1)}, bf16[1536,512]{1,0:T(8,128)(2,1)S(1)}, u32[]{:S(2)}, u32[]{:S(2)}) collective-permute-start(bf16[1536,512]{1,0:T(8,128)(2,1)S(1)} %bitcast.67), channel_id=1, source_target_pairs={{0,16},{16,0},{1,17},{17,1},{2,18},{18,2},{3,19},{19,3},{4,20},{20... | collective-permute-start | bytes 4718600 | tf_op jit(solution)/shard_map/ppermute | solution.py:1080
  169.0 3.7 collective-permute-start.5
  169.2 63.6 %collective-permute-start.8 = (bf16[1024,2048]{1,0:T(8,128)(2,1)}, bf16[1024,2048]{1,0:T(8,128)(2,1)}, u32[]{:S(2)}, u32[]{:S(2)}) collective-permute-start(bf16[1024,2048]{1,0:T(8,128)(2,1)} %get-tuple-element.86), channel_id=1, source_target_pairs={{0,1},{1,0},{2,3},{3,2},{4,5},{5,4},{6,7},{7,6},{8,9},{9,8},{10,11... | collective-permute-start | bytes 12582920 | tf_op jit(solution)/shard_map/ppermute | solution.py:1029
  175.7 66.9 %all-to-all-start.3 = ((bf16[16,96,512]{2,1,0:T(8,128)(2,1)}), bf16[16,96,512]{2,1,0:T(8,128)(2,1)S(1)}, u32[]{:S(2)}, u32[]{:S(2)}) async-start(bf16[16,96,512]{2,1,0:T(8,128)(2,1)} %bitcast.60), calls=%async_computation.3 | async-start | bytes 3145728 | tf_op jit(solution)/shard_map/all_to_all | solution.py:1104
  183.7 73.1 %collective-permute-start.7 = (bf16[1024,1024]{1,0:T(8,128)(2,1)}, bf16[1024,1024]{1,0:T(8,128)(2,1)}, u32[]{:S(2)}, u32[]{:S(2)}) collective-permute-start(bf16[1024,1024]{1,0:T(8,128)(2,1)} %get-tuple-element.84.dense_ref), channel_id=1, source_target_pairs={{0,16},{16,0},{1,17},{17,1},{2,18},{18,2},{3,19},{19,3},{4,20},{20... | collective-permute-start | bytes 6291464 | tf_op jit(solution)/shard_map/ppermute | solution.py:1080
  188.4 44.3 %copy-start.26 = (bf16[1024,1024]{1,0:T(8,128)(2,1)S(1)}, bf16[1024,1024]{1,0:T(8,128)(2,1)}, u32[]{:S(2)}) copy-start(bf16[1024,1024]{1,0:T(8,128)(2,1)} %copy-done.25) | copy-start | bytes 6291460
  198.6 49.5 %collective-permute-start.6 = (bf16[1536,512]{1,0:T(8,128)(2,1)}, bf16[1536,512]{1,0:T(8,128)(2,1)}, u32[]{:S(2)}, u32[]{:S(2)}) collective-permute-start(bf16[1536,512]{1,0:T(8,128)(2,1)} %get-tuple-element.80), channel_id=1, source_target_pairs={{0,16},{16,0},{1,17},{17,1},{2,18},{18,2},{3,19},{19,3},{4,20},{20... | collective-permute-start | bytes 4718600 | tf_op jit(solution)/shard_map/ppermute | solution.py:1080
  246.0 10.9 %collective-permute-start.9 = (bf16[1024,512]{1,0:T(8,128)(2,1)}, bf16[1024,512]{1,0:T(8,128)(2,1)S(1)}, u32[]{:S(2)}, u32[]{:S(2)}) collective-permute-start(bf16[1024,512]{1,0:T(8,128)(2,1)} %combine.1.token_ref), channel_id=1, source_target_pairs={{0,16},{16,0},{1,17},{17,1},{2,18},{18,2},{3,19},{19,3},{4,20},{20... | collective-permute-start | bytes 3145736 | tf_op jit(solution)/shard_map/ppermute | solution.py:1080
  246.0 72.5 %collective-permute-start.20 = (bf16[512,2048]{1,0:T(8,128)(2,1)}, bf16[512,2048]{1,0:T(8,128)(2,1)}, u32[]{:S(2)}, u32[]{:S(2)}) collective-permute-start(bf16[512,2048]{1,0:T(8,128)(2,1)} %get-tuple-element.122), channel_id=1, source_target_pairs={{0,2},{1,3},{2,0},{3,1},{4,6},{5,7},{6,4},{7,5},{8,10},{9,11},{10,... | collective-permute-start | bytes 6291464 | tf_op jit(solution)/shard_map/ppermute | solution.py:1029
  251.1 104.3 %all-to-all-start.2 = ((bf16[16,96,512]{2,1,0:T(8,128)(2,1)}), bf16[16,96,512]{2,1,0:T(8,128)(2,1)}, u32[]{:S(2)}, u32[]{:S(2)}) async-start(bf16[16,96,512]{2,1,0:T(8,128)(2,1)} %bitcast.18), calls=%async_computation.2 | async-start | bytes 3145728 | tf_op jit(solution)/shard_map/all_to_all | solution.py:1104
  315.8 31.1 %collective-permute-start.10 = (bf16[512,1664]{1,0:T(8,128)(2,1)}, bf16[512,1664]{1,0:T(8,128)(2,1)}, u32[]{:S(2)}, u32[]{:S(2)}) collective-permute-start(bf16[512,1664]{1,0:T(8,128)(2,1)} %get-tuple-element.93), channel_id=1, source_target_pairs={{0,1},{1,0},{2,3},{3,2},{4,5},{5,4},{6,7},{7,6},{8,9},{9,8},{10,11... | collective-permute-start | bytes 5111816 | tf_op jit(solution)/shard_map/ppermute | solution.py:1029
  318.5 25.1 %collective-permute-start.13 = (bf16[256,1024]{1,0:T(8,128)(2,1)}, bf16[256,1024]{1,0:T(8,128)(2,1)}, u32[]{:S(2)}, u32[]{:S(2)}) collective-permute-start(bf16[256,1024]{1,0:T(8,128)(2,1)} %get-tuple-element.102), channel_id=1, source_target_pairs={{0,1},{1,0},{2,3},{3,2},{4,5},{5,4},{6,7},{7,6},{8,9},{9,8},{10,11... | collective-permute-start | bytes 1572872 | tf_op jit(solution)/shard_map/ppermute | solution.py:1029
  318.6 73.7 %collective-permute-start.15 = (bf16[512,1024]{1,0:T(8,128)(2,1)}, bf16[512,1024]{1,0:T(8,128)(2,1)}, u32[]{:S(2)}, u32[]{:S(2)}) collective-permute-start(bf16[512,1024]{1,0:T(8,128)(2,1)} %get-tuple-element.108), channel_id=1, source_target_pairs={{0,16},{16,0},{1,17},{17,1},{2,18},{18,2},{3,19},{19,3},{4,20},{20... | collective-permute-start | bytes 3145736 | tf_op jit(solution)/shard_map/ppermute | solution.py:1080
  344.8 10.6 %collective-permute-start.14 = (bf16[128,1024]{1,0:T(8,128)(2,1)S(1)}, bf16[128,1024]{1,0:T(8,128)(2,1)}, u32[]{:S(2)}, u32[]{:S(2)}) collective-permute-start(bf16[128,1024]{1,0:T(8,128)(2,1)S(1)} %get-tuple-element.135), channel_id=1, source_target_pairs={{0,2},{1,3},{2,0},{3,1},{4,6},{5,7},{6,4},{7,5},{8,10},{9,11},{10,... | collective-permute-start | bytes 786440 | tf_op jit(solution)/shard_map/ppermute | solution.py:1029
  350.5 17.2 %collective-permute-start.12 = (bf16[256,1664]{1,0:T(8,128)(2,1)}, bf16[256,1664]{1,0:T(8,128)(2,1)}, u32[]{:S(2)}, u32[]{:S(2)}) collective-permute-start(bf16[256,1664]{1,0:T(8,128)(2,1)} %get-tuple-element.127), channel_id=1, source_target_pairs={{0,2},{1,3},{2,0},{3,1},{4,6},{5,7},{6,4},{7,5},{8,10},{9,11},{10,... | collective-permute-start | bytes 2555912 | tf_op jit(solution)/shard_map/ppermute | solution.py:1029
  353.4 45.1 %collective-permute-start.21 = (bf16[128,2048]{1,0:T(8,128)(2,1)}, bf16[128,2048]{1,0:T(8,128)(2,1)}, u32[]{:S(2)}, u32[]{:S(2)}) collective-permute-start(bf16[128,2048]{1,0:T(8,128)(2,1)} %get-tuple-element.124), channel_id=1, source_target_pairs={{0,4},{1,5},{2,6},{3,7},{4,8},{5,9},{6,10},{7,11},{8,12},{9,13},{1... | collective-permute-start | bytes 1572872 | tf_op jit(solution)/shard_map/ppermute | solution.py:1029
  356.4 15.7 %collective-permute-start.17 = (bf16[32,1024]{1,0:T(8,128)(2,1)S(1)}, bf16[32,1024]{1,0:T(8,128)(2,1)S(1)}, u32[]{:S(2)}, u32[]{:S(2)}) collective-permute-start(bf16[32,1024]{1,0:T(8,128)(2,1)S(1)} %get-tuple-element.139), channel_id=1, source_target_pairs={{0,4},{1,5},{2,6},{3,7},{4,8},{5,9},{6,10},{7,11},{8,12},{9,13},{1... | collective-permute-start | bytes 196616 | tf_op jit(solution)/shard_map/ppermute | solution.py:1029
  357.9 14.8 %collective-permute-start.18 = (bf16[32,1024]{1,0:T(8,128)(2,1)S(1)}, bf16[32,1024]{1,0:T(8,128)(2,1)S(1)}, u32[]{:S(2)}, u32[]{:S(2)}) collective-permute-start(bf16[32,1024]{1,0:T(8,128)(2,1)S(1)} %get-tuple-element.138), channel_id=1, source_target_pairs={{0,8},{1,9},{2,10},{3,11},{4,12},{5,13},{6,14},{7,15},{8,0},{9,1},... | collective-permute-start | bytes 196616 | tf_op jit(solution)/shard_map/ppermute | solution.py:1029
  367.7 24.5 %collective-permute-start.19 = (bf16[32,1024]{1,0:T(8,128)(2,1)S(1)}, bf16[32,1024]{1,0:T(8,128)(2,1)S(1)}, u32[]{:S(2)}, u32[]{:S(2)}) collective-permute-start(bf16[32,1024]{1,0:T(8,128)(2,1)S(1)} %get-tuple-element.137), channel_id=1, source_target_pairs={{0,12},{1,13},{2,14},{3,15},{4,0},{5,1},{6,2},{7,3},{8,4},{9,5},{1... | collective-permute-start | bytes 196616 | tf_op jit(solution)/shard_map/ppermute | solution.py:1029
  372.1 27.0 %collective-permute-start.22 = (bf16[128,2048]{1,0:T(8,128)(2,1)S(1)}, bf16[128,2048]{1,0:T(8,128)(2,1)S(1)}, u32[]{:S(2)}, u32[]{:S(2)}) collective-permute-start(bf16[128,2048]{1,0:T(8,128)(2,1)S(1)} %copy-done.42), channel_id=1, source_target_pairs={{0,8},{1,9},{2,10},{3,11},{4,12},{5,13},{6,14},{7,15},{8,0},{9,1},... | collective-permute-start | bytes 1572872 | tf_op jit(solution)/shard_map/ppermute | solution.py:1029
  372.8 41.0 %collective-permute-start.23 = (bf16[128,2048]{1,0:T(8,128)(2,1)S(1)}, bf16[128,2048]{1,0:T(8,128)(2,1)S(1)}, u32[]{:S(2)}, u32[]{:S(2)}) collective-permute-start(bf16[128,2048]{1,0:T(8,128)(2,1)S(1)} %copy-done.41), channel_id=1, source_target_pairs={{0,12},{1,13},{2,14},{3,15},{4,0},{5,1},{6,2},{7,3},{8,4},{9,5},{1... | collective-permute-start | bytes 1572872 | tf_op jit(solution)/shard_map/ppermute | solution.py:1029
  392.3 24.3 %collective-permute-start.11 = (bf16[512,1024]{1,0:T(8,128)(2,1)S(1)}, bf16[512,1024]{1,0:T(8,128)(2,1)S(1)}, u32[]{:S(2)}, u32[]{:S(2)}) collective-permute-start(bf16[512,1024]{1,0:T(8,128)(2,1)S(1)} %slice.197), channel_id=1, source_target_pairs={{0,16},{16,0},{1,17},{17,1},{2,18},{18,2},{3,19},{19,3},{4,20},{20... | collective-permute-start | bytes 3145736 | tf_op jit(solution)/shard_map/ppermute | solution.py:1080
  392.3 25.8 %collective-permute-start.16 = (bf16[64,1664]{1,0:T(8,128)(2,1)S(1)}, bf16[64,1664]{1,0:T(8,128)(2,1)S(1)}, u32[]{:S(2)}, u32[]{:S(2)}) collective-permute-start(bf16[64,1664]{1,0:T(8,128)(2,1)S(1)} %get-tuple-element.131), channel_id=1, source_target_pairs={{0,4},{1,5},{2,6},{3,7},{4,8},{5,9},{6,10},{7,11},{8,12},{9,13},{1... | collective-permute-start | bytes 638984 | tf_op jit(solution)/shard_map/ppermute | solution.py:1029
  398.5 23.0 %collective-permute-start.24 = (bf16[64,1664]{1,0:T(8,128)(2,1)S(1)}, bf16[64,1664]{1,0:T(8,128)(2,1)S(1)}, u32[]{:S(2)}, u32[]{:S(2)}) collective-permute-start(bf16[64,1664]{1,0:T(8,128)(2,1)S(1)} %get-tuple-element.130), channel_id=1, source_target_pairs={{0,8},{1,9},{2,10},{3,11},{4,12},{5,13},{6,14},{7,15},{8,0},{9,1},... | collective-permute-start | bytes 638984 | tf_op jit(solution)/shard_map/ppermute | solution.py:1029
  399.1 22.3 %collective-permute-start.25 = (bf16[64,1664]{1,0:T(8,128)(2,1)S(1)}, bf16[64,1664]{1,0:T(8,128)(2,1)S(1)}, u32[]{:S(2)}, u32[]{:S(2)}) collective-permute-start(bf16[64,1664]{1,0:T(8,128)(2,1)S(1)} %get-tuple-element.129), channel_id=1, source_target_pairs={{0,12},{1,13},{2,14},{3,15},{4,0},{5,1},{6,2},{7,3},{8,4},{9,5},{1... | collective-permute-start | bytes 638984 | tf_op jit(solution)/shard_map/ppermute | solution.py:1029
  421.9 1.8 collective-permute-start.26
  (48 other events, 476.9 us)

commit v6 on v5

--- a/solution.py
+++ b/solution.py
@@ -60,6 +60,10 @@
 
 def struct(shape, kind):
     return jax.ShapeDtypeStruct(shape, kind)
+
+
+def far(shape, kind):
+    return pltpu.HBM(shape, kind)
 
 
 def chunks(count, size, step):
@@ -348,9 +352,9 @@
             scratch_shapes=[pltpu.VMEM((seq, width // 2), BF16)],
         ),
         out_shape=[
-            struct((seq, width), F32),
-            struct((seq, width), BF16),
-            struct((slots, width // 2), BF16),
+            far((seq, width), F32),
+            far((seq, width), BF16),
+            far((slots, width // 2), BF16),
         ],
         cost_estimate=pl.CostEstimate(
             flops=2 * seq * width * width + seq * slots * width,
@@ -382,7 +386,7 @@
     *refs,
 ):
     weight_refs = refs[:parts]
-    inner_ref, acc_ref, turn_ref = refs[parts:]
+    acc_ref, turn_ref = refs[parts:]
     half = token_ref.shape[1]
     node = node_ref[0]
     step = pl.program_id(0)
@@ -394,12 +398,13 @@
         order = functools.partial(grid.place, node_ref[0], node_ref[1])
         turn_ref[...] = permutation(order, 0, half, half // grid.members, half)
 
-    inner_ref[...] = dense_ref[...].astype(F32) + dense_other_ref[...].astype(F32)
-    inner_ref[:, pl.ds(pl.multiple_of(node * half, half), half)] += token_ref[...].astype(F32)
-    inner_ref[:, pl.ds(pl.multiple_of((1 - node) * half, half), half)] += token_other_ref[
-        ...
-    ].astype(F32)
-    inner = inner_ref[...]
+    tok, tok_other = token_ref[...], token_other_ref[...]
+    left, right = row_pick(node, 0, tok, tok_other), row_pick(node, 0, tok_other, tok)
+    inner = (
+        dense_ref[...].astype(F32)
+        + dense_other_ref[...].astype(F32)
+        + jnp.concatenate([left, right], axis=1).astype(F32)
+    )
     gain = gain_ref[...]
     _, base, inverse = layer_norm(hidden_ref[...], gain)
     ln_ref[0:1, :] += 0.5 * jnp.sum(inner * base, axis=0, keepdims=True)
@@ -452,7 +457,6 @@
             ],
             out_specs=[mine, row(half), fixed((8, width))] + [fixed(result)] * parts,
             scratch_shapes=[
-                pltpu.VMEM((rows, width), F32),
                 pltpu.VMEM((half, width), F32),
                 pltpu.VMEM((half, half), BF16),
             ],
@@ -576,7 +580,7 @@
             bytes_accessed=4 * rows * width,
             transcendentals=0,
         ),
-        compiler_params=pltpu.CompilerParams(vmem_limit_bytes=20 << 20),
+        compiler_params=pltpu.CompilerParams(vmem_limit_bytes=LIMIT),
         name="combine_out",
     )(node, place, got, dense, share)
 
@@ -978,7 +982,7 @@
             scratch_shapes=[pltpu.VMEM((seq, width), F32)],
         ),
         out_shape=[struct((seq // 2, width), F32), struct((seq // 2, width), BF16)]
-        + [struct((width // parts, steps * half + LANES), BF16)] * parts,
+        + [far((width // parts, steps * half + LANES), BF16)] * parts,
         cost_estimate=pl.CostEstimate(
             flops=6 * seq * width * width, bytes_accessed=16 * seq * width, transcendentals=0
         ),
@@ -1110,7 +1114,12 @@
 
     got_cot = exchange(dispatch_rows(scalar, place_rows, own_cot, other_cot, slots))
 
-    qkv, normed_low = front(scalar, own_tokens, other_tokens, ln1_gain, w_qkv)
+    route_column = group_routes[:, None]
+    head_t = jnp.concatenate(
+        [w_router, w_mix, jnp.zeros((width, LANES - experts - 2), BF16)], axis=1
+    ).T
+    first_gain = after(ln1_gain, route_column, head_t)
+    qkv, normed_low = front(scalar, own_tokens, other_tokens, first_gain, w_qkv)
     attended_own, lse = attend(qkv, pairs)
     hidden, inner_low, sent_rows = middle(
         scalar, own_tokens, other_tokens, attended_own, swap(attended_own), w_out, ln2_gain,
@@ -1118,12 +1127,9 @@
     )
 
     got_rows = exchange(sent_rows)
-    head_t = jnp.concatenate(
-        [w_router, w_mix, jnp.zeros((width, LANES - experts - 2), BF16)], axis=1
-    ).T
     picked = (jnp.arange(LANES) == member).astype(F32)[None]
     results = branch(
-        scalar, grid, [inner_low], [own_cot, other_cot, group_routes[:, None]], picked, head_t, w_up, w_down,
+        scalar, grid, [inner_low], [own_cot, other_cot, route_column], picked, head_t, w_up, w_down,
         experts, parts,
     )
     dense_out, dense_dx, small_dense, share = results[:4]
@@ -1164,16 +1170,16 @@
     out1 = grid.add(out0, out_came, 0, grad_keep)
     out_came = grid.send(out1, 1)
     grad_expert_up = expert_up_grad(scalar, *expert_rows, after(expert_dpre, grad_keep))
-    last1 = grid.add(last0, last_came, 0, grad_expert_up)
+    out2 = grid.add(out1, out_came, 1, grad_expert_up)
+    out_came = grid.send(out2, 2)
+    last1 = grid.add(last0, last_came, 0, grad_expert_up, *out2)
     last_came = grid.send(last1, 1)
 
     total_out = combine_out(scalar, place_column, after(got_out, last1), dense_out, share)
     out_mine, out_other = total_out[:own_rows], swap(total_out[own_rows:])
-    out2 = grid.add(out1, out_came, 1, last1)
-    out_came = grid.send(out2, 2)
-
-
-    last2 = grid.add(last1, last_came, 1, total_out, out2)
+
+
+    last2 = grid.add(last1, last_came, 1, total_out)
     last_came = grid.send(last2, 2)
 
     unit = width // members

time: 436 us -> 473 us (1.085)
  the two profiles are of different devices: /device:TPU:0 before, /device:TPU:11 now
where the time goes in v6:
time: 473 us; the launch traced here: 467 us
  Pallas kernels  215 us (45%)
  waiting for transfers between devices  134 us (28%)
  starting transfers between devices  49.7 us (11%)
  other arithmetic  35 us (7%)
  local copies, waits for them, and re-layouts  29.9 us (6%)
    ppermute x15, waiting for transfers between devices, send(): lax.ppermute(parts[by], ('node', 'expert'), self.shift(stage, by))  122 us
    pallas_call x2, Pallas kernels, branch(): pl.pallas_call(functools.partial(branch_kernel, dense, experts, parts, la...  93.3 us
    all_to_all x4, starting transfers between devices, exchange(): lax.all_to_all(value, 'expert', split_axis=0, concat_axis=0, tiled=True)  25.9 us
    unnamed x84, local copies, waits for them, and re-layouts  21.8 us
    pallas_call x1, Pallas kernels, attend_back(): pl.pallas_call(attend_back_kernel, grid=(pairs,), in_specs=head_specs(seq...  18.2 us
    pallas_call x1, Pallas kernels, tail(): pl.pallas_call(functools.partial(tail_kernel, parts, ln_lane, grid), grid...  16.2 us
    pallas_call x1, Pallas kernels, expert_up_grad(): pl.pallas_call(expert_up_kernel, grid_spec=pltpu.PrefetchScalarGridSpec(n...  15 us
    pallas_call x1, Pallas kernels, attend(): pl.pallas_call(attend_kernel, grid=(pairs,), in_specs=head_specs(seq, pai...  14.2 us
  transfers between devices with their start and end apart: 31, of which 16 were waited for; matrix products, arithmetic and copies ran while one was open for 9% of the time, Pallas kernels for 36%

profile of v6, /device:TPU:11, one launch (start us, length us, event | category | flops | bytes accessed | tf_op | source)
XLA Modules:
  0.0 466.6 jit_solution(10558771867763319112)
XLA Ops:
  5.1 4.5 dispatch.1
  9.6 6.8 %all-to-all-start.1 = ((bf16[16,96,512]{2,1,0:T(8,128)(2,1)}), bf16[16,96,512]{2,1,0:T(8,128)(2,1)}, u32[]{:S(2)}, u32[]{:S(2)}) async-start(bf16[16,96,512]{2,1,0:T(8,128)(2,1)} %bitcast.14), calls=%async_computation.1 | async-start | bytes 3145728 | tf_op jit(solution)/shard_map/all_to_all | solution.py:1108
  20.1 7.3 %front.1 = (bf16[1024,1536]{1,0:T(8,128)(2,1)S(1)}, bf16[1024,1024]{1,0:T(8,128)(2,1)S(1)}) custom-call(s32[2]{0:T(128)S(1)} %pad_add_fusion.node_ref, bf16[512,1024]{1,0:T(8,128)(2,1)S(1)} %bitcast.50, bf16[512,1024]{1,0:T(8,128)(2,1)S(1)} %collective-permute-done.other_ref.tok_other_ref, f32[1,1024]{1,0:T(1,128)S(1)} %bitcast.57, ...), custom_call_target="tpu_custom_call" | custom-call | flops 3221225472 | bytes 7340032 | tf_op jit(solution)/shard_map/front/pallas_call | solution.py:126
  28.9 14.2 %attend.1 = (bf16[1024,512]{1,0:T(8,128)(2,1)S(1)}, f32[4,8,1024]{2,1,0:T(8,128)S(1)}) custom-call(bf16[1024,1536]{1,0:T(8,128)(2,1)S(1)} %get-tuple-element.68.q_ref.k_ref.v_ref, bf16[1024,1536]{1,0:T(8,128)(2,1)S(1)} %get-tuple-element.68.q_ref.k_ref.v_ref, bf16[1024,1536]{1,0:T(8,128)(2,1)S(1)} %get-tuple-element.68.q_ref.k_ref.v_ref), custom_call_target="tpu_custom_call" | custom-call | flops 4294967296 | bytes 4194304 | tf_op jit(solution)/shard_map/attend/pallas_call | solution.py:192
  46.4 8.5 %middle.1 = (f32[1024,1024]{1,0:T(8,128)}, bf16[1024,1024]{1,0:T(8,128)(2,1)}, bf16[1536,512]{1,0:T(8,128)(2,1)}) custom-call(s32[2]{0:T(128)S(1)} %pad_add_fusion.node_ref, bf16[512,1024]{1,0:T(8,128)(2,1)S(1)} %bitcast.51, bf16[512,1024]{1,0:T(8,128)(2,1)S(1)} %collective-permute-done.other_ref.tok_other_ref, ...), custom_call_target="tpu_custom_call" | custom-call | flops 3758096384 | bytes 12582912 | tf_op jit(solution)/shard_map/middle/pallas_call | solution.py:333
  55.9 6.7 %all-to-all-start = ((bf16[16,96,512]{2,1,0:T(8,128)(2,1)}), bf16[16,96,512]{2,1,0:T(8,128)(2,1)S(1)}, u32[]{:S(2)}, u32[]{:S(2)}) async-start(bf16[16,96,512]{2,1,0:T(8,128)(2,1)} %bitcast.72), calls=%async_computation | async-start | bytes 3145728 | tf_op jit(solution)/shard_map/all_to_all | solution.py:1108
  64.2 47.7 %dense_branch.1 = (bf16[1024,1024]{1,0:T(8,128)(2,1)}, bf16[1024,1024]{1,0:T(8,128)(2,1)}, f32[128,1024]{1,0:T(8,128)}, f32[1024,128]{1,0:T(8,128)}, bf16[1024,2...) custom-call(s32[2]{0:T(128)} %copy-done.10, bf16[1024,1024]{1,0:T(8,128)(2,1)} %get-tuple-element.72.refs_0_, ...), custom_call_target="tpu_custom_call" | custom-call | flops 25769803776 | bytes 33554432 | tf_op jit(solution)/shard_map/dense_branch/pallas_call | solution.py:767
  113.0 3.3 collective-permute-done.4.refs_3_
  119.6 45.6 %expert_branch.1 = (bf16[1536,512]{1,0:T(8,128)(2,1)}, bf16[1536,512]{1,0:T(8,128)(2,1)}, bf16[1536,512]{1,0:T(8,128)(2,1)}, bf16[1536,512]{1,0:T(8,128)(2,1)}, ...) custom-call(s32[2]{0:T(128)} %copy-done.10, ...), custom_call_target="tpu_custom_call" | custom-call | flops 25769803776 | bytes 37748736 | tf_op jit(solution)/shard_map/expert_branch/pallas_call | solution.py:767
  168.8 3.0 add_convert_fusion.3
  171.8 7.0 %all-to-all-start.3 = ((bf16[16,96,512]{2,1,0:T(8,128)(2,1)}), bf16[16,96,512]{2,1,0:T(8,128)(2,1)S(1)}, u32[]{:S(2)}, u32[]{:S(2)}) async-start(bf16[16,96,512]{2,1,0:T(8,128)(2,1)} %bitcast.62), calls=%async_computation.3 | async-start | bytes 3145728 | tf_op jit(solution)/shard_map/all_to_all | solution.py:1108
  182.1 2.8 copy-done.18
  186.8 10.0 %expert_down_grad.1 = f32[2048,1024]{1,0:T(8,128)} custom-call(bf16[1536,2048]{1,0:T(8,128)(2,1)S(1)} %copy-done.18, bf16[1536,1024]{1,0:T(8,128)(2,1)S(1)} %copy-done.24), custom_call_target="tpu_custom_call" | custom-call | flops 6442450944 | bytes 14680064 | tf_op jit(solution)/shard_map/expert_down_grad/pallas_call | solution.py:849
  196.7 31.5 %collective-permute-done.8 = bf16[1024,2048]{1,0:T(8,128)(2,1)} collective-permute-done((bf16[1024,2048]{1,0:T(8,128)(2,1)}, bf16[1024,2048]{1,0:T(8,128)(2,1)}, u32[]{:S(2)}, u32[]{:S(2)}) %collective-permute-start.8) | collective-permute-done | bytes 4194336 | tf_op jit(solution)/shard_map/ppermute | solution.py:1033
  228.3 4.0 turn.1.xt_ref
  233.6 4.5 add_convert_fusion
  245.0 14.2 %middle_back.1 = (f32[512,1024]{1,0:T(8,128)}, bf16[1024,512]{1,0:T(8,128)(2,1)}, f32[8,1024]{1,0:T(8,128)}, bf16[256,1024]{1,0:T(8,128)(2,1)}, bf16[256,1024]{1,0:T(8,128)(2,1)}) custom-call(s32[2]{0:T(128)} %copy-done.10, bf16[1024,1024]{1,0:T(8,128)(2,1)} %get-tuple-element.86.dense_ref, bf16[1024,1024]{1,0:T(8,128)(2,1)} %collective-permute-done.7.dense_other_ref, ...), custom_call_target="tpu_custom_call" | custom-call | flops 2147483648 | bytes 18874368 | tf_op jit(solution)/shard_map/middle_back/pallas_call | solution.py:441
  264.3 18.2 %attend_back.1.packed_ref = bf16[3,1024,512]{2,1,0:T(8,128)(2,1)S(1)} custom-call(bf16[1024,1536]{1,0:T(8,128)(2,1)S(1)} %copy-done.17, bf16[1024,1536]{1,0:T(8,128)(2,1)S(1)} %copy-done.17, bf16[1024,1536]{1,0:T(8,128)(2,1)S(1)} %copy-done.17, bf16[1024,512]{1,0:T(8,128)(2,1)S(1)} %copy-done.6, bf16[1024,512]{1,0:T(8,128)(2,1)S(1)} %copy-done.15, ...), custom_call_target="tpu_custom_call" | custom-call | flops 10737418240 | bytes 8388608 | tf_op jit(solution)/shard_map/attend_back/pallas_call | solution.py:263
  285.3 16.2 %tail.1 = (f32[512,1024]{1,0:T(8,128)S(1)}, bf16[512,1024]{1,0:T(8,128)(2,1)}, bf16[512,1664]{1,0:T(8,128)(2,1)}, bf16[512,1664]{1,0:T(8,128)(2,1)}) custom-call(s32[2]{0:T(128)S(1)} %copy-done.12, bf16[1024,1024]{1,0:T(8,128)(2,1)S(1)} %copy-done.21, bf16[1024,1024]{1,0:T(8,128)(2,1)S(1)} %copy-done.23, f32[1,1024]{1,0:T(1,128)S(1)} %bitcast.58, ...), custom_call_target="tpu_custom_call" | custom-call | flops 6442450944 | bytes 16777216 | tf_op jit(solution)/shard_map/tail/pallas_call | solution.py:967
  302.7 3.1 add_convert_fusion.2
  305.7 5.5 %all-to-all-start.2 = ((bf16[16,96,512]{2,1,0:T(8,128)(2,1)}), bf16[16,96,512]{2,1,0:T(8,128)(2,1)}, u32[]{:S(2)}, u32[]{:S(2)}) async-start(bf16[16,96,512]{2,1,0:T(8,128)(2,1)} %bitcast.61), calls=%async_computation.2 | async-start | bytes 3145728 | tf_op jit(solution)/shard_map/all_to_all | solution.py:1108
  313.4 45.1 %collective-permute-done.11 = bf16[256,1024]{1,0:T(8,128)(2,1)} collective-permute-done((bf16[256,1024]{1,0:T(8,128)(2,1)}, bf16[256,1024]{1,0:T(8,128)(2,1)}, u32[]{:S(2)}, u32[]{:S(2)}) %collective-permute-start.11) | collective-permute-done | bytes 524320 | tf_op jit(solution)/shard_map/ppermute | solution.py:1033
  360.4 15.0 %expert_up_grad.1 = f32[1024,2048]{1,0:T(8,128)} custom-call(s32[2]{0:T(128)} %copy-done.10, bf16[1536,512]{1,0:T(8,128)(2,1)} %bitcast.71, bf16[1536,512]{1,0:T(8,128)(2,1)} %copy-done.40, bf16[1536,2048]{1,0:T(8,128)(2,1)} %get-tuple-element.98.dpre_ref), custom_call_target="tpu_custom_call" | custom-call | flops 6442450944 | bytes 14680064 | tf_op jit(solution)/shard_map/expert_up_grad/pallas_call | solution.py:821
  375.5 3.7 add_convert_fusion.5
  380.1 4.8 %collective-permute-start.15 = (bf16[512,1024]{1,0:T(8,128)(2,1)}, bf16[512,1024]{1,0:T(8,128)(2,1)}, u32[]{:S(2)}, u32[]{:S(2)}) collective-permute-start(bf16[512,1024]{1,0:T(8,128)(2,1)} %get-tuple-element.110), channel_id=1, source_target_pairs={{0,16},{16,0},{1,17},{17,1},{2,18},{18,2},{3,19},{19,3},{4,20},{20... | collective-permute-start | bytes 3145736 | tf_op jit(solution)/shard_map/ppermute | solution.py:1084
  384.9 2.8 add_convert_fusion.9
  391.3 6.9 %combine_out.1 = bf16[1024,1024]{1,0:T(8,128)(2,1)} custom-call(s32[2]{0:T(128)} %copy-done.10, s32[1024,1]{1,0:T(8,128)} %copy-done.1, bf16[1536,512]{1,0:T(8,128)(2,1)} %bitcast.19.got_ref, bf16[1024,1024]{1,0:T(8,128)(2,1)} %get-tuple-element.105.dense_ref, f32[1024,128]{1,0:T(8,128)} %get-tuple-element.106.share_ref), custom_call_target="tpu_custom_call" | custom-call | flops 1610612736 | bytes 4194304 | tf_op jit(solution)/shard_map/combine_out/pallas_call | solution.py:563
  405.0 6.6 %collective-permute-done.18 = bf16[32,1024]{1,0:T(8,128)(2,1)S(1)} collective-permute-done((bf16[32,1024]{1,0:T(8,128)(2,1)S(1)}, bf16[32,1024]{1,0:T(8,128)(2,1)S(1)}, u32[]{:S(2)}, u32[]{:S(2)}) %collective-permute-start.18) | collective-permute-done | bytes 65568 | tf_op jit(solution)/shard_map/ppermute | solution.py:1033
  411.6 7.0 %collective-permute-done.19 = bf16[32,1024]{1,0:T(8,128)(2,1)S(1)} collective-permute-done((bf16[32,1024]{1,0:T(8,128)(2,1)S(1)}, bf16[32,1024]{1,0:T(8,128)(2,1)S(1)}, u32[]{:S(2)}, u32[]{:S(2)}) %collective-permute-start.19) | collective-permute-done | bytes 65568 | tf_op jit(solution)/shard_map/ppermute | solution.py:1033
  421.4 3.5 fusion.8
  425.9 18.5 %collective-permute-done.22 = bf16[128,2048]{1,0:T(8,128)(2,1)S(1)} collective-permute-done((bf16[128,2048]{1,0:T(8,128)(2,1)S(1)}, bf16[128,2048]{1,0:T(8,128)(2,1)S(1)}, u32[]{:S(2)}, u32[]{:S(2)}) %collective-permute-start.22) | collective-permute-done | bytes 524320 | tf_op jit(solution)/shard_map/ppermute | solution.py:1033
  444.6 6.9 %collective-permute-done.23 = bf16[128,2048]{1,0:T(8,128)(2,1)S(1)} collective-permute-done((bf16[128,2048]{1,0:T(8,128)(2,1)S(1)}, bf16[128,2048]{1,0:T(8,128)(2,1)S(1)}, u32[]{:S(2)}, u32[]{:S(2)}) %collective-permute-start.23) | collective-permute-done | bytes 524320 | tf_op jit(solution)/shard_map/ppermute | solution.py:1033
  (180 shorter events, 80.0 us)
Async XLA Ops:
  0.6 3.2 collective-permute-start.2
  1.4 15.9 %collective-permute-start = (bf16[512,1024]{1,0:T(8,128)(2,1)}, bf16[512,1024]{1,0:T(8,128)(2,1)S(1)}, u32[]{:S(2)}, u32[]{:S(2)}) collective-permute-start(bf16[512,1024]{1,0:T(8,128)(2,1)} %bitcast.49), channel_id=1, source_target_pairs={{0,16},{16,0},{1,17},{17,1},{2,18},{18,2},{3,19},{19,3},{4,20},{20... | collective-permute-start | bytes 3145736 | tf_op jit(solution)/shard_map/ppermute | solution.py:1084
  9.6 46.3 %all-to-all-start.1 = ((bf16[16,96,512]{2,1,0:T(8,128)(2,1)}), bf16[16,96,512]{2,1,0:T(8,128)(2,1)}, u32[]{:S(2)}, u32[]{:S(2)}) async-start(bf16[16,96,512]{2,1,0:T(8,128)(2,1)} %bitcast.14), calls=%async_computation.1 | async-start | bytes 3145728 | tf_op jit(solution)/shard_map/all_to_all | solution.py:1108
  43.1 3.3 collective-permute-start.1
  55.9 56.9 %all-to-all-start = ((bf16[16,96,512]{2,1,0:T(8,128)(2,1)}), bf16[16,96,512]{2,1,0:T(8,128)(2,1)S(1)}, u32[]{:S(2)}, u32[]{:S(2)}) async-start(bf16[16,96,512]{2,1,0:T(8,128)(2,1)} %bitcast.72), calls=%async_computation | async-start | bytes 3145728 | tf_op jit(solution)/shard_map/all_to_all | solution.py:1108
  111.9 4.3 collective-permute-start.4
  112.9 5.5 %collective-permute-start.3 = (bf16[1536,512]{1,0:T(8,128)(2,1)S(1)}, bf16[1536,512]{1,0:T(8,128)(2,1)S(1)}, u32[]{:S(2)}, u32[]{:S(2)}) collective-permute-start(bf16[1536,512]{1,0:T(8,128)(2,1)S(1)} %bitcast.69), channel_id=1, source_target_pairs={{0,16},{16,0},{1,17},{17,1},{2,18},{18,2},{3,19},{19,3},{4,20},{20... | collective-permute-start | bytes 4718600 | tf_op jit(solution)/shard_map/ppermute | solution.py:1084
  165.1 3.7 collective-permute-start.5
  165.6 62.7 %collective-permute-start.8 = (bf16[1024,2048]{1,0:T(8,128)(2,1)}, bf16[1024,2048]{1,0:T(8,128)(2,1)}, u32[]{:S(2)}, u32[]{:S(2)}) collective-permute-start(bf16[1024,2048]{1,0:T(8,128)(2,1)} %get-tuple-element.88), channel_id=1, source_target_pairs={{0,1},{1,0},{2,3},{3,2},{4,5},{5,4},{6,7},{7,6},{8,9},{9,8},{10,11... | collective-permute-start | bytes 12582920 | tf_op jit(solution)/shard_map/ppermute | solution.py:1033
  171.8 66.3 %all-to-all-start.3 = ((bf16[16,96,512]{2,1,0:T(8,128)(2,1)}), bf16[16,96,512]{2,1,0:T(8,128)(2,1)S(1)}, u32[]{:S(2)}, u32[]{:S(2)}) async-start(bf16[16,96,512]{2,1,0:T(8,128)(2,1)} %bitcast.62), calls=%async_computation.3 | async-start | bytes 3145728 | tf_op jit(solution)/shard_map/all_to_all | solution.py:1108
  181.1 57.0 %copy-start.1 = (s32[1024,1]{1,0:T(8,128)}, s32[1024,1]{1,0:T(8,128)S(1)}, u32[]{:S(2)}) copy-start(s32[1024,1]{1,0:T(8,128)S(1)} %add_select_fusion.place_ref) | copy-start | bytes 12292
  181.1 60.8 %collective-permute-start.7 = (bf16[1024,1024]{1,0:T(8,128)(2,1)}, bf16[1024,1024]{1,0:T(8,128)(2,1)}, u32[]{:S(2)}, u32[]{:S(2)}) collective-permute-start(bf16[1024,1024]{1,0:T(8,128)(2,1)} %get-tuple-element.86.dense_ref), channel_id=1, source_target_pairs={{0,16},{16,0},{1,17},{17,1},{2,18},{18,2},{3,19},{19,3},{4,20},{20... | collective-permute-start | bytes 6291464 | tf_op jit(solution)/shard_map/ppermute | solution.py:1084
  240.7 3.3 collective-permute-start.9
  241.8 60.9 %collective-permute-start.6 = (bf16[1536,512]{1,0:T(8,128)(2,1)}, bf16[1536,512]{1,0:T(8,128)(2,1)}, u32[]{:S(2)}, u32[]{:S(2)}) collective-permute-start(bf16[1536,512]{1,0:T(8,128)(2,1)} %get-tuple-element.82), channel_id=1, source_target_pairs={{0,16},{16,0},{1,17},{17,1},{2,18},{18,2},{3,19},{19,3},{4,20},{20... | collective-permute-start | bytes 4718600 | tf_op jit(solution)/shard_map/ppermute | solution.py:1084
  301.5 74.0 %collective-permute-start.10 = (bf16[512,1664]{1,0:T(8,128)(2,1)}, bf16[512,1664]{1,0:T(8,128)(2,1)}, u32[]{:S(2)}, u32[]{:S(2)}) collective-permute-start(bf16[512,1664]{1,0:T(8,128)(2,1)} %get-tuple-element.95), channel_id=1, source_target_pairs={{0,1},{1,0},{2,3},{3,2},{4,5},{5,4},{6,7},{7,6},{8,9},{9,8},{10,11... | collective-permute-start | bytes 5111816 | tf_op jit(solution)/shard_map/ppermute | solution.py:1033
  305.7 85.6 %all-to-all-start.2 = ((bf16[16,96,512]{2,1,0:T(8,128)(2,1)}), bf16[16,96,512]{2,1,0:T(8,128)(2,1)}, u32[]{:S(2)}, u32[]{:S(2)}) async-start(bf16[16,96,512]{2,1,0:T(8,128)(2,1)} %bitcast.61), calls=%async_computation.2 | async-start | bytes 3145728 | tf_op jit(solution)/shard_map/all_to_all | solution.py:1108
  311.2 47.2 %collective-permute-start.11 = (bf16[256,1024]{1,0:T(8,128)(2,1)}, bf16[256,1024]{1,0:T(8,128)(2,1)}, u32[]{:S(2)}, u32[]{:S(2)}) collective-permute-start(bf16[256,1024]{1,0:T(8,128)(2,1)} %get-tuple-element.100), channel_id=1, source_target_pairs={{0,1},{1,0},{2,3},{3,2},{4,5},{5,4},{6,7},{7,6},{8,9},{9,8},{10,11... | collective-permute-start | bytes 1572872 | tf_op jit(solution)/shard_map/ppermute | solution.py:1033
  312.6 67.5 %collective-permute-start.20 = (bf16[512,2048]{1,0:T(8,128)(2,1)}, bf16[512,2048]{1,0:T(8,128)(2,1)}, u32[]{:S(2)}, u32[]{:S(2)}) collective-permute-start(bf16[512,2048]{1,0:T(8,128)(2,1)} %get-tuple-element.124), channel_id=1, source_target_pairs={{0,2},{1,3},{2,0},{3,1},{4,6},{5,7},{6,4},{7,5},{8,10},{9,11},{10,... | collective-permute-start | bytes 6291464 | tf_op jit(solution)/shard_map/ppermute | solution.py:1033
  359.8 15.7 %collective-permute-start.12 = (bf16[128,1024]{1,0:T(8,128)(2,1)S(1)}, bf16[128,1024]{1,0:T(8,128)(2,1)S(1)}, u32[]{:S(2)}, u32[]{:S(2)}) collective-permute-start(bf16[128,1024]{1,0:T(8,128)(2,1)S(1)} %get-tuple-element.137), channel_id=1, source_target_pairs={{0,2},{1,3},{2,0},{3,1},{4,6},{5,7},{6,4},{7,5},{8,10},{9,11},{10,... | collective-permute-start | bytes 786440 | tf_op jit(solution)/shard_map/ppermute | solution.py:1033
  379.2 20.5 %collective-permute-start.14 = (bf16[256,1664]{1,0:T(8,128)(2,1)}, bf16[256,1664]{1,0:T(8,128)(2,1)}, u32[]{:S(2)}, u32[]{:S(2)}) collective-permute-start(bf16[256,1664]{1,0:T(8,128)(2,1)} %get-tuple-element.129), channel_id=1, source_target_pairs={{0,2},{1,3},{2,0},{3,1},{4,6},{5,7},{6,4},{7,5},{8,10},{9,11},{10,... | collective-permute-start | bytes 2555912 | tf_op jit(solution)/shard_map/ppermute | solution.py:1033
  380.1 39.2 %collective-permute-start.15 = (bf16[512,1024]{1,0:T(8,128)(2,1)}, bf16[512,1024]{1,0:T(8,128)(2,1)}, u32[]{:S(2)}, u32[]{:S(2)}) collective-permute-start(bf16[512,1024]{1,0:T(8,128)(2,1)} %get-tuple-element.110), channel_id=1, source_target_pairs={{0,16},{16,0},{1,17},{17,1},{2,18},{18,2},{3,19},{19,3},{4,20},{20... | collective-permute-start | bytes 3145736 | tf_op jit(solution)/shard_map/ppermute | solution.py:1084
  387.8 37.8 %collective-permute-start.21 = (bf16[128,2048]{1,0:T(8,128)(2,1)}, bf16[128,2048]{1,0:T(8,128)(2,1)}, u32[]{:S(2)}, u32[]{:S(2)}) collective-permute-start(bf16[128,2048]{1,0:T(8,128)(2,1)} %get-tuple-element.126), channel_id=1, source_target_pairs={{0,4},{1,5},{2,6},{3,7},{4,8},{5,9},{6,10},{7,11},{8,12},{9,13},{1... | collective-permute-start | bytes 1572872 | tf_op jit(solution)/shard_map/ppermute | solution.py:1033
  389.0 13.9 %collective-permute-start.17 = (bf16[32,1024]{1,0:T(8,128)(2,1)S(1)}, bf16[32,1024]{1,0:T(8,128)(2,1)S(1)}, u32[]{:S(2)}, u32[]{:S(2)}) collective-permute-start(bf16[32,1024]{1,0:T(8,128)(2,1)S(1)} %get-tuple-element.141), channel_id=1, source_target_pairs={{0,4},{1,5},{2,6},{3,7},{4,8},{5,9},{6,10},{7,11},{8,12},{9,13},{1... | collective-permute-start | bytes 196616 | tf_op jit(solution)/shard_map/ppermute | solution.py:1033
  390.2 21.4 %collective-permute-start.18 = (bf16[32,1024]{1,0:T(8,128)(2,1)S(1)}, bf16[32,1024]{1,0:T(8,128)(2,1)S(1)}, u32[]{:S(2)}, u32[]{:S(2)}) collective-permute-start(bf16[32,1024]{1,0:T(8,128)(2,1)S(1)} %get-tuple-element.140), channel_id=1, source_target_pairs={{0,8},{1,9},{2,10},{3,11},{4,12},{5,13},{6,14},{7,15},{8,0},{9,1},... | collective-permute-start | bytes 196616 | tf_op jit(solution)/shard_map/ppermute | solution.py:1033
  399.7 18.9 %collective-permute-start.19 = (bf16[32,1024]{1,0:T(8,128)(2,1)S(1)}, bf16[32,1024]{1,0:T(8,128)(2,1)S(1)}, u32[]{:S(2)}, u32[]{:S(2)}) collective-permute-start(bf16[32,1024]{1,0:T(8,128)(2,1)S(1)} %get-tuple-element.139), channel_id=1, source_target_pairs={{0,12},{1,13},{2,14},{3,15},{4,0},{5,1},{6,2},{7,3},{8,4},{9,5},{1... | collective-permute-start | bytes 196616 | tf_op jit(solution)/shard_map/ppermute | solution.py:1033
  402.9 41.5 %collective-permute-start.22 = (bf16[128,2048]{1,0:T(8,128)(2,1)S(1)}, bf16[128,2048]{1,0:T(8,128)(2,1)S(1)}, u32[]{:S(2)}, u32[]{:S(2)}) collective-permute-start(bf16[128,2048]{1,0:T(8,128)(2,1)S(1)} %copy-done.35), channel_id=1, source_target_pairs={{0,8},{1,9},{2,10},{3,11},{4,12},{5,13},{6,14},{7,15},{8,0},{9,1},... | collective-permute-start | bytes 1572872 | tf_op jit(solution)/shard_map/ppermute | solution.py:1033
  411.5 40.0 %collective-permute-start.23 = (bf16[128,2048]{1,0:T(8,128)(2,1)S(1)}, bf16[128,2048]{1,0:T(8,128)(2,1)S(1)}, u32[]{:S(2)}, u32[]{:S(2)}) collective-permute-start(bf16[128,2048]{1,0:T(8,128)(2,1)S(1)} %copy-done.34), channel_id=1, source_target_pairs={{0,12},{1,13},{2,14},{3,15},{4,0},{5,1},{6,2},{7,3},{8,4},{9,5},{1... | collective-permute-start | bytes 1572872 | tf_op jit(solution)/shard_map/ppermute | solution.py:1033
  418.6 35.8 %collective-permute-start.13 = (bf16[512,1024]{1,0:T(8,128)(2,1)S(1)}, bf16[512,1024]{1,0:T(8,128)(2,1)S(1)}, u32[]{:S(2)}, u32[]{:S(2)}) collective-permute-start(bf16[512,1024]{1,0:T(8,128)(2,1)S(1)} %slice.201), channel_id=1, source_target_pairs={{0,16},{16,0},{1,17},{17,1},{2,18},{18,2},{3,19},{19,3},{4,20},{20... | collective-permute-start | bytes 3145736 | tf_op jit(solution)/shard_map/ppermute | solution.py:1084
  419.4 36.6 %collective-permute-start.16 = (bf16[64,1664]{1,0:T(8,128)(2,1)S(1)}, bf16[64,1664]{1,0:T(8,128)(2,1)S(1)}, u32[]{:S(2)}, u32[]{:S(2)}) collective-permute-start(bf16[64,1664]{1,0:T(8,128)(2,1)S(1)} %get-tuple-element.133), channel_id=1, source_target_pairs={{0,4},{1,5},{2,6},{3,7},{4,8},{5,9},{6,10},{7,11},{8,12},{9,13},{1... | collective-permute-start | bytes 638984 | tf_op jit(solution)/shard_map/ppermute | solution.py:1033
  425.6 32.5 %collective-permute-start.24 = (bf16[64,1664]{1,0:T(8,128)(2,1)S(1)}, bf16[64,1664]{1,0:T(8,128)(2,1)S(1)}, u32[]{:S(2)}, u32[]{:S(2)}) collective-permute-start(bf16[64,1664]{1,0:T(8,128)(2,1)S(1)} %get-tuple-element.132), channel_id=1, source_target_pairs={{0,8},{1,9},{2,10},{3,11},{4,12},{5,13},{6,14},{7,15},{8,0},{9,1},... | collective-permute-start | bytes 638984 | tf_op jit(solution)/shard_map/ppermute | solution.py:1033
  444.4 16.3 %collective-permute-start.25 = (bf16[64,1664]{1,0:T(8,128)(2,1)S(1)}, bf16[64,1664]{1,0:T(8,128)(2,1)S(1)}, u32[]{:S(2)}, u32[]{:S(2)}) collective-permute-start(bf16[64,1664]{1,0:T(8,128)(2,1)S(1)} %get-tuple-element.131), channel_id=1, source_target_pairs={{0,12},{1,13},{2,14},{3,15},{4,0},{5,1},{6,2},{7,3},{8,4},{9,5},{1... | collective-permute-start | bytes 638984 | tf_op jit(solution)/shard_map/ppermute | solution.py:1033
  461.1 2.0 collective-permute-start.26
  (40 other events, 464.0 us)
